TPU v7x, 32 devices: a whole 2x2x4 slice. The times are simulated.
32 devices in a mesh: group: 2 (over x), strip: 16 (over z, y, core).
Axes of the slice: x: 2, y: 2, z: 4, core: 2. Of those that a mesh axis runs over, the one named last changes fastest.
Arguments:
- frame_tokens: bfloat16 [16384, 768], P(('group', 'strip')), parts along dimension 0, may hold values from -6 to 6
- window_reach: int32 [32], P('group'), parts along dimension 0, may hold values from 64 to 128, as said below
- valid_count: int32 [32], P('group'), parts along dimension 0, may hold values from 256 to 512, as said below
- space_gain: float32 [768], replicated, may hold values from 0.1 to 1.9
- space_project: bfloat16 [768, 2304], replicated, may hold values from -32 to 32
- space_output: bfloat16 [768, 768], replicated, may hold values from -0.21875 to 0.21875
- time_gain: float32 [768], replicated, may hold values from 0.1 to 1.9
- time_project: bfloat16 [768, 2304], replicated, may hold values from -32 to 32
- time_output: bfloat16 [768, 768], replicated, may hold values from -0.21875 to 0.21875
Outputs:
- restored: bfloat16 [16384, 768], P(('group', 'strip')), parts along dimension 0
There are 2 independent parts, one for each index of `group`. A program takes and returns all parts, laid end to end along the dimension named above; an argument that names none is the same for every part. Nothing has to cross between parts.
Inputs may be any that keep to these rules, and one draw needn't show every extreme that they name: `window_reach`: some frame has reach exactly 128. `valid_count`: some frame is fully valid.
All inputs are finite; a program needn't handle non-finite values.
Results may differ from a plain program's by a relative error of at most 0.01.
Values may be sent and summed in bfloat16 or wider, within the bound.
No kernel may reach another device: no remote copies, remote signals or barrier semaphores. Data moves between devices by JAX's collectives and lax.ppermute only.
A program may use at most 128 MiB of HBM per device.

v0:
```python
import jax
import jax.numpy as jnp
from jax import lax
from jax.sharding import PartitionSpec as P

F = 16
HALO = 128
LAYERS = 2
H = 12
HD = 64
D = 768


epsilon = 1e-06


def padded(x, sides, width):
    for axis, dim in sides:
        peers, length = (lax.axis_size(axis), x.shape[dim])
        up = [(i, (i + 1) % peers) for i in range(peers - 1)]
        down = [(j, i) for i, j in up]
        last = lax.slice_in_dim(x, length - width, length, axis=dim)
        leading = lax.slice_in_dim(x, 0, width, axis=dim)
        before = lax.ppermute(last, axis, up)
        after = lax.ppermute(leading, axis, down)
        x = jnp.concatenate([before, x, after], axis=dim)
    return x


def normed(values, gain):
    wide = values.astype(jnp.float32)
    meansq = jnp.mean(wide * wide, axis=-1, keepdims=True)
    return (wide * lax.rsqrt(meansq + epsilon) * gain).astype(jnp.bfloat16)


def lookup(table, index):
    hits = index[:, None] == jnp.arange(table.shape[0], dtype=jnp.int32)[None, :]
    return jnp.sum(jnp.where(hits, table[None, :], 0), axis=-1)


def make_mask(query_pos, key_pos, window_reach, valid_count, frame_len, total):
    distance = jnp.abs(query_pos[:, None] - key_pos[None, :])
    inside = (key_pos >= 0) & (key_pos < total)
    clamped = jnp.clip(key_pos, 0, total - 1)
    key_count = lookup(valid_count, clamped // frame_len)
    reach_rows = lookup(window_reach, query_pos // frame_len)
    living = (clamped % frame_len >= frame_len - key_count)[None, :] | (distance == 0)
    return (distance <= reach_rows[:, None]) & inside[None, :] & living


def attend(query_rows, key_rows, value_rows, allowed):
    rows_q = query_rows.shape[0]
    rows_k = key_rows.shape[0]
    query_heads = query_rows.reshape(rows_q, H, HD)
    key_heads = key_rows.reshape(rows_k, H, HD)
    value_heads = value_rows.reshape(rows_k, H, HD)
    scores = jnp.einsum(
        "qhd,khd->hqk", query_heads, key_heads, preferred_element_type=jnp.float32
    ) * HD ** (-0.5)
    scores = jnp.where(allowed[None], scores, -jnp.inf)
    highest = jnp.max(scores, axis=-1, keepdims=True)
    expon = jnp.exp(scores - highest)
    weights = (expon / jnp.sum(expon, axis=-1, keepdims=True)).astype(jnp.bfloat16)
    mixed = jnp.einsum("hqk,khd->qhd", weights, value_heads, preferred_element_type=jnp.float32)
    return mixed.astype(jnp.bfloat16).reshape(rows_q, H * HD)


def temporal(columns, positions, valid_count, frame_len):
    count = columns.shape[1]
    split = columns.reshape(F, count, 3, H, HD)
    scores = jnp.einsum(
        "fphd,gphd->hpfg", split[:, :, 0], split[:, :, 1], preferred_element_type=jnp.float32
    ) * HD ** (-0.5)
    living = positions[:, None] >= frame_len - valid_count[None, :]
    diagonal = jnp.eye(F, dtype=bool)
    allowed = living[:, None, :] | diagonal[None]
    scores = jnp.where(allowed[None], scores, -jnp.inf)
    highest = jnp.max(scores, axis=-1, keepdims=True)
    expon = jnp.exp(scores - highest)
    weights = (expon / jnp.sum(expon, axis=-1, keepdims=True)).astype(jnp.bfloat16)
    mixed = jnp.einsum(
        "hpfg,gphd->fphd", weights, split[:, :, 2], preferred_element_type=jnp.float32
    )
    return mixed.astype(jnp.bfloat16).reshape(F * count, H * HD)


def on_device(
    frame_tokens,
    window_reach,
    valid_count,
    space_gain,
    space_project,
    space_output,
    time_gain,
    time_project,
    time_output,
):
    devices = lax.axis_size("strip")
    device_index = lax.axis_index("strip")
    local_rows = frame_tokens.shape[0]
    total_rows = local_rows * devices
    frame_len = total_rows // F
    per_frame = devices // F
    piece = local_rows // devices
    offset = device_index * local_rows
    query_pos = offset + jnp.arange(local_rows, dtype=jnp.int32)
    key_pos = offset - HALO + jnp.arange(local_rows + 2 * HALO, dtype=jnp.int32)
    allowed = make_mask(query_pos, key_pos, window_reach, valid_count, frame_len, total_rows)
    query_weight = space_project[:, :D]
    pair_weight = space_project[:, D:]
    state = frame_tokens
    for layer in range(LAYERS):
        hidden = normed(state, space_gain)
        queries = jnp.dot(hidden, query_weight, preferred_element_type=jnp.float32).astype(
            jnp.bfloat16
        )
        pairs = jnp.dot(hidden, pair_weight, preferred_element_type=jnp.float32).astype(
            jnp.bfloat16
        )
        beside_all = padded(pairs, (("strip", 0),), HALO)
        mixed = attend(queries, beside_all[:, :D], beside_all[:, D:], allowed)
        update = jnp.dot(mixed, space_output, preferred_element_type=jnp.float32)
        state = (state.astype(jnp.float32) + update).astype(jnp.bfloat16)
    time_hidden = normed(state, time_gain)
    gathered = lax.all_to_all(
        time_hidden.reshape(devices, piece, D), "strip", split_axis=0, concat_axis=0, tiled=True
    )
    columns = jnp.dot(
        gathered.reshape(devices * piece, D), time_project, preferred_element_type=jnp.float32
    ).astype(jnp.bfloat16)
    columns = columns.reshape(F, per_frame * piece, 3 * D)
    quarter = jnp.arange(per_frame, dtype=jnp.int32)[:, None] * local_rows
    within = device_index * piece + jnp.arange(piece, dtype=jnp.int32)[None, :]
    positions = (quarter + within).reshape(per_frame * piece)
    time_mixed = temporal(columns, positions, valid_count, frame_len)
    time_update = jnp.dot(time_mixed, time_output, preferred_element_type=jnp.float32).astype(
        jnp.bfloat16
    )
    returned = lax.all_to_all(
        time_update.reshape(devices, piece, D), "strip", split_axis=0, concat_axis=0, tiled=True
    )
    returned = returned.reshape(local_rows, D)
    return (state.astype(jnp.float32) + returned.astype(jnp.float32)).astype(jnp.bfloat16)


def solution(mesh):
    return jax.shard_map(
        on_device,
        mesh=mesh,
        in_specs=(
            P(("group", "strip"), None),
            P("group"),
            P("group"),
            P(),
            P(),
            P(),
            P(),
            P(),
            P(),
        ),
        out_specs=P(("group", "strip"), None),
        check_vma=False,
    )
```

profile of v0, /device:TPU:1, one launch (start us, length us, event | category | flops | bytes accessed | tf_op | source)
XLA Modules:
  0.0 188.5 jit_solution(14769032596906128529)
XLA Ops:
  1.5 3.4 %convolution_convert_fusion.2 = bf16[512,1536]{1,0:T(8,128)(2,1)S(1)} fusion(bf16[768,2304]{1,0:T(8,128)(2,1)} %param.13, bf16[512,768]{1,0:T(8,128)(2,1)} %param.9, f32[768]{0:T(1024)} %param.12, f32[512]{0:T(512)S(1)} %add_rsqrt_fusion.2), kind=kOutput, calls=%fused_computation.24 | convolution fusion | flops 1210318848 | bytes 4724736 | tf_op jit(solution)/shard_map/dot_general | solution.py:117
  7.1 1.9 %collective-permute-start.1 = (bf16[128,1536]{1,0:T(8,128)(2,1)}, bf16[128,1536]{1,0:T(8,128)(2,1)}, u32[]{:S(2)}, u32[]{:S(2)}) collective-permute-start(bf16[128,1536]{1,0:T(8,128)(2,1)} %get-tuple-element.15), channel_id=1, source_target_pairs={{1,0},{2,1},{3,2},{4,3},{5,4},{6,5},{7,6},{8,7},{9,8},{10,9},{11,1... | collective-permute-start | bytes 1179656 | tf_op jit(solution)/shard_map/ppermute | solution.py:25
  9.0 4.5 %collective-permute-start = (bf16[128,1536]{1,0:T(8,128)(2,1)}, bf16[128,1536]{1,0:T(8,128)(2,1)}, u32[]{:S(2)}, u32[]{:S(2)}) collective-permute-start(bf16[128,1536]{1,0:T(8,128)(2,1)} %get-tuple-element.14), channel_id=1, source_target_pairs={{0,1},{1,2},{2,3},{3,4},{4,5},{5,6},{6,7},{7,8},{8,9},{9,10},{10,1... | collective-permute-start | bytes 1179656 | tf_op jit(solution)/shard_map/ppermute | solution.py:24
  13.6 3.0 %convolution_convert_fusion.6 = bf16[512,768]{1,0:T(8,128)(2,1)} fusion(bf16[768,2304]{1,0:T(8,128)(2,1)} %param.13, bf16[512,768]{1,0:T(8,128)(2,1)S(1)} %copy-done.5, f32[768]{0:T(1024)S(1)} %copy-done.14, f32[512]{0:T(512)S(1)} %add_rsqrt_fusion.2), kind=kOutput, calls=%fused_computation.71 | convolution fusion | flops 605945856 | bytes 2757632 | tf_op jit(solution)/shard_map/dot_general | solution.py:114
  17.4 2.3 %copy.32 = bf16[512,768]{0,1:T(8,128)(2,1)} copy(bf16[512,768]{1,0:T(8,128)(2,1)} %convolution_convert_fusion.6) | data formatting | bytes 1572864 | tf_op jit(solution)/shard_map/convert_element_type | solution.py:114
  20.4 2.2 %fusion.35 = pred[512,768]{1,0:T(8,128)(4,1)} fusion(s32[512]{0:T(512)S(1)} %select_reduce_fusion.1, s32[768]{0:T(1024)S(1)} %get-tuple-element.29, s32[512]{0:T(512)S(1)} %get-tuple-element.27, pred[768]{0:T(1024)(128)(4,1)S(1)} %fusion.49, pred[768]{0:T(1024)(128)(4,1)} %fusion.55), kind=kLoop, calls=%fused_computation.63 | loop fusion | flops 2752512 | bytes 401920 | tf_op jit(solution)/shard_map/and | solution.py:48
  22.6 1.7 pad_maximum_fusion
  25.9 2.4 %copy.31 = bf16[768,768]{0,1:T(8,128)(2,1)} copy(bf16[768,768]{1,0:T(8,128)(2,1)} %get-tuple-element.11) | data formatting | bytes 2359296 | tf_op jit(solution)/shard_map/slice | solution.py:121
  28.3 2.4 %copy.33 = bf16[768,768]{0,1:T(8,128)(2,1)} copy(bf16[768,768]{1,0:T(8,128)(2,1)} %get-tuple-element.10) | data formatting | bytes 2359296 | tf_op jit(solution)/shard_map/slice | solution.py:121
  30.7 12.2 %fusion.75 = (f32[12,512]{1,0:T(8,128)}, f32[12,512,768]{2,1,0:T(8,128)}) fusion(pred[512,768]{1,0:T(8,128)(4,1)} %fusion.35, bf16[512,12,64]{0,2,1:T(8,128)(2,1)} %bitcast.54, bf16[768,12,64]{0,2,1:T(8,128)(2,1)} %bitcast.53), kind=kOutput, calls=%fused_computation.123 | convolution fusion | flops 622854912 | bytes 21258240 | tf_op jit(solution)/shard_map/sub | solution.py:62
  42.9 8.5 %fusion.42 = bf16[12,64,512]{2,1,0:T(8,128)(2,1)S(1)} fusion(bf16[768,12,64]{0,2,1:T(8,128)(2,1)} %bitcast.51, f32[12,512,768]{2,1,0:T(8,128)} %get-tuple-element.17, f32[12,512]{1,0:T(8,128)} %get-tuple-element.16), kind=kOutput, calls=%fused_computation.68 | convolution fusion | flops 613810176 | bytes 20865024 | tf_op jit(solution)/shard_map/hqk,khd->qhd/dot_general | solution.py:64
  57.2 1.9 %collective-permute-start.3 = (bf16[128,1536]{1,0:T(8,128)(2,1)}, bf16[128,1536]{1,0:T(8,128)(2,1)}, u32[]{:S(2)}, u32[]{:S(2)}) collective-permute-start(bf16[128,1536]{1,0:T(8,128)(2,1)} %get-tuple-element.13), channel_id=1, source_target_pairs={{1,0},{2,1},{3,2},{4,3},{5,4},{6,5},{7,6},{8,7},{9,8},{10,9},{11,1... | collective-permute-start | bytes 1179656 | tf_op jit(solution)/shard_map/ppermute | solution.py:25
  59.2 3.8 %collective-permute-start.2 = (bf16[128,1536]{1,0:T(8,128)(2,1)}, bf16[128,1536]{1,0:T(8,128)(2,1)}, u32[]{:S(2)}, u32[]{:S(2)}) collective-permute-start(bf16[128,1536]{1,0:T(8,128)(2,1)} %get-tuple-element.12), channel_id=1, source_target_pairs={{0,1},{1,2},{2,3},{3,4},{4,5},{5,6},{6,7},{7,8},{8,9},{9,10},{10,1... | collective-permute-start | bytes 1179656 | tf_op jit(solution)/shard_map/ppermute | solution.py:24
  63.0 1.7 convolution_convert_fusion.5
  64.7 2.3 %copy.35 = bf16[512,768]{0,1:T(8,128)(2,1)} copy(bf16[512,768]{1,0:T(8,128)(2,1)} %convolution_convert_fusion.5) | data formatting | bytes 1572864 | tf_op jit(solution)/shard_map/convert_element_type | solution.py:114
  67.1 4.8 %collective-permute-done.2 = bf16[128,1536]{1,0:T(8,128)(2,1)} collective-permute-done((bf16[128,1536]{1,0:T(8,128)(2,1)}, bf16[128,1536]{1,0:T(8,128)(2,1)}, u32[]{:S(2)}, u32[]{:S(2)}) %collective-permute-start.2) | collective-permute-done | bytes 393248 | tf_op jit(solution)/shard_map/ppermute | solution.py:24
  71.9 1.7 pad_maximum_fusion.1
  75.2 2.4 %copy.34 = bf16[768,768]{0,1:T(8,128)(2,1)} copy(bf16[768,768]{1,0:T(8,128)(2,1)} %get-tuple-element.9) | data formatting | bytes 2359296 | tf_op jit(solution)/shard_map/slice | solution.py:121
  77.6 2.4 %copy.36 = bf16[768,768]{0,1:T(8,128)(2,1)} copy(bf16[768,768]{1,0:T(8,128)(2,1)} %get-tuple-element.8) | data formatting | bytes 2359296 | tf_op jit(solution)/shard_map/slice | solution.py:121
  80.0 12.2 %fusion.76 = (f32[12,512]{1,0:T(8,128)}, f32[12,512,768]{2,1,0:T(8,128)}) fusion(pred[512,768]{1,0:T(8,128)(4,1)} %fusion.35, bf16[512,12,64]{0,2,1:T(8,128)(2,1)} %bitcast.55, bf16[768,12,64]{0,2,1:T(8,128)(2,1)} %bitcast.52), kind=kOutput, calls=%fused_computation.124 | convolution fusion | flops 622854912 | bytes 21258240 | tf_op jit(solution)/shard_map/sub | solution.py:62
  92.2 8.5 %fusion.41 = bf16[12,64,512]{2,1,0:T(8,128)(2,1)S(1)} fusion(bf16[768,12,64]{0,2,1:T(8,128)(2,1)} %bitcast.50, f32[12,512,768]{2,1,0:T(8,128)} %get-tuple-element.21, f32[12,512]{1,0:T(8,128)} %get-tuple-element.20), kind=kOutput, calls=%fused_computation.67 | convolution fusion | flops 613810176 | bytes 20865024 | tf_op jit(solution)/shard_map/hqk,khd->qhd/dot_general | solution.py:64
  103.8 6.2 %all-to-all-start = ((bf16[16,32,768]{2,1,0:T(8,128)(2,1)}), bf16[16,32,768]{2,1,0:T(8,128)(2,1)}, u32[]{:S(2)}, u32[]{:S(2)}) async-start(bf16[16,32,768]{2,1,0:T(8,128)(2,1)} %bitcast.49), calls=%async_computation | async-start | bytes 1572864 | tf_op jit(solution)/shard_map/all_to_all | solution.py:125
  110.9 17.8 %all-to-all-done = bf16[16,32,768]{2,1,0:T(8,128)(2,1)} async-done(((bf16[16,32,768]{2,1,0:T(8,128)(2,1)}), bf16[16,32,768]{2,1,0:T(8,128)(2,1)}, u32[]{:S(2)}, u32[]{:S(2)}) %all-to-all-start) | async-done | bytes 786464 | tf_op jit(solution)/shard_map/all_to_all | solution.py:125
  128.7 4.6 %convolution_convert_fusion = bf16[512,2304]{1,0:T(8,128)(2,1)} fusion(bf16[512,768]{1,0:T(8,128)(2,1)} %bitcast.11, bf16[768,2304]{1,0:T(8,128)(2,1)S(1)} %copy-done), kind=kOutput, calls=%fused_computation.19 | convolution fusion | flops 1813118976 | bytes 6684672 | tf_op jit(solution)/shard_map/dot_general | solution.py:128
  133.3 8.2 %reshape_reshape.3 = bf16[16,32,3,12,64]{4,3,2,1,0:T(8,128)(2,1)} reshape(bf16[512,2304]{1,0:T(8,128)(2,1)} %convolution_convert_fusion) | data formatting | bytes 4718592 | tf_op jit(solution)/shard_map/reshape;reshape | solution.py:70
  141.4 4.8 %fusion.70 = (bf16[16,32,1,12,64]{4,3,2,1,0:T(8,128)(2,1)S(1)}, bf16[16,32,1,12,64]{4,3,2,1,0:T(8,128)(2,1)S(1)}, bf16[16,32,1,12,64]{4,3,2,1,0:T(8,128)(2,1)S(1)}) fusion(bf16[16,32,3,12,64]{4,3,2,1,0:T(8,128)(2,1)} %reshape_reshape.3), kind=kLoop, calls=%fused_computation.118 | loop fusion | bytes 4718592 | tf_op jit(solution)/shard_map/slice | solution.py:82
  146.3 3.5 %fusion.28 = f32[12,32,16,16]{2,3,1,0:T(8,128)S(1)} fusion(bf16[16,32,1,12,64]{4,3,2,1,0:T(8,128)(2,1)S(1)} %get-tuple-element.6, bf16[16,32,1,12,64]{4,3,2,1,0:T(8,128)(2,1)S(1)} %get-tuple-element.7), kind=kOutput, calls=%fused_computation.53 | convolution fusion | flops 12582912 | bytes 1966080 | tf_op jit(solution)/shard_map/fphd,gphd->hpfg/dot_general | solution.py:71
  149.8 2.2 %fusion.77 = (f32[12,32,16]{2,1,0:T(8,128)S(1)}, f32[12,32,16,16]{2,3,1,0:T(8,128)S(1)}) fusion(f32[12,32,16,16]{2,3,1,0:T(8,128)S(1)} %fusion.28, pred[32,16,16]{1,2,0:T(8,128)(4,1)S(1)} %copy-done.7), kind=kOutput, calls=%fused_computation.125 | output fusion | flops 589839 | bytes 819200 | tf_op jit(solution)/shard_map/sub | solution.py:79
  153.4 1.9 copy.41
  155.3 3.9 %reshape.261 = bf16[512,768]{1,0:T(8,128)(2,1)} reshape(bf16[16,32,12,64]{3,2,1,0:T(8,128)(2,1)} %copy.41) | data formatting | bytes 1572864 | tf_op jit(solution)/shard_map/reshape | solution.py:84
  159.1 2.4 %convolution_convert_fusion.4 = bf16[512,768]{1,0:T(8,128)(2,1)S(1)} fusion(bf16[512,768]{1,0:T(8,128)(2,1)} %reshape.261, bf16[768,768]{1,0:T(8,128)(2,1)} %param.17), kind=kOutput, calls=%fused_computation.69 | convolution fusion | flops 604372992 | bytes 2752512 | tf_op jit(solution)/shard_map/dot_general | solution.py:136
  161.5 25.9 %all_to_all.10 = bf16[16,32,768]{2,1,0:T(8,128)(2,1)S(1)} all-to-all(bf16[16,32,768]{2,1,0:T(8,128)(2,1)S(1)} %bitcast.56), channel_id=1, replica_groups=mesh['group'=2,'strip'=16] {'strip'}, dimensions={0} | all-to-all | bytes 1572864 | tf_op jit(solution)/shard_map/all_to_all | solution.py:139
  (64 shorter events, 20.3 us)
Async XLA Ops:
  0.0 128.7 %copy-start = (bf16[768,2304]{1,0:T(8,128)(2,1)S(1)}, bf16[768,2304]{1,0:T(8,128)(2,1)}, u32[]{:S(2)}) copy-start(bf16[768,2304]{1,0:T(8,128)(2,1)} %param.16) | copy-start | bytes 10616836
  1.5 12.1 %copy-start.5 = (bf16[512,768]{1,0:T(8,128)(2,1)S(1)}, bf16[512,768]{1,0:T(8,128)(2,1)}, u32[]{:S(2)}) copy-start(bf16[512,768]{1,0:T(8,128)(2,1)} %param.9) | copy-start | bytes 2359300
  1.5 12.1 %copy-start.14 = (f32[768]{0:T(1024)S(1)}, f32[768]{0:T(1024)}, u32[]{:S(2)}) copy-start(f32[768]{0:T(1024)} %param.12) | copy-start | bytes 9220
  5.0 1.2 copy-start.1
  7.1 15.5 %collective-permute-start.1 = (bf16[128,1536]{1,0:T(8,128)(2,1)}, bf16[128,1536]{1,0:T(8,128)(2,1)}, u32[]{:S(2)}, u32[]{:S(2)}) collective-permute-start(bf16[128,1536]{1,0:T(8,128)(2,1)} %get-tuple-element.15), channel_id=1, source_target_pairs={{1,0},{2,1},{3,2},{4,3},{5,4},{6,5},{7,6},{8,7},{9,8},{10,9},{11,1... | collective-permute-start | bytes 1179656 | tf_op jit(solution)/shard_map/ppermute | solution.py:25
  9.0 13.5 %collective-permute-start = (bf16[128,1536]{1,0:T(8,128)(2,1)}, bf16[128,1536]{1,0:T(8,128)(2,1)}, u32[]{:S(2)}, u32[]{:S(2)}) collective-permute-start(bf16[128,1536]{1,0:T(8,128)(2,1)} %get-tuple-element.14), channel_id=1, source_target_pairs={{0,1},{1,2},{2,3},{3,4},{4,5},{5,6},{6,7},{7,8},{8,9},{9,10},{10,1... | collective-permute-start | bytes 1179656 | tf_op jit(solution)/shard_map/ppermute | solution.py:24
  13.6 3.1 %copy-start.9 = (s32[16]{0:T(128)S(1)}, s32[16]{0:T(128)}, u32[]{:S(2)}) copy-start(s32[16]{0:T(128)} %param.11) | copy-start | bytes 196
  42.9 8.5 %copy-start.6 = (bf16[512,768]{1,0:T(8,128)(2,1)S(1)}, bf16[512,768]{1,0:T(8,128)(2,1)}, u32[]{:S(2)}) copy-start(bf16[512,768]{1,0:T(8,128)(2,1)} %param.9) | copy-start | bytes 2359300
  42.9 8.6 %copy-start.12 = (bf16[768,768]{1,0:T(8,128)(2,1)S(1)}, bf16[768,768]{1,0:T(8,128)(2,1)}, u32[]{:S(2)}) copy-start(bf16[768,768]{1,0:T(8,128)(2,1)} %param.14) | copy-start | bytes 3538948
  51.5 2.2 %copy-start.11 = (bf16[768,2304]{1,0:T(8,128)(2,1)S(1)}, bf16[768,2304]{1,0:T(8,128)(2,1)}, u32[]{:S(2)}) copy-start(bf16[768,2304]{1,0:T(8,128)(2,1)} %param.13) | copy-start | bytes 10616836
  51.5 2.2 %copy-start.15 = (f32[768]{0:T(1024)S(1)}, f32[768]{0:T(1024)}, u32[]{:S(2)}) copy-start(f32[768]{0:T(1024)} %param.12) | copy-start | bytes 9220
  52.4 10.5 %copy-start.16 = (bf16[512,768]{1,0:T(8,128)(2,1)}, bf16[512,768]{1,0:T(8,128)(2,1)S(1)}, u32[]{:S(2)}) copy-start(bf16[512,768]{1,0:T(8,128)(2,1)S(1)} %get-tuple-element.19) | copy-start | bytes 2359300
  55.1 1.2 copy-start.2
  57.2 9.8 %collective-permute-start.3 = (bf16[128,1536]{1,0:T(8,128)(2,1)}, bf16[128,1536]{1,0:T(8,128)(2,1)}, u32[]{:S(2)}, u32[]{:S(2)}) collective-permute-start(bf16[128,1536]{1,0:T(8,128)(2,1)} %get-tuple-element.13), channel_id=1, source_target_pairs={{1,0},{2,1},{3,2},{4,3},{5,4},{6,5},{7,6},{8,7},{9,8},{10,9},{11,1... | collective-permute-start | bytes 1179656 | tf_op jit(solution)/shard_map/ppermute | solution.py:25
  59.2 12.8 %collective-permute-start.2 = (bf16[128,1536]{1,0:T(8,128)(2,1)}, bf16[128,1536]{1,0:T(8,128)(2,1)}, u32[]{:S(2)}, u32[]{:S(2)}) collective-permute-start(bf16[128,1536]{1,0:T(8,128)(2,1)} %get-tuple-element.12), channel_id=1, source_target_pairs={{0,1},{1,2},{2,3},{3,4},{4,5},{5,6},{6,7},{7,8},{8,9},{9,10},{10,1... | collective-permute-start | bytes 1179656 | tf_op jit(solution)/shard_map/ppermute | solution.py:24
  92.2 8.5 %copy-start.13 = (bf16[768,768]{1,0:T(8,128)(2,1)S(1)}, bf16[768,768]{1,0:T(8,128)(2,1)}, u32[]{:S(2)}) copy-start(bf16[768,768]{1,0:T(8,128)(2,1)} %param.14) | copy-start | bytes 3538948
  92.2 8.6 %copy-start.17 = (bf16[512,768]{1,0:T(8,128)(2,1)S(1)}, bf16[512,768]{1,0:T(8,128)(2,1)}, u32[]{:S(2)}) copy-start(bf16[512,768]{1,0:T(8,128)(2,1)} %copy-done.16) | copy-start | bytes 2359300
  100.8 1.8 copy-start.8
  101.8 0.9 copy-start.3
  101.8 8.2 %copy-start.10 = (s32[16]{0:T(128)S(1)}, s32[16]{0:T(128)}, u32[]{:S(2)}) copy-start(s32[16]{0:T(128)} %param.11) | copy-start | bytes 196
  103.8 24.9 %all-to-all-start = ((bf16[16,32,768]{2,1,0:T(8,128)(2,1)}), bf16[16,32,768]{2,1,0:T(8,128)(2,1)}, u32[]{:S(2)}, u32[]{:S(2)}) async-start(bf16[16,32,768]{2,1,0:T(8,128)(2,1)} %bitcast.49), calls=%async_computation | async-start | bytes 1572864 | tf_op jit(solution)/shard_map/all_to_all | solution.py:125
  146.3 3.5 %copy-start.7 = (pred[32,16,16]{1,2,0:T(8,128)(4,1)S(1)}, pred[32,16,16]{1,2,0:T(8,128)(4,1)}, u32[]{:S(2)}) copy-start(pred[32,16,16]{1,2,0:T(8,128)(4,1)} %broadcast_or_fusion) | copy-start | bytes 24580
  159.1 28.2 %copy-start.4 = (bf16[512,768]{1,0:T(8,128)(2,1)S(1)}, bf16[512,768]{1,0:T(8,128)(2,1)}, u32[]{:S(2)}) copy-start(bf16[512,768]{1,0:T(8,128)(2,1)} %copy-done.3) | copy-start | bytes 2359300
where the time goes:
time: 189 us; the launch traced here: 188 us
  matrix products  64.8 us (34%)
  local copies, waits for them, and re-layouts  42.4 us (22%)
  blocking collectives  25.9 us (14%)
  waiting for transfers between devices  22.7 us (12%)
  starting transfers between devices  18.4 us (10%)
  other arithmetic  14 us (7%)
    all_to_all x1, blocking collectives, on_device(): lax.all_to_all(time_update.reshape(devices, piece, D), 'strip', split_axi...  25.9 us
    sub x2, matrix products, attend(): expon = jnp.exp(scores - highest)  24.5 us
    all_to_all x1, waiting for transfers between devices, on_device(): lax.all_to_all(time_hidden.reshape(devices, piece, D), 'strip', split_axi...  17.8 us
    dot_general x2, matrix products, attend(): jnp.einsum('hqk,khd->qhd', weights, value_heads, preferred_element_type=j...  17.1 us
    slice x6, local copies, waits for them, and re-layouts, on_device(): mixed = attend(queries, beside_all[:, :D], beside_all[:, D:], allowed)  12.7 us
    ppermute x2, starting transfers between devices, padded(): before = lax.ppermute(last, axis, up)  8.36 us
    another operation x1, local copies, waits for them, and re-layouts, temporal(): split = columns.reshape(F, count, 3, H, HD)  8.16 us
    all_to_all x1, starting transfers between devices, on_device(): lax.all_to_all(time_hidden.reshape(devices, piece, D), 'strip', split_axi...  6.2 us
  transfers between devices with their start and end apart: 5, of which 2 were waited for; matrix products, arithmetic and copies ran while one was open for 7% of the time, Pallas kernels for 0%

commit v1 on v0

v1 whole, which is shorter than its diff:
```python
import functools

import jax
import jax.numpy as jnp
from jax import lax
from jax.experimental import pallas as pl
from jax.experimental.pallas import tpu as pltpu
from jax.sharding import PartitionSpec as P

F = 16
HALO = 128
H = 12
HD = 64
D = 768
BLK = HALO
WIN = 3 * BLK
PAIR = 2 * HD
CHUNK = 2 * BLK
COLS = 256
EPS = 1e-06
MASKED = -1e30

BF16 = jnp.bfloat16
F32 = jnp.float32


def norm_rows(values, gain):
    wide = values.astype(F32)
    meansq = jnp.mean(wide * wide, axis=-1, keepdims=True)
    return (wide * lax.rsqrt(meansq + EPS) * gain).astype(BF16)


def project(x, weight_ref, first, last, store):
    def step(i, carry):
        at = pl.multiple_of(first + i * COLS, COLS)
        store(at, jnp.dot(x, weight_ref[:, pl.ds(at, COLS)], preferred_element_type=F32))
        return carry

    lax.fori_loop(0, (last - first) // COLS, step, 0)


def pair_attention(q, k, v, bias):
    rows = q.shape[0]
    lane = lax.broadcasted_iota(jnp.int32, (1, PAIR), 1)
    scale = HD ** (-0.5)
    left = jnp.where(lane < HD, scale, 0.0).astype(BF16)
    right = jnp.where(lane < HD, 0.0, scale).astype(BF16)
    both = jnp.concatenate([q * left, q * right], axis=0)
    scores = lax.dot_general(both, k, (((1,), (1,)), ((), ())), preferred_element_type=F32)
    scores = scores.reshape(2, rows, -1) + bias[None]
    highest = jnp.max(scores, axis=-1, keepdims=True)
    expon = jnp.exp(scores - highest)
    total = jnp.sum(expon, axis=-1, keepdims=True)
    mixed = jnp.dot(expon.reshape(2 * rows, -1).astype(BF16), v, preferred_element_type=F32)
    mixed = mixed.reshape(2, rows, PAIR) * (1.0 / total)
    return jnp.where(lane < HD, mixed[0], mixed[1]).astype(BF16)


def window_bias(start, reach_ref, count_ref, frame_len, total):
    row = lax.broadcasted_iota(jnp.int32, (BLK, WIN), 0)
    col = lax.broadcasted_iota(jnp.int32, (BLK, WIN), 1)
    distance = col - BLK - row
    reach = reach_ref[lax.div(jnp.clip(start, 0, total - 1), frame_len)]
    least = jnp.zeros((1, WIN), jnp.int32)
    place = lax.broadcasted_iota(jnp.int32, (1, WIN), 1)
    for j in range(3):
        at = start + (j - 1) * BLK
        inside = (at >= 0) & (at < total)
        frame = lax.div(jnp.clip(at, 0, total - 1), frame_len)
        first = (frame + 1) * frame_len - count_ref[frame] - at
        first = jnp.where(inside, first, WIN) + j * BLK
        least = jnp.where(place >= j * BLK, first, least)
    living = (col >= least) | (distance == 0)
    return jnp.where((jnp.abs(distance) <= reach) & living, 0.0, MASKED).astype(F32)


def space_attention(blocks, start_of, q_ref, k_ref, v_ref, bias_ref, mixed_ref, tables):
    def one_block(i, carry):
        rows = pl.ds(pl.multiple_of(i * BLK, BLK), BLK)
        keys = pl.ds(pl.multiple_of(i * BLK, BLK), WIN)
        bias_ref[...] = window_bias(start_of(i), *tables)
        for pair in range(H // 2):
            lanes = slice(pair * PAIR, (pair + 1) * PAIR)
            mixed_ref[rows, lanes] = pair_attention(
                q_ref[rows, lanes], k_ref[keys, lanes], v_ref[keys, lanes], bias_ref[...]
            )
        return carry

    lax.fori_loop(0, blocks, one_block, 0)


def middle_kernel(
    frame_len,
    total,
    reach_ref,
    count_ref,
    index_ref,
    x_ref,
    gain_ref,
    project_ref,
    output_ref,
    first_ref,
    state_ref,
    second_ref,
    q_s,
    k_s,
    v_s,
    mixed_s,
    bias_s,
):
    rows = x_ref.shape[0]
    inner = rows - 2 * BLK
    offset = index_ref[0] * rows
    gain = gain_ref[...]

    def store_first(at, value):
        first_ref[:, pl.ds(at, COLS)] = value.astype(BF16)

    project(norm_rows(x_ref[...], gain), project_ref, 0, 3 * D, store_first)
    q_s[...] = first_ref[BLK : rows - BLK, :D]
    k_s[...] = first_ref[:, D : 2 * D]
    v_s[...] = first_ref[:, 2 * D :]
    tables = (reach_ref, count_ref, frame_len, total)
    space_attention(
        inner // BLK, lambda i: offset + (i + 1) * BLK, q_s, k_s, v_s, bias_s, mixed_s, tables
    )

    def store_state(at, value):
        old = x_ref[BLK : rows - BLK, pl.ds(at, COLS)].astype(F32)
        state_ref[:, pl.ds(at, COLS)] = (old + value).astype(BF16)

    project(mixed_s[...], output_ref, 0, D, store_state)

    def store_second(at, value):
        second_ref[:, pl.ds(at, COLS)] = value.astype(BF16)

    project(norm_rows(state_ref[...], gain), project_ref, 0, 3 * D, store_second)


def side_kernel(
    frame_len,
    total,
    local_rows,
    after,
    reach_ref,
    count_ref,
    index_ref,
    halo_ref,
    x_ref,
    first_ref,
    middle_ref,
    second_ref,
    gain_ref,
    time_gain_ref,
    project_ref,
    output_ref,
    state_ref,
    hidden_ref,
    q_s,
    k_s,
    v_s,
    mixed_s,
    edge_s,
    bias_s,
):
    offset = index_ref[0] * local_rows
    gain = gain_ref[...]
    half = 2 * BLK
    tables = (reach_ref, count_ref, frame_len, total)
    if after:
        start = offset + local_rows - half
        own, far = 0, half
        own_edge = slice(half - BLK, half)
        far_edge = slice(0, BLK)
        edge_blocks = (0, BLK)
    else:
        start = offset - half
        own, far = half, 0
        own_edge = slice(0, BLK)
        far_edge = slice(BLK, half)
        edge_blocks = (BLK, 0)
    own_at, far_at = edge_blocks
    k_s[own : own + half, :] = first_ref[:, D : 2 * D]
    v_s[own : own + half, :] = first_ref[:, 2 * D :]
    q_s[own_at : own_at + BLK, :] = first_ref[own_edge, :D]
    hidden = norm_rows(halo_ref[...], gain)

    def store_query(at, value):
        q_s[far_at : far_at + BLK, pl.ds(at, COLS)] = value.astype(BF16)

    def store_key(at, value):
        k_s[far : far + half, pl.ds(at - D, COLS)] = value.astype(BF16)

    def store_value(at, value):
        v_s[far : far + half, pl.ds(at - 2 * D, COLS)] = value.astype(BF16)

    project(hidden[far_edge], project_ref, 0, D, store_query)
    project(hidden, project_ref, D, 2 * D, store_key)
    project(hidden, project_ref, 2 * D, 3 * D, store_value)
    space_attention(2, lambda i: start + (i + 1) * BLK, q_s, k_s, v_s, bias_s, mixed_s, tables)

    def store_edge(at, value):
        cols = pl.ds(at, COLS)
        edge_s[own_at : own_at + BLK, cols] = (
            x_ref[own_edge, cols].astype(F32) + value[own_at : own_at + BLK]
        ).astype(BF16)
        edge_s[far_at : far_at + BLK, cols] = (
            halo_ref[far_edge, cols].astype(F32) + value[far_at : far_at + BLK]
        ).astype(BF16)

    project(mixed_s[...], output_ref, 0, D, store_edge)

    if after:
        mid, edge, begin = 0, half, start - BLK
        own_mid = slice(BLK, half)
        q_mid, q_edge = 0, BLK
    else:
        mid, edge, begin = half, 0, start + BLK
        own_mid = slice(0, BLK)
        q_mid, q_edge = BLK, 0
    k_s[mid : mid + half, :] = second_ref[:, D : 2 * D]
    v_s[mid : mid + half, :] = second_ref[:, 2 * D :]
    q_s[q_mid : q_mid + BLK, :] = second_ref[own_mid, :D]
    hidden = norm_rows(edge_s[...], gain)

    def store_query2(at, value):
        q_s[q_edge : q_edge + BLK, pl.ds(at, COLS)] = value.astype(BF16)

    def store_key2(at, value):
        k_s[edge : edge + half, pl.ds(at - D, COLS)] = value.astype(BF16)

    def store_value2(at, value):
        v_s[edge : edge + half, pl.ds(at - 2 * D, COLS)] = value.astype(BF16)

    project(hidden[own_at : own_at + BLK], project_ref, 0, D, store_query2)
    project(hidden, project_ref, D, 2 * D, store_key2)
    project(hidden, project_ref, 2 * D, 3 * D, store_value2)
    space_attention(2, lambda i: begin + (i + 1) * BLK, q_s, k_s, v_s, bias_s, mixed_s, tables)

    def store_state(at, value):
        cols = pl.ds(at, COLS)
        state_ref[q_edge : q_edge + BLK, cols] = (
            edge_s[own_at : own_at + BLK, cols].astype(F32) + value[q_edge : q_edge + BLK]
        ).astype(BF16)
        state_ref[q_mid : q_mid + BLK, cols] = (
            middle_ref[own_mid, cols].astype(F32) + value[q_mid : q_mid + BLK]
        ).astype(BF16)

    project(mixed_s[...], output_ref, 0, D, store_state)
    hidden_ref[...] = norm_rows(state_ref[...], time_gain_ref[...])


def time_kernel(
    frame_len,
    local_rows,
    devices,
    chunk,
    count_ref,
    index_ref,
    x_ref,
    project_ref,
    output_ref,
    update_ref,
    qkv_s,
    mixed_s,
    bias_s,
):
    rows = x_ref.shape[0]
    slots = rows // F
    piece = rows // devices

    def store_qkv(at, value):
        qkv_s[:, pl.ds(at, COLS)] = value.astype(BF16)

    project(x_ref[...], project_ref, 0, 3 * D, store_qkv)
    row = lax.broadcasted_iota(jnp.int32, (rows, rows), 0)
    col = lax.broadcasted_iota(jnp.int32, (rows, rows), 1)
    key = lax.broadcasted_iota(jnp.int32, (1, rows), 1)
    key_frame = lax.div(key, slots)
    key_slot = lax.rem(key, slots)
    place = lax.div(key_slot, piece) * local_rows + lax.rem(key_slot, piece)
    place = place + chunk * rows + index_ref[0] * piece
    least = jnp.zeros((1, rows), jnp.int32)
    for g in range(F):
        least = jnp.where(key_frame == g, frame_len - count_ref[g], least)
    living = jnp.where(place >= least, 1, 0)
    same = lax.rem(row, slots) == lax.rem(col, slots)
    bias_s[...] = jnp.where(same & ((living == 1) | (row == col)), 0.0, MASKED).astype(F32)

    for pair in range(H // 2):
        lanes = slice(pair * PAIR, (pair + 1) * PAIR)
        mixed_s[:, lanes] = pair_attention(
            qkv_s[:, lanes],
            qkv_s[:, D + pair * PAIR : D + (pair + 1) * PAIR],
            qkv_s[:, 2 * D + pair * PAIR : 2 * D + (pair + 1) * PAIR],
            bias_s[...],
        )

    def store_update(at, value):
        update_ref[:, pl.ds(at, COLS)] = value.astype(BF16)

    project(mixed_s[...], output_ref, 0, D, store_update)


def smem():
    return pl.BlockSpec(memory_space=pltpu.SMEM)


def rows_of(block_rows, cols, at):
    return pl.BlockSpec((block_rows, cols), lambda i: (at, 0))


def whole(shape):
    return pl.BlockSpec(shape, lambda i: (0,) * len(shape))


def params():
    return pltpu.CompilerParams(
        dimension_semantics=("arbitrary",), vmem_limit_bytes=32 << 20
    )


def cost(flops, bytes_accessed, exps):
    return pl.CostEstimate(flops=flops, bytes_accessed=bytes_accessed, transcendentals=exps)


def on_device(
    frame_tokens,
    window_reach,
    valid_count,
    space_gain,
    space_project,
    space_output,
    time_gain,
    time_project,
    time_output,
):
    devices = lax.axis_size("strip")
    local_rows = frame_tokens.shape[0]
    total = local_rows * devices
    frame_len = total // F
    if local_rows != 2 * CHUNK or frame_len % local_rows or CHUNK % devices:
        raise ValueError("unsupported sizes")
    index = lax.axis_index("strip").reshape(1)
    gain = space_gain.reshape(1, D)
    gain_t = time_gain.reshape(1, D)

    up = [(i, i + 1) for i in range(devices - 1)]
    down = [(i + 1, i) for i in range(devices - 1)]
    before = lax.ppermute(frame_tokens[local_rows - CHUNK :], "strip", up)
    after = lax.ppermute(frame_tokens[:CHUNK], "strip", down)

    weight_bytes = 2 * D * 4 * D
    first, middle, second = pl.pallas_call(
        functools.partial(middle_kernel, frame_len, total),
        grid=(1,),
        out_shape=(
            jax.ShapeDtypeStruct((local_rows, 3 * D), BF16),
            jax.ShapeDtypeStruct((CHUNK, D), BF16),
            jax.ShapeDtypeStruct((CHUNK, 3 * D), BF16),
        ),
        in_specs=[smem(), smem(), smem(), whole((local_rows, D)), whole((1, D)), whole((D, 3 * D)), whole((D, D))],
        out_specs=(whole((local_rows, 3 * D)), whole((CHUNK, D)), whole((CHUNK, 3 * D))),
        scratch_shapes=[
            pltpu.VMEM((CHUNK, D), BF16),
            pltpu.VMEM((local_rows, D), BF16),
            pltpu.VMEM((local_rows, D), BF16),
            pltpu.VMEM((CHUNK, D), BF16),
            pltpu.VMEM((BLK, WIN), F32),
        ],
        compiler_params=params(),
        cost_estimate=cost(2 * D * D * 3 * 3 * CHUNK, weight_bytes, H * CHUNK * WIN),
        name="middle",
    )(window_reach, valid_count, index, frame_tokens, gain, space_project, space_output)

    def side(halo, is_after):
        at = 1 if is_after else 0
        return pl.pallas_call(
            functools.partial(side_kernel, frame_len, total, local_rows, is_after),
            grid=(1,),
            out_shape=(jax.ShapeDtypeStruct((CHUNK, D), BF16),) * 2,
            in_specs=[
                smem(),
                smem(),
                smem(),
                whole((CHUNK, D)),
                rows_of(CHUNK, D, at),
                rows_of(CHUNK, 3 * D, at),
                whole((CHUNK, D)),
                whole((CHUNK, 3 * D)),
                whole((1, D)),
                whole((1, D)),
                whole((D, 3 * D)),
                whole((D, D)),
            ],
            out_specs=(whole((CHUNK, D)),) * 2,
            scratch_shapes=[
                pltpu.VMEM((CHUNK, D), BF16),
                pltpu.VMEM((2 * CHUNK, D), BF16),
                pltpu.VMEM((2 * CHUNK, D), BF16),
                pltpu.VMEM((CHUNK, D), BF16),
                pltpu.VMEM((CHUNK, D), BF16),
                pltpu.VMEM((BLK, WIN), F32),
            ],
            compiler_params=params(),
            cost_estimate=cost(2 * D * D * 8 * CHUNK, weight_bytes, 2 * H * CHUNK * WIN),
            name="after" if is_after else "before",
        )(
            window_reach,
            valid_count,
            index,
            halo,
            frame_tokens,
            first,
            middle,
            second,
            gain,
            gain_t,
            space_project,
            space_output,
        )

    def exchange(x):
        return lax.all_to_all(x, "strip", split_axis=0, concat_axis=0, tiled=True)

    def temporal(x, chunk):
        return pl.pallas_call(
            functools.partial(time_kernel, frame_len, local_rows, devices, chunk),
            grid=(1,),
            out_shape=jax.ShapeDtypeStruct((CHUNK, D), BF16),
            in_specs=[smem(), smem(), whole((CHUNK, D)), whole((D, 3 * D)), whole((D, D))],
            out_specs=whole((CHUNK, D)),
            scratch_shapes=[
                pltpu.VMEM((CHUNK, 3 * D), BF16),
                pltpu.VMEM((CHUNK, D), BF16),
                pltpu.VMEM((CHUNK, CHUNK), F32),
            ],
            compiler_params=params(),
            cost_estimate=cost(2 * D * D * 5 * CHUNK, weight_bytes, H * CHUNK * CHUNK),
            name="time%d" % chunk,
        )(valid_count, index, x, time_project, time_output)

    state0, hidden0 = side(before, False)
    sent0 = exchange(hidden0)
    state1, hidden1 = side(after, True)
    sent1 = exchange(hidden1)
    back0 = exchange(temporal(sent0, 0))
    back1 = exchange(temporal(sent1, 1))
    wide = [
        (s.astype(F32) + b.astype(F32)).astype(BF16) for s, b in ((state0, back0), (state1, back1))
    ]
    return jnp.concatenate(wide, axis=0)


def solution(mesh):
    return jax.shard_map(
        on_device,
        mesh=mesh,
        in_specs=(
            P(("group", "strip"), None),
            P("group"),
            P("group"),
            P(),
            P(),
            P(),
            P(),
            P(),
            P(),
        ),
        out_specs=P(("group", "strip"), None),
        check_vma=False,
    )
```

time: 189 us -> 133 us (0.70)
  matrix products: 64.8 us -> 0 us
  Pallas kernels: 0 us -> 54.3 us
  blocking collectives: 25.9 us -> 0 us
  local copies, waits for them, and re-layouts: 42.4 us -> 21.9 us
  other arithmetic: 14 us -> 1.17 us
  starting transfers between devices: 18.4 us -> 29.5 us
  waiting for transfers between devices: 22.7 us -> 24.8 us
    pallas_call x0 -> x5, Pallas kernels: none -> 54.3 us  [the longest x2 30 us: side(): pl.pallas_call(functools.partial(side_kernel, frame_len, total, local_row...]
    dot_general x12 -> x0, matrix products: 40.4 us -> none  [the longest x2 17.1 us: attend(): jnp.einsum('hqk,khd->qhd', weights, value_heads, preferred_element_type=j...]
    all_to_all x1 -> x0, blocking collectives: 25.9 us -> none  [on_device(): lax.all_to_all(time_update.reshape(devices, piece, D), 'strip', split_axi...]
    sub x2 -> x0, matrix products: 24.5 us -> none  [attend(): expon = jnp.exp(scores - highest)]
    all_to_all x1 -> x4, starting transfers between devices: 6.2 us -> 23.9 us  [exchange(): return lax.all_to_all(x, 'strip', split_axis=0, concat_axis=0, tiled=True)]
    slice x9 -> x1, local copies, waits for them, and re-layouts: 19.4 us -> 1.98 us  [on_device(): before = lax.ppermute(frame_tokens[local_rows - CHUNK:], 'strip', up)]
    unnamed x36 -> x58, local copies, waits for them, and re-layouts: 4.45 us -> 20 us
    another operation x1 -> x0, local copies, waits for them, and re-layouts: 8.16 us -> none  [temporal(): split = columns.reshape(F, count, 3, H, HD)]
  transfers between devices with their start and end apart: 5 -> 6, of which waited for: 2 -> 4; matrix products, arithmetic and copies ran while one was open for 7% -> 0% of each run, Pallas kernels for 0% -> 30%
where the time goes in v1:
time: 133 us; the launch traced here: 132 us
  Pallas kernels  54.3 us (41%)
  starting transfers between devices  29.5 us (22%)
  waiting for transfers between devices  24.8 us (19%)
  local copies, waits for them, and re-layouts  21.9 us (16%)
    pallas_call x2, Pallas kernels, side(): pl.pallas_call(functools.partial(side_kernel, frame_len, total, local_row...  30 us
    all_to_all x4, starting transfers between devices, exchange(): return lax.all_to_all(x, 'strip', split_axis=0, concat_axis=0, tiled=True)  23.9 us
    unnamed x58, local copies, waits for them, and re-layouts  20 us
    all_to_all x4, waiting for transfers between devices, exchange(): return lax.all_to_all(x, 'strip', split_axis=0, concat_axis=0, tiled=True)  17.8 us
    pallas_call x2, Pallas kernels, temporal(): pl.pallas_call(functools.partial(time_kernel, frame_len, local_rows, devi...  12.5 us
    pallas_call x1, Pallas kernels, on_device(): pl.pallas_call(functools.partial(middle_kernel, frame_len, total), grid=(...  11.8 us
    ppermute x1, waiting for transfers between devices, on_device(): before = lax.ppermute(frame_tokens[local_rows - CHUNK:], 'strip', up)  6.98 us
    ppermute x1, starting transfers between devices, on_device(): before = lax.ppermute(frame_tokens[local_rows - CHUNK:], 'strip', up)  3.71 us
  transfers between devices with their start and end apart: 6, of which 4 were waited for; matrix products, arithmetic and copies ran while one was open for 0% of the time, Pallas kernels for 30%

profile of v1, /device:TPU:1, one launch (start us, length us, event | category | flops | bytes accessed | tf_op | source)
XLA Modules:
  0.0 132.0 jit_solution(5351178551821742716)
XLA Ops:
  0.0 2.0 %fusion.2 = (bf16[256,768]{1,0:T(8,128)(2,1)}, bf16[256,768]{1,0:T(8,128)(2,1)S(1)}) fusion(bf16[512,768]{1,0:T(8,128)(2,1)} %x_ref.5), kind=kLoop, calls=%fused_computation.5 | loop fusion | bytes 1572864 | tf_op jit(solution)/shard_map/slice | solution.py:350
  2.0 1.9 %collective-permute-start.1 = (bf16[256,768]{1,0:T(8,128)(2,1)S(1)}, bf16[256,768]{1,0:T(8,128)(2,1)S(1)}, u32[]{:S(2)}, u32[]{:S(2)}) collective-permute-start(bf16[256,768]{1,0:T(8,128)(2,1)S(1)} %get-tuple-element.20), channel_id=1, source_target_pairs={{1,0},{2,1},{3,2},{4,3},{5,4},{6,5},{7,6},{8,7},{9,8},{10,9},{11,1... | collective-permute-start | bytes 1179656 | tf_op jit(solution)/shard_map/ppermute | solution.py:351
  4.0 2.0 %copy-done = bf16[768,2304]{1,0:T(8,128)(2,1)S(1)} copy-done((bf16[768,2304]{1,0:T(8,128)(2,1)S(1)}, bf16[768,2304]{1,0:T(8,128)(2,1)}, u32[]{:S(2)}) %copy-start) | copy-done | bytes 3538968
  6.0 1.3 copy-done.7
  7.3 11.8 %middle.1 = (bf16[512,2304]{1,0:T(8,128)(2,1)S(1)}, bf16[256,768]{1,0:T(8,128)(2,1)S(1)}, bf16[256,2304]{1,0:T(8,128)(2,1)S(1)}) custom-call(s32[16]{0:T(128)S(1)} %copy-done.21, s32[16]{0:T(128)S(1)} %copy-done.22, s32[1]{0:T(128)} %bitcast.index_ref, bf16[512,768]{1,0:T(8,128)(2,1)S(1)} %copy-done.4, f32[1,768]{1,0:T(1,128)S(1)} %reshape.22.gain_ref, ...), custom_call_target="tpu_custom_call" | custom-call | flops 2717908992 | bytes 4718592 | tf_op jit(solution)/shard_map/middle/pallas_call | solution.py:354
  19.1 0.8 copy-done.13
  19.9 1.3 copy-done.14
  21.2 15.0 %after.1 = (bf16[256,768]{1,0:T(8,128)(2,1)S(1)}, bf16[256,768]{1,0:T(8,128)(2,1)S(1)}) custom-call(s32[16]{0:T(128)S(1)} %copy-done.21, s32[16]{0:T(128)S(1)} %copy-done.22, s32[1]{0:T(128)} %bitcast.index_ref, bf16[256,768]{1,0:T(8,128)(2,1)S(1)} %copy-done.14, bf16[512,768]{1,0:T(8,128)(2,1)S(1)} %copy-done.5, ...), custom_call_target="tpu_custom_call" | custom-call | flops 2415919104 | bytes 4718592 | tf_op jit(solution)/shard_map/after/pallas_call | solution.py:378
  36.2 0.7 copy-done.15
  37.7 7.5 %all-to-all-start.2 = ((bf16[16,16,768]{2,1,0:T(8,128)(2,1)}), bf16[16,16,768]{2,1,0:T(8,128)(2,1)}, u32[]{:S(2)}, u32[]{:S(2)}) async-start(bf16[16,16,768]{2,1,0:T(8,128)(2,1)} %bitcast.13), calls=%async_computation.2 | async-start | bytes 786432 | tf_op jit(solution)/shard_map/all_to_all | solution.py:424
  45.2 3.7 %collective-permute-start = (bf16[256,768]{1,0:T(8,128)(2,1)}, bf16[256,768]{1,0:T(8,128)(2,1)S(1)}, u32[]{:S(2)}, u32[]{:S(2)}) collective-permute-start(bf16[256,768]{1,0:T(8,128)(2,1)} %get-tuple-element.19), channel_id=1, source_target_pairs={{0,1},{1,2},{2,3},{3,4},{4,5},{5,6},{6,7},{7,8},{8,9},{9,10},{10,1... | collective-permute-start | bytes 1179656 | tf_op jit(solution)/shard_map/ppermute | solution.py:350
  48.9 7.0 %collective-permute-done.halo_ref = bf16[256,768]{1,0:T(8,128)(2,1)S(1)} collective-permute-done((bf16[256,768]{1,0:T(8,128)(2,1)}, bf16[256,768]{1,0:T(8,128)(2,1)S(1)}, u32[]{:S(2)}, u32[]{:S(2)}) %collective-permute-start) | collective-permute-done | bytes 393248 | tf_op jit(solution)/shard_map/ppermute | solution.py:350
  55.9 1.7 %copy-done.3 = bf16[512,2304]{1,0:T(8,128)(2,1)S(1)} copy-done((bf16[512,2304]{1,0:T(8,128)(2,1)S(1)}, bf16[512,2304]{1,0:T(8,128)(2,1)}, u32[]{:S(2)}) %copy-start.3) | copy-done | bytes 2359320
  57.5 1.1 copy-done.6
  58.7 1.3 copy-done.8
  59.9 1.3 copy-done.10
  61.2 1.0 copy-done.12
  62.2 15.0 %before.1 = (bf16[256,768]{1,0:T(8,128)(2,1)S(1)}, bf16[256,768]{1,0:T(8,128)(2,1)S(1)}) custom-call(s32[16]{0:T(128)S(1)} %copy-done.21, s32[16]{0:T(128)S(1)} %copy-done.22, s32[1]{0:T(128)} %bitcast.index_ref, bf16[256,768]{1,0:T(8,128)(2,1)S(1)} %collective-permute-done.halo_ref, bf16[512,768]{1,0:T(8,128)(2,1)S(1)} %copy-done.6, ...), custom_call_target="tpu_custom_call" | custom-call | flops 2415919104 | bytes 4718592 | tf_op jit(solution)/shard_map/before/pallas_call | solution.py:378
  77.3 0.7 copy-done.16
  78.0 0.7 copy-done.19
  78.8 8.8 %all-to-all-start = ((bf16[16,16,768]{2,1,0:T(8,128)(2,1)}), bf16[16,16,768]{2,1,0:T(8,128)(2,1)S(1)}, u32[]{:S(2)}, u32[]{:S(2)}) async-start(bf16[16,16,768]{2,1,0:T(8,128)(2,1)} %bitcast.14), calls=%async_computation | async-start | bytes 786432 | tf_op jit(solution)/shard_map/all_to_all | solution.py:424
  87.6 2.0 %copy-done.23 = bf16[768,2304]{1,0:T(8,128)(2,1)S(1)} copy-done((bf16[768,2304]{1,0:T(8,128)(2,1)S(1)}, bf16[768,2304]{1,0:T(8,128)(2,1)}, u32[]{:S(2)}) %copy-start.23) | copy-done | bytes 3538968
  89.5 1.3 copy-done.25
  90.8 6.5 %time1.1 = bf16[256,768]{1,0:T(8,128)(2,1)} custom-call(s32[16]{0:T(128)S(1)} %copy-done.22, s32[1]{0:T(128)} %bitcast.index_ref, bf16[256,768]{1,0:T(8,128)(2,1)} %bitcast.6.x_ref, bf16[768,2304]{1,0:T(8,128)(2,1)S(1)} %copy-done.23, bf16[768,768]{1,0:T(8,128)(2,1)S(1)} %copy-done.25), custom_call_target="tpu_custom_call" | custom-call | flops 1509949440 | bytes 4718592 | tf_op jit(solution)/shard_map/time1/pallas_call | solution.py:427
  97.3 2.1 %all-to-all-done = bf16[16,16,768]{2,1,0:T(8,128)(2,1)S(1)} async-done(((bf16[16,16,768]{2,1,0:T(8,128)(2,1)}), bf16[16,16,768]{2,1,0:T(8,128)(2,1)S(1)}, u32[]{:S(2)}, u32[]{:S(2)}) %all-to-all-start) | async-done | bytes 393248 | tf_op jit(solution)/shard_map/all_to_all | solution.py:424
  99.4 3.9 %all-to-all-start.3 = ((bf16[16,16,768]{2,1,0:T(8,128)(2,1)}), bf16[16,16,768]{2,1,0:T(8,128)(2,1)S(1)}, u32[]{:S(2)}, u32[]{:S(2)}) async-start(bf16[16,16,768]{2,1,0:T(8,128)(2,1)} %bitcast.7), calls=%async_computation.3 | async-start | bytes 786432 | tf_op jit(solution)/shard_map/all_to_all | solution.py:424
  103.4 2.0 %copy-done.24 = bf16[768,2304]{1,0:T(8,128)(2,1)S(1)} copy-done((bf16[768,2304]{1,0:T(8,128)(2,1)S(1)}, bf16[768,2304]{1,0:T(8,128)(2,1)}, u32[]{:S(2)}) %copy-start.24) | copy-done | bytes 3538968
  105.4 6.0 %time0.1 = bf16[256,768]{1,0:T(8,128)(2,1)} custom-call(s32[16]{0:T(128)S(1)} %copy-done.22, s32[1]{0:T(128)} %bitcast.index_ref, bf16[256,768]{1,0:T(8,128)(2,1)S(1)} %bitcast.15, bf16[768,2304]{1,0:T(8,128)(2,1)S(1)} %copy-done.24, bf16[768,768]{1,0:T(8,128)(2,1)S(1)} %copy-done.26), custom_call_target="tpu_custom_call" | custom-call | flops 1509949440 | bytes 4718592 | tf_op jit(solution)/shard_map/time0/pallas_call | solution.py:427
  111.3 3.9 %all-to-all-done.3 = bf16[16,16,768]{2,1,0:T(8,128)(2,1)S(1)} async-done(((bf16[16,16,768]{2,1,0:T(8,128)(2,1)}), bf16[16,16,768]{2,1,0:T(8,128)(2,1)S(1)}, u32[]{:S(2)}, u32[]{:S(2)}) %all-to-all-start.3) | async-done | bytes 393248 | tf_op jit(solution)/shard_map/all_to_all | solution.py:424
  115.2 3.7 %all-to-all-start.1 = ((bf16[16,16,768]{2,1,0:T(8,128)(2,1)}), bf16[16,16,768]{2,1,0:T(8,128)(2,1)S(1)}, u32[]{:S(2)}, u32[]{:S(2)}) async-start(bf16[16,16,768]{2,1,0:T(8,128)(2,1)} %bitcast.3), calls=%async_computation.1 | async-start | bytes 786432 | tf_op jit(solution)/shard_map/all_to_all | solution.py:424
  119.1 11.8 %all-to-all-done.1 = bf16[16,16,768]{2,1,0:T(8,128)(2,1)S(1)} async-done(((bf16[16,16,768]{2,1,0:T(8,128)(2,1)}), bf16[16,16,768]{2,1,0:T(8,128)(2,1)S(1)}, u32[]{:S(2)}, u32[]{:S(2)}) %all-to-all-start.1) | async-done | bytes 393248 | tf_op jit(solution)/shard_map/all_to_all | solution.py:424
  131.0 0.9 pad_maximum_fusion
  (49 shorter events, 1.1 us)
Async XLA Ops:
  0.0 4.0 %copy-start.4 = (bf16[512,768]{1,0:T(8,128)(2,1)S(1)}, bf16[512,768]{1,0:T(8,128)(2,1)}, u32[]{:S(2)}) copy-start(bf16[512,768]{1,0:T(8,128)(2,1)} %x_ref.5) | copy-start | bytes 2359300
  0.0 3.9 %copy-start.27 = (f32[768]{0:T(1024)S(1)}, f32[768]{0:T(1024)}, u32[]{:S(2)}) copy-start(f32[768]{0:T(1024)} %param.12) | copy-start | bytes 9220
  0.0 4.0 %copy-start.28 = (f32[768]{0:T(1024)S(1)}, f32[768]{0:T(1024)}, u32[]{:S(2)}) copy-start(f32[768]{0:T(1024)} %param.15) | copy-start | bytes 9220
  0.0 4.0 %copy-start.21 = (s32[16]{0:T(128)S(1)}, s32[16]{0:T(128)}, u32[]{:S(2)}) copy-start(s32[16]{0:T(128)} %reach_ref.5) | copy-start | bytes 196
  0.0 4.0 %copy-start.22 = (s32[16]{0:T(128)S(1)}, s32[16]{0:T(128)}, u32[]{:S(2)}) copy-start(s32[16]{0:T(128)} %count_ref.9) | copy-start | bytes 196
  2.0 17.1 %collective-permute-start.1 = (bf16[256,768]{1,0:T(8,128)(2,1)S(1)}, bf16[256,768]{1,0:T(8,128)(2,1)S(1)}, u32[]{:S(2)}, u32[]{:S(2)}) collective-permute-start(bf16[256,768]{1,0:T(8,128)(2,1)S(1)} %get-tuple-element.20), channel_id=1, source_target_pairs={{1,0},{2,1},{3,2},{4,3},{5,4},{6,5},{7,6},{8,7},{9,8},{10,9},{11,1... | collective-permute-start | bytes 1179656 | tf_op jit(solution)/shard_map/ppermute | solution.py:351
  4.0 2.0 %copy-start = (bf16[768,2304]{1,0:T(8,128)(2,1)S(1)}, bf16[768,2304]{1,0:T(8,128)(2,1)}, u32[]{:S(2)}) copy-start(bf16[768,2304]{1,0:T(8,128)(2,1)} %project_ref.8) | copy-start | bytes 10616836
  6.0 1.3 copy-start.7
  7.3 12.6 %copy-start.5 = (bf16[512,768]{1,0:T(8,128)(2,1)S(1)}, bf16[512,768]{1,0:T(8,128)(2,1)}, u32[]{:S(2)}) copy-start(bf16[512,768]{1,0:T(8,128)(2,1)} %x_ref.5) | copy-start | bytes 2359300
  19.0 17.1 %copy-start.2 = (bf16[512,2304]{1,0:T(8,128)(2,1)}, bf16[512,2304]{1,0:T(8,128)(2,1)S(1)}, u32[]{:S(2)}) copy-start(bf16[512,2304]{1,0:T(8,128)(2,1)S(1)} %get-tuple-element.12.first_ref) | copy-start | bytes 7077892
  19.1 17.1 %copy-start.9 = (bf16[256,2304]{1,0:T(8,128)(2,1)}, bf16[256,2304]{1,0:T(8,128)(2,1)S(1)}, u32[]{:S(2)}) copy-start(bf16[256,2304]{1,0:T(8,128)(2,1)S(1)} %get-tuple-element.14.second_ref) | copy-start | bytes 3538948
  19.1 17.1 %copy-start.11 = (bf16[256,768]{1,0:T(8,128)(2,1)}, bf16[256,768]{1,0:T(8,128)(2,1)S(1)}, u32[]{:S(2)}) copy-start(bf16[256,768]{1,0:T(8,128)(2,1)S(1)} %get-tuple-element.13.middle_ref) | copy-start | bytes 1179652
  19.1 0.8 copy-start.13
  19.9 1.3 copy-start.14
  21.2 34.7 %copy-start.1 = (bf16[768,2304]{1,0:T(8,128)(2,1)S(1)}, bf16[768,2304]{1,0:T(8,128)(2,1)}, u32[]{:S(2)}) copy-start(bf16[768,2304]{1,0:T(8,128)(2,1)} %project_ref.8) | copy-start | bytes 10616836
  36.2 0.8 copy-start.15
  37.7 41.1 %all-to-all-start.2 = ((bf16[16,16,768]{2,1,0:T(8,128)(2,1)}), bf16[16,16,768]{2,1,0:T(8,128)(2,1)}, u32[]{:S(2)}, u32[]{:S(2)}) async-start(bf16[16,16,768]{2,1,0:T(8,128)(2,1)} %bitcast.13), calls=%async_computation.2 | async-start | bytes 786432 | tf_op jit(solution)/shard_map/all_to_all | solution.py:424
  45.2 10.7 %collective-permute-start = (bf16[256,768]{1,0:T(8,128)(2,1)}, bf16[256,768]{1,0:T(8,128)(2,1)S(1)}, u32[]{:S(2)}, u32[]{:S(2)}) collective-permute-start(bf16[256,768]{1,0:T(8,128)(2,1)} %get-tuple-element.19), channel_id=1, source_target_pairs={{0,1},{1,2},{2,3},{3,4},{4,5},{5,6},{6,7},{7,8},{8,9},{9,10},{10,1... | collective-permute-start | bytes 1179656 | tf_op jit(solution)/shard_map/ppermute | solution.py:350
  55.9 1.7 %copy-start.3 = (bf16[512,2304]{1,0:T(8,128)(2,1)S(1)}, bf16[512,2304]{1,0:T(8,128)(2,1)}, u32[]{:S(2)}) copy-start(bf16[512,2304]{1,0:T(8,128)(2,1)} %copy-done.2) | copy-start | bytes 7077892
  57.5 1.1 copy-start.6
  58.7 1.3 copy-start.8
  59.9 1.3 copy-start.10
  61.2 1.0 copy-start.12
  78.8 20.7 %all-to-all-start = ((bf16[16,16,768]{2,1,0:T(8,128)(2,1)}), bf16[16,16,768]{2,1,0:T(8,128)(2,1)S(1)}, u32[]{:S(2)}, u32[]{:S(2)}) async-start(bf16[16,16,768]{2,1,0:T(8,128)(2,1)} %bitcast.14), calls=%async_computation | async-start | bytes 786432 | tf_op jit(solution)/shard_map/all_to_all | solution.py:424
  87.5 2.0 %copy-start.23 = (bf16[768,2304]{1,0:T(8,128)(2,1)S(1)}, bf16[768,2304]{1,0:T(8,128)(2,1)}, u32[]{:S(2)}) copy-start(bf16[768,2304]{1,0:T(8,128)(2,1)} %project_ref.9) | copy-start | bytes 10616836
  89.5 1.3 copy-start.25
  90.8 12.5 %copy-start.26 = (bf16[768,768]{1,0:T(8,128)(2,1)S(1)}, bf16[768,768]{1,0:T(8,128)(2,1)}, u32[]{:S(2)}) copy-start(bf16[768,768]{1,0:T(8,128)(2,1)} %output_ref.9) | copy-start | bytes 3538948
  99.4 15.8 %all-to-all-start.3 = ((bf16[16,16,768]{2,1,0:T(8,128)(2,1)}), bf16[16,16,768]{2,1,0:T(8,128)(2,1)S(1)}, u32[]{:S(2)}, u32[]{:S(2)}) async-start(bf16[16,16,768]{2,1,0:T(8,128)(2,1)} %bitcast.7), calls=%async_computation.3 | async-start | bytes 786432 | tf_op jit(solution)/shard_map/all_to_all | solution.py:424
  103.4 2.0 %copy-start.24 = (bf16[768,2304]{1,0:T(8,128)(2,1)S(1)}, bf16[768,2304]{1,0:T(8,128)(2,1)}, u32[]{:S(2)}) copy-start(bf16[768,2304]{1,0:T(8,128)(2,1)} %project_ref.9) | copy-start | bytes 10616836
  105.4 13.6 %copy-start.18 = (bf16[256,768]{1,0:T(8,128)(2,1)S(1)}, bf16[256,768]{1,0:T(8,128)(2,1)}, u32[]{:S(2)}) copy-start(bf16[256,768]{1,0:T(8,128)(2,1)} %copy-done.17) | copy-start | bytes 1179652
  111.3 19.6 %copy-start.20 = (bf16[256,768]{1,0:T(8,128)(2,1)S(1)}, bf16[256,768]{1,0:T(8,128)(2,1)}, u32[]{:S(2)}) copy-start(bf16[256,768]{1,0:T(8,128)(2,1)} %copy-done.19) | copy-start | bytes 1179652
  115.2 15.7 %all-to-all-start.1 = ((bf16[16,16,768]{2,1,0:T(8,128)(2,1)}), bf16[16,16,768]{2,1,0:T(8,128)(2,1)S(1)}, u32[]{:S(2)}, u32[]{:S(2)}) async-start(bf16[16,16,768]{2,1,0:T(8,128)(2,1)} %bitcast.3), calls=%async_computation.1 | async-start | bytes 786432 | tf_op jit(solution)/shard_map/all_to_all | solution.py:424
  (3 other events, 2.2 us)

commit v2 on v1

v2 whole, which is shorter than its diff:
```python
import functools

import jax
import jax.numpy as jnp
from jax import lax
from jax.experimental import pallas as pl
from jax.experimental.pallas import tpu as pltpu
from jax.sharding import PartitionSpec as P


F = 16
HALO = 128
H = 12
HD = 64
D = 768
BLK = HALO
WIN = 3 * BLK
PAIR = 2 * HD
CHUNK = 2 * BLK
VMEM_LIMIT = 60 * 1024 * 1024
EPS = 1e-06
MASKED = -1e30

BF16 = jnp.bfloat16
F32 = jnp.float32


def norm_rows(values, gain):
    wide = values.astype(F32)
    meansq = jnp.mean(wide * wide, axis=-1, keepdims=True)
    return (wide * lax.rsqrt(meansq + EPS) * gain).astype(BF16)


def pair_scores(q, k):
    lane = lax.broadcasted_iota(jnp.int32, (1, PAIR), 1)
    scale = HD ** (-0.5)
    left = jnp.where(lane < HD, scale, 0.0).astype(BF16)
    right = jnp.where(lane < HD, 0.0, scale).astype(BF16)
    both = jnp.concatenate([q * left, q * right], axis=0)
    return lax.dot_general(both, k, (((1,), (1,)), ((), ())), preferred_element_type=F32)


def pair_expon(scores, bias):
    rows, keys = bias.shape
    scores = scores.reshape(2, rows, keys) + bias[None]
    highest = jnp.max(scores, axis=-1, keepdims=True)
    return jnp.exp(scores - highest).reshape(2 * rows, keys).astype(BF16)


def pair_mixed(expon, v):
    rows = expon.shape[0] // 2
    lane = lax.broadcasted_iota(jnp.int32, (1, PAIR), 1)
    mixed = jnp.dot(
        expon, jnp.concatenate([v, jnp.ones_like(v)], axis=1), preferred_element_type=F32
    )
    mixed = (mixed[:, :PAIR] * (1.0 / mixed[:, PAIR:])).reshape(2, rows, PAIR)
    return jnp.where(lane < HD, mixed[0], mixed[1]).astype(BF16)


def lanes_of(pair):
    return slice(pair * PAIR, (pair + 1) * PAIR)


def attention(query, key, value, store, bias_ref, scores_s, expon_s):
    for pair in range(H // 2):
        scores_s[pair] = pair_scores(query(lanes_of(pair)), key(lanes_of(pair)))
    for pair in range(H // 2):
        expon_s[pair] = pair_expon(scores_s[pair], bias_ref[...])
    for pair in range(H // 2):
        store(lanes_of(pair), pair_mixed(expon_s[pair], value(lanes_of(pair))))


def window_bias(start, reach_ref, count_ref, frame_len, total):
    row = lax.broadcasted_iota(jnp.int32, (BLK, WIN), 0)
    col = lax.broadcasted_iota(jnp.int32, (BLK, WIN), 1)
    distance = col - BLK - row
    reach = reach_ref[lax.div(jnp.clip(start, 0, total - 1), frame_len)]
    least = jnp.zeros((1, WIN), jnp.int32)
    place = lax.broadcasted_iota(jnp.int32, (1, WIN), 1)
    for j in range(3):
        at = start + (j - 1) * BLK
        inside = (at >= 0) & (at < total)
        frame = lax.div(jnp.clip(at, 0, total - 1), frame_len)
        first = (frame + 1) * frame_len - count_ref[frame] - at
        first = jnp.where(inside, first, WIN) + j * BLK
        least = jnp.where(place >= j * BLK, first, least)
    living = (col >= least) | (distance == 0)
    return jnp.where((jnp.abs(distance) <= reach) & living, 0.0, MASKED).astype(F32)


def space_attention(start, tables, q, k, v, mixed_s, bias_s, scores_s, expon_s):
    def load(what, length, i):
        ref, row, column = what
        rows = pl.ds(pl.multiple_of(row + i * BLK, BLK), length)
        return lambda lanes: ref[rows, column + lanes.start : column + lanes.stop]

    def one_block(i, carry):
        bias_s[...] = window_bias(start + i * BLK, *tables)
        rows = pl.ds(pl.multiple_of(i * BLK, BLK), BLK)

        def store(lanes, mixed):
            mixed_s[rows, lanes] = mixed

        attention(load(q, BLK, i), load(k, WIN, i), load(v, WIN, i), store, bias_s, scores_s, expon_s)
        return carry

    lax.fori_loop(0, 2, one_block, 0)


def times(x, weight):
    return jnp.dot(x, weight, preferred_element_type=F32)


def copies(sems, *pairs):
    made = [pltpu.make_async_copy(a, b, sems.at[i]) for i, (a, b) in enumerate(pairs)]
    for copy in made:
        copy.start()
    return made


QUERY, KEY, VALUE = slice(0, D), slice(D, 2 * D), slice(2 * D, 3 * D)


def middle_kernel(
    frame_len,
    total,
    reach_ref,
    count_ref,
    index_ref,
    gain_ref,
    x_hbm,
    project_hbm,
    output_hbm,
    first_hbm,
    state_hbm,
    second_hbm,
    x_s,
    project_s,
    output_s,
    first_s,
    state_s,
    second_s,
    mixed_s,
    bias_s,
    scores_s,
    expon_s,
    in_sems,
    out_sems,
):
    rows = x_s.shape[0]
    offset = index_ref[0] * rows
    gain = gain_ref[...]
    inner = slice(BLK, rows - BLK)
    x_in, query_in, key_in, value_in, output_in = copies(
        in_sems,
        (x_hbm, x_s),
        (project_hbm.at[:, QUERY], project_s.at[:, QUERY]),
        (project_hbm.at[:, KEY], project_s.at[:, KEY]),
        (project_hbm.at[:, VALUE], project_s.at[:, VALUE]),
        (output_hbm, output_s),
    )
    x_in.wait()
    hidden = norm_rows(x_s[...], gain)
    for copy, cols in ((query_in, QUERY), (key_in, KEY), (value_in, VALUE)):
        copy.wait()
        first_s[:, cols] = times(hidden, project_s[:, cols]).astype(BF16)
    first_out = pltpu.make_async_copy(first_s, first_hbm, out_sems.at[0])
    first_out.start()
    tables = (reach_ref, count_ref, frame_len, total)
    space_attention(
        offset + BLK,
        tables,
        (first_s, BLK, 0),
        (first_s, 0, D),
        (first_s, 0, 2 * D),
        mixed_s,
        bias_s,
        scores_s,
        expon_s,
    )
    output_in.wait()
    state_s[...] = (x_s[inner].astype(F32) + times(mixed_s[...], output_s[...])).astype(BF16)
    state_out = pltpu.make_async_copy(state_s, state_hbm, out_sems.at[1])
    state_out.start()
    hidden = norm_rows(state_s[...], gain)
    for cols in (QUERY, KEY, VALUE):
        second_s[:, cols] = times(hidden, project_s[:, cols]).astype(BF16)
    second_out = pltpu.make_async_copy(second_s, second_hbm, out_sems.at[2])
    second_out.start()
    first_out.wait()
    state_out.wait()
    second_out.wait()


def side_kernel(
    frame_len,
    total,
    after,
    reach_ref,
    count_ref,
    index_ref,
    gain_ref,
    time_gain_ref,
    halo_hbm,
    x_hbm,
    first_hbm,
    middle_hbm,
    second_hbm,
    project_hbm,
    output_hbm,
    state_ref,
    hidden_ref,
    halo_s,
    x_s,
    middle_s,
    project_s,
    output_s,
    q_s,
    k_s,
    v_s,
    q2_s,
    k2_s,
    v2_s,
    edge_s,
    mixed_s,
    bias_s,
    scores_s,
    expon_s,
    in_sems,
):
    local_rows = x_hbm.shape[0]
    offset = index_ref[0] * local_rows
    gain = gain_ref[...]
    half = 2 * BLK
    low, high = slice(0, BLK), slice(BLK, half)
    front, back = slice(0, half), slice(half, 2 * half)
    if after:
        begin = local_rows - half
        own_part, far_part = front, back
        mid_part, edge_part = front, back
        far_edge = low
        own_at, far_at = low, high
        mid_own, mid_at, edge_at = high, low, high
        start1, start2 = begin + BLK, begin
        own_rows = pl.ds(begin, half)
        edge_rows = pl.ds(local_rows - BLK, BLK)
    else:
        own_part, far_part = back, front
        mid_part, edge_part = back, front
        far_edge = high
        own_at, far_at = high, low
        mid_own, mid_at, edge_at = low, high, low
        start1, start2 = -BLK, 0
        own_rows = pl.ds(0, half)
        edge_rows = pl.ds(0, BLK)
    halo_in, key_in, value_in, query_in, k_in, v_in, q_in, output_in, x_in, k2_in, v2_in, q2_in, middle_in = copies(
        in_sems,
        (halo_hbm, halo_s),
        (project_hbm.at[:, KEY], project_s.at[:, KEY]),
        (project_hbm.at[:, VALUE], project_s.at[:, VALUE]),
        (project_hbm.at[:, QUERY], project_s.at[:, QUERY]),
        (first_hbm.at[own_rows, KEY], k_s.at[own_part]),
        (first_hbm.at[own_rows, VALUE], v_s.at[own_part]),
        (first_hbm.at[edge_rows, QUERY], q_s.at[own_at]),
        (output_hbm, output_s),
        (x_hbm.at[edge_rows], x_s),
        (second_hbm.at[:, KEY], k2_s.at[mid_part]),
        (second_hbm.at[:, VALUE], v2_s.at[mid_part]),
        (second_hbm.at[mid_own, QUERY], q2_s.at[mid_at]),
        (middle_hbm.at[mid_own], middle_s),
    )
    tables = (reach_ref, count_ref, frame_len, total)
    halo_in.wait()
    hidden = norm_rows(halo_s[...], gain)
    key_in.wait()
    k_s[far_part] = times(hidden, project_s[:, KEY]).astype(BF16)
    value_in.wait()
    v_s[far_part] = times(hidden, project_s[:, VALUE]).astype(BF16)
    query_in.wait()
    q_s[far_at] = times(hidden[far_edge], project_s[:, QUERY]).astype(BF16)
    k_in.wait()
    v_in.wait()
    q_in.wait()
    work = (mixed_s, bias_s, scores_s, expon_s)
    space_attention(offset + start1, tables, (q_s, 0, 0), (k_s, 0, 0), (v_s, 0, 0), *work)
    output_in.wait()
    x_in.wait()
    update = times(mixed_s[...], output_s[...])
    edge_s[own_at] = (x_s[...].astype(F32) + update[own_at]).astype(BF16)
    edge_s[far_at] = (halo_s[far_edge].astype(F32) + update[far_at]).astype(BF16)

    hidden = norm_rows(edge_s[...], gain)
    k2_s[edge_part] = times(hidden, project_s[:, KEY]).astype(BF16)
    v2_s[edge_part] = times(hidden, project_s[:, VALUE]).astype(BF16)
    q2_s[edge_at] = times(hidden[own_at], project_s[:, QUERY]).astype(BF16)
    k2_in.wait()
    v2_in.wait()
    q2_in.wait()
    space_attention(offset + start2, tables, (q2_s, 0, 0), (k2_s, 0, 0), (v2_s, 0, 0), *work)
    middle_in.wait()
    update = times(mixed_s[...], output_s[...])
    state_ref[edge_at] = (edge_s[own_at].astype(F32) + update[edge_at]).astype(BF16)
    state_ref[mid_at] = (middle_s[...].astype(F32) + update[mid_at]).astype(BF16)
    hidden_ref[...] = norm_rows(state_ref[...], time_gain_ref[...])


def time_kernel(
    frame_len,
    local_rows,
    devices,
    chunk,
    count_ref,
    index_ref,
    x_hbm,
    project_hbm,
    output_hbm,
    update_ref,
    x_s,
    project_s,
    output_s,
    qkv_s,
    mixed_s,
    bias_s,
    scores_s,
    expon_s,
    in_sems,
):
    rows = x_s.shape[0]
    slots = rows // F
    piece = rows // devices
    x_in, query_in, key_in, value_in, output_in = copies(
        in_sems,
        (x_hbm, x_s),
        (project_hbm.at[:, QUERY], project_s.at[:, QUERY]),
        (project_hbm.at[:, KEY], project_s.at[:, KEY]),
        (project_hbm.at[:, VALUE], project_s.at[:, VALUE]),
        (output_hbm, output_s),
    )
    row = lax.broadcasted_iota(jnp.int32, (rows, rows), 0)
    col = lax.broadcasted_iota(jnp.int32, (rows, rows), 1)
    key = lax.broadcasted_iota(jnp.int32, (1, rows), 1)
    key_frame = lax.div(key, slots)
    key_slot = lax.rem(key, slots)
    place = lax.div(key_slot, piece) * local_rows + lax.rem(key_slot, piece)
    place = place + chunk * rows + index_ref[0] * piece
    least = jnp.zeros((1, rows), jnp.int32)
    for g in range(F):
        least = jnp.where(key_frame == g, frame_len - count_ref[g], least)
    living = jnp.where(place >= least, 1, 0)
    same = lax.rem(row, slots) == lax.rem(col, slots)
    bias_s[...] = jnp.where(same & ((living == 1) | (row == col)), 0.0, MASKED).astype(F32)

    x_in.wait()
    for copy, cols in ((query_in, QUERY), (key_in, KEY), (value_in, VALUE)):
        copy.wait()
        qkv_s[:, cols] = times(x_s[...], project_s[:, cols]).astype(BF16)

    def columns(first):
        return lambda lanes: qkv_s[:, first + lanes.start : first + lanes.stop]

    def store(lanes, mixed):
        mixed_s[:, lanes] = mixed

    attention(columns(0), columns(D), columns(2 * D), store, bias_s, scores_s, expon_s)
    output_in.wait()
    update_ref[...] = times(mixed_s[...], output_s[...]).astype(BF16)


def smem():
    return pl.BlockSpec(memory_space=pltpu.SMEM)


def vmem():
    return pl.BlockSpec(memory_space=pltpu.VMEM)


def hbm():
    return pl.BlockSpec(memory_space=pl.ANY)


def rows16(rows, cols):
    return jax.ShapeDtypeStruct((rows, cols), BF16)


def scratch(rows, cols):
    return pltpu.VMEM((rows, cols), BF16)


def work(rows, keys):
    return [
        scratch(CHUNK, D),
        pltpu.VMEM((rows, keys), F32),
        pltpu.VMEM((H // 2, 2 * rows, keys), F32),
        pltpu.VMEM((H // 2, 2 * rows, keys), BF16),
    ]


def sems(count):
    return pltpu.SemaphoreType.DMA((count,))


def call(kernel, flops, exps, **rest):
    return pl.pallas_call(
        kernel,
        compiler_params=pltpu.CompilerParams(vmem_limit_bytes=VMEM_LIMIT),
        cost_estimate=pl.CostEstimate(
            flops=flops, bytes_accessed=16 * D * D, transcendentals=exps
        ),
        **rest,
    )


def on_device(
    frame_tokens,
    window_reach,
    valid_count,
    space_gain,
    space_project,
    space_output,
    time_gain,
    time_project,
    time_output,
):
    devices = lax.axis_size("strip")
    local_rows = frame_tokens.shape[0]
    total = local_rows * devices
    frame_len = total // F
    if local_rows != 2 * CHUNK or frame_len % local_rows or CHUNK % devices:
        raise ValueError("unsupported sizes")
    index = lax.axis_index("strip").reshape(1)
    gain = space_gain.reshape(1, D)
    gain_t = time_gain.reshape(1, D)

    up = [(i, i + 1) for i in range(devices - 1)]
    down = [(i + 1, i) for i in range(devices - 1)]
    before = lax.ppermute(frame_tokens[local_rows - CHUNK :], "strip", up)
    after = lax.ppermute(frame_tokens[:CHUNK], "strip", down)

    first, middle, second = call(
        functools.partial(middle_kernel, frame_len, total),
        2 * D * D * 10 * CHUNK,
        H * CHUNK * WIN,
        out_shape=(rows16(local_rows, 3 * D), rows16(CHUNK, D), rows16(CHUNK, 3 * D)),
        in_specs=[smem()] * 3 + [vmem()] + [hbm()] * 3,
        out_specs=(hbm(),) * 3,
        scratch_shapes=[
            scratch(local_rows, D),
            scratch(D, 3 * D),
            scratch(D, D),
            scratch(local_rows, 3 * D),
            scratch(CHUNK, D),
            scratch(CHUNK, 3 * D),
            *work(BLK, WIN),
            sems(5),
            sems(3),
        ],
    )(window_reach, valid_count, index, gain, frame_tokens, space_project, space_output)

    def side(halo, is_after):
        return call(
            functools.partial(side_kernel, frame_len, total, is_after),
            2 * D * D * 10 * CHUNK,
            2 * H * CHUNK * WIN,
            out_shape=(rows16(CHUNK, D),) * 2,
            in_specs=[smem()] * 3 + [vmem()] * 2 + [hbm()] * 7,
            out_specs=(vmem(),) * 2,
            scratch_shapes=[
                scratch(CHUNK, D),
                scratch(BLK, D),
                scratch(BLK, D),
                scratch(D, 3 * D),
                scratch(D, D),
                scratch(CHUNK, D),
                scratch(2 * CHUNK, D),
                scratch(2 * CHUNK, D),
                scratch(CHUNK, D),
                scratch(2 * CHUNK, D),
                scratch(2 * CHUNK, D),
                scratch(CHUNK, D),
                *work(BLK, WIN),
                sems(13),
            ],
        )(
            window_reach,
            valid_count,
            index,
            gain,
            gain_t,
            halo,
            frame_tokens,
            first,
            middle,
            second,
            space_project,
            space_output,
        )

    def exchange(x):
        return lax.all_to_all(x, "strip", split_axis=0, concat_axis=0, tiled=True)

    def temporal(x, chunk):
        return call(
            functools.partial(time_kernel, frame_len, local_rows, devices, chunk),
            2 * D * D * 5 * CHUNK,
            H * CHUNK * CHUNK,
            out_shape=rows16(CHUNK, D),
            in_specs=[smem()] * 2 + [hbm()] * 3,
            out_specs=vmem(),
            scratch_shapes=[
                scratch(CHUNK, D),
                scratch(D, 3 * D),
                scratch(D, D),
                scratch(CHUNK, 3 * D),
                *work(CHUNK, CHUNK),
                sems(5),
            ],
        )(valid_count, index, x, time_project, time_output)

    state0, hidden0 = side(before, False)
    sent0 = exchange(hidden0)
    state1, hidden1 = side(after, True)
    sent1 = exchange(hidden1)
    back0 = exchange(temporal(sent0, 0))
    back1 = exchange(temporal(sent1, 1))
    wide = [
        (s.astype(F32) + b.astype(F32)).astype(BF16) for s, b in ((state0, back0), (state1, back1))
    ]
    return jnp.concatenate(wide, axis=0)


def solution(mesh):
    return jax.shard_map(
        on_device,
        mesh=mesh,
        in_specs=(
            P(("group", "strip"), None),
            P("group"),
            P("group"),
            P(),
            P(),
            P(),
            P(),
            P(),
            P(),
        ),
        out_specs=P(("group", "strip"), None),
        check_vma=False,
    )
```

time: 133 us -> 110 us (0.83)
  local copies, waits for them, and re-layouts: 21.9 us -> 3.89 us
  Pallas kernels: 54.3 us -> 44.1 us
  waiting for transfers between devices: 24.8 us -> 30.2 us
    unnamed x58 -> x16, local copies, waits for them, and re-layouts: 20 us -> 1.51 us
    pallas_call x5, Pallas kernels: 54.3 us -> 44.1 us  [the longest x2 21.8 us: side(): call(functools.partial(side_kernel, frame_len, total, is_after), 2 * D *...]
    all_to_all x4, waiting for transfers between devices: 17.8 us -> 23.3 us  [exchange(): return lax.all_to_all(x, 'strip', split_axis=0, concat_axis=0, tiled=True)]
  transfers between devices with their start and end apart: 6 -> 6, of which waited for: 4 -> 4; matrix products, arithmetic and copies ran while one was open for 0% -> 1% of each run, Pallas kernels for 30% -> 30%
where the time goes in v2:
time: 110 us; the launch traced here: 109 us
  Pallas kernels  44.1 us (40%)
  waiting for transfers between devices  30.2 us (27%)
  starting transfers between devices  29.5 us (27%)
  local copies, waits for them, and re-layouts  3.89 us (4%)
  other arithmetic  1.17 us (1%)
    all_to_all x4, starting transfers between devices, exchange(): return lax.all_to_all(x, 'strip', split_axis=0, concat_axis=0, tiled=True)  23.9 us
    all_to_all x4, waiting for transfers between devices, exchange(): return lax.all_to_all(x, 'strip', split_axis=0, concat_axis=0, tiled=True)  23.3 us
    pallas_call x2, Pallas kernels, side(): call(functools.partial(side_kernel, frame_len, total, is_after), 2 * D *...  21.8 us
    pallas_call x2, Pallas kernels, temporal(): call(functools.partial(time_kernel, frame_len, local_rows, devices, chunk...  12.3 us
    pallas_call x1, Pallas kernels, on_device(): call(functools.partial(middle_kernel, frame_len, total), 2 * D * D * 10 *...  9.98 us
    ppermute x1, waiting for transfers between devices, on_device(): before = lax.ppermute(frame_tokens[local_rows - CHUNK:], 'strip', up)  6.88 us
    ppermute x1, starting transfers between devices, on_device(): before = lax.ppermute(frame_tokens[local_rows - CHUNK:], 'strip', up)  3.71 us
  transfers between devices with their start and end apart: 6, of which 4 were waited for; matrix products, arithmetic and copies ran while one was open for 1% of the time, Pallas kernels for 30%

profile of v2, /device:TPU:1, one launch (start us, length us, event | category | flops | bytes accessed | tf_op | source)
XLA Modules:
  0.0 109.0 jit_solution(3010721914668020715)
XLA Ops:
  0.0 1.2 %fusion.2 = (bf16[256,768]{1,0:T(8,128)(2,1)S(1)}, bf16[256,768]{1,0:T(8,128)(2,1)S(1)}) fusion(bf16[512,768]{1,0:T(8,128)(2,1)} %x_hbm.5), kind=kLoop, calls=%fused_computation.5 | loop fusion | bytes 1572864 | tf_op jit(solution)/shard_map/slice | solution.py:436
  1.2 1.9 %collective-permute-start.1 = (bf16[256,768]{1,0:T(8,128)(2,1)S(1)}, bf16[256,768]{1,0:T(8,128)(2,1)S(1)}, u32[]{:S(2)}, u32[]{:S(2)}) collective-permute-start(bf16[256,768]{1,0:T(8,128)(2,1)S(1)} %get-tuple-element.20), channel_id=1, source_target_pairs={{1,0},{2,1},{3,2},{4,3},{5,4},{6,5},{7,6},{8,7},{9,8},{10,9},{11,1... | collective-permute-start | bytes 1179656 | tf_op jit(solution)/shard_map/ppermute | solution.py:437
  3.1 0.0 copy-done.4
  3.1 0.6 reshape.22.gain_ref
  3.7 0.0 copy-done.5
  3.7 0.6 reshape.23.time_gain_ref
  4.3 10.0 %shard_map.91 = (bf16[512,2304]{1,0:T(8,128)(2,1)}, bf16[256,768]{1,0:T(8,128)(2,1)}, bf16[256,2304]{1,0:T(8,128)(2,1)}) custom-call(s32[16]{0:T(128)} %reach_ref.5, s32[16]{0:T(128)} %count_ref.9, s32[1]{0:T(128)} %bitcast.index_ref, f32[1,768]{1,0:T(1,128)} %reshape.22.gain_ref, bf16[512,768]{1,0:T(8,128)(2,1)} %x_hbm.5, bf16[768,2304]{1,0:T(8,128)(2,1)} %project_hbm.8, ...), custom_call_target="tpu_custom_call" | custom-call | flops 3019898880 | bytes 9437184 | tf_op jit(solution)/shard_map/pallas_call | solution.py:439
  14.3 0.0 collective-permute-done.1.halo_hbm
  14.3 0.0 copy-start.6
  14.3 0.7 copy-done.6
  15.1 10.9 %shard_map.94 = (bf16[256,768]{1,0:T(8,128)(2,1)}, bf16[256,768]{1,0:T(8,128)(2,1)}) custom-call(s32[16]{0:T(128)} %reach_ref.5, s32[16]{0:T(128)} %count_ref.9, s32[1]{0:T(128)} %bitcast.index_ref, f32[1,768]{1,0:T(1,128)} %reshape.22.gain_ref, f32[1,768]{1,0:T(1,128)} %reshape.23.time_gain_ref, bf16[256,768]{1,0:T(8,128)(2,1)} %copy-done.6, ...), custom_call_target="tpu_custom_call" | custom-call | flops 3019898880 | bytes 9437184 | tf_op jit(solution)/shard_map/pallas_call | solution.py:460
  26.0 7.5 %all-to-all-start.2 = ((bf16[16,16,768]{2,1,0:T(8,128)(2,1)}), bf16[16,16,768]{2,1,0:T(8,128)(2,1)S(1)}, u32[]{:S(2)}, u32[]{:S(2)}) async-start(bf16[16,16,768]{2,1,0:T(8,128)(2,1)} %bitcast.14), calls=%async_computation.2 | async-start | bytes 786432 | tf_op jit(solution)/shard_map/all_to_all | solution.py:499
  33.5 3.7 %collective-permute-start = (bf16[256,768]{1,0:T(8,128)(2,1)S(1)}, bf16[256,768]{1,0:T(8,128)(2,1)S(1)}, u32[]{:S(2)}, u32[]{:S(2)}) collective-permute-start(bf16[256,768]{1,0:T(8,128)(2,1)S(1)} %get-tuple-element.19), channel_id=1, source_target_pairs={{0,1},{1,2},{2,3},{3,4},{4,5},{5,6},{6,7},{7,8},{8,9},{9,10},{10,1... | collective-permute-start | bytes 1179656 | tf_op jit(solution)/shard_map/ppermute | solution.py:436
  37.2 6.9 %collective-permute-done.halo_hbm = bf16[256,768]{1,0:T(8,128)(2,1)S(1)} collective-permute-done((bf16[256,768]{1,0:T(8,128)(2,1)S(1)}, bf16[256,768]{1,0:T(8,128)(2,1)S(1)}, u32[]{:S(2)}, u32[]{:S(2)}) %collective-permute-start) | collective-permute-done | bytes 393248 | tf_op jit(solution)/shard_map/ppermute | solution.py:436
  44.1 0.7 copy-done.7
  44.9 10.9 %shard_map.92 = (bf16[256,768]{1,0:T(8,128)(2,1)}, bf16[256,768]{1,0:T(8,128)(2,1)}) custom-call(s32[16]{0:T(128)} %reach_ref.5, s32[16]{0:T(128)} %count_ref.9, s32[1]{0:T(128)} %bitcast.index_ref, f32[1,768]{1,0:T(1,128)} %reshape.22.gain_ref, f32[1,768]{1,0:T(1,128)} %reshape.23.time_gain_ref, bf16[256,768]{1,0:T(8,128)(2,1)} %copy-done.7, ...), custom_call_target="tpu_custom_call" | custom-call | flops 3019898880 | bytes 9437184 | tf_op jit(solution)/shard_map/pallas_call | solution.py:460
  55.8 0.0 all-to-all-done.2
  55.8 0.0 copy-start
  55.8 8.9 %all-to-all-start = ((bf16[16,16,768]{2,1,0:T(8,128)(2,1)}), bf16[16,16,768]{2,1,0:T(8,128)(2,1)S(1)}, u32[]{:S(2)}, u32[]{:S(2)}) async-start(bf16[16,16,768]{2,1,0:T(8,128)(2,1)} %bitcast.15), calls=%async_computation | async-start | bytes 786432 | tf_op jit(solution)/shard_map/all_to_all | solution.py:499
  64.7 0.0 copy-done
  64.7 6.1 %shard_map.95 = bf16[256,768]{1,0:T(8,128)(2,1)} custom-call(s32[16]{0:T(128)} %count_ref.9, s32[1]{0:T(128)} %bitcast.index_ref, bf16[256,768]{1,0:T(8,128)(2,1)} %bitcast.13, bf16[768,2304]{1,0:T(8,128)(2,1)} %project_hbm.9, bf16[768,768]{1,0:T(8,128)(2,1)} %output_hbm.9), custom_call_target="tpu_custom_call" | custom-call | flops 1509949440 | bytes 9437184 | tf_op jit(solution)/shard_map/pallas_call | solution.py:502
  70.8 5.8 %all-to-all-done = bf16[16,16,768]{2,1,0:T(8,128)(2,1)S(1)} async-done(((bf16[16,16,768]{2,1,0:T(8,128)(2,1)}), bf16[16,16,768]{2,1,0:T(8,128)(2,1)S(1)}, u32[]{:S(2)}, u32[]{:S(2)}) %all-to-all-start) | async-done | bytes 393248 | tf_op jit(solution)/shard_map/all_to_all | solution.py:499
  76.6 3.7 %all-to-all-start.3 = ((bf16[16,16,768]{2,1,0:T(8,128)(2,1)}), bf16[16,16,768]{2,1,0:T(8,128)(2,1)S(1)}, u32[]{:S(2)}, u32[]{:S(2)}) async-start(bf16[16,16,768]{2,1,0:T(8,128)(2,1)} %bitcast.18), calls=%async_computation.3 | async-start | bytes 786432 | tf_op jit(solution)/shard_map/all_to_all | solution.py:499
  80.3 0.0 copy-done.1
  80.3 0.0 copy-start.2
  80.3 6.2 %shard_map.93 = bf16[256,768]{1,0:T(8,128)(2,1)} custom-call(s32[16]{0:T(128)} %count_ref.9, s32[1]{0:T(128)} %bitcast.index_ref, bf16[256,768]{1,0:T(8,128)(2,1)} %bitcast.16, bf16[768,2304]{1,0:T(8,128)(2,1)} %project_hbm.9, bf16[768,768]{1,0:T(8,128)(2,1)} %output_hbm.9), custom_call_target="tpu_custom_call" | custom-call | flops 1509949440 | bytes 9437184 | tf_op jit(solution)/shard_map/pallas_call | solution.py:502
  86.6 5.7 %all-to-all-done.3 = bf16[16,16,768]{2,1,0:T(8,128)(2,1)S(1)} async-done(((bf16[16,16,768]{2,1,0:T(8,128)(2,1)}), bf16[16,16,768]{2,1,0:T(8,128)(2,1)S(1)}, u32[]{:S(2)}, u32[]{:S(2)}) %all-to-all-start.3) | async-done | bytes 393248 | tf_op jit(solution)/shard_map/all_to_all | solution.py:499
  92.3 3.7 %all-to-all-start.1 = ((bf16[16,16,768]{2,1,0:T(8,128)(2,1)}), bf16[16,16,768]{2,1,0:T(8,128)(2,1)S(1)}, u32[]{:S(2)}, u32[]{:S(2)}) async-start(bf16[16,16,768]{2,1,0:T(8,128)(2,1)} %bitcast.17), calls=%async_computation.1 | async-start | bytes 786432 | tf_op jit(solution)/shard_map/all_to_all | solution.py:499
  96.0 0.1 fusion
  96.1 11.8 %all-to-all-done.1 = bf16[16,16,768]{2,1,0:T(8,128)(2,1)S(1)} async-done(((bf16[16,16,768]{2,1,0:T(8,128)(2,1)}), bf16[16,16,768]{2,1,0:T(8,128)(2,1)S(1)}, u32[]{:S(2)}, u32[]{:S(2)}) %all-to-all-start.1) | async-done | bytes 393248 | tf_op jit(solution)/shard_map/all_to_all | solution.py:499
  108.0 0.1 fusion.1
  108.1 0.9 pad_maximum_fusion
  (7 shorter events, 0.0 us)
Async XLA Ops:
  0.0 3.1 %copy-start.4 = (f32[768]{0:T(1024)S(1)}, f32[768]{0:T(1024)}, u32[]{:S(2)}) copy-start(f32[768]{0:T(1024)} %param.12) | copy-start | bytes 9220
  0.0 3.7 %copy-start.5 = (f32[768]{0:T(1024)S(1)}, f32[768]{0:T(1024)}, u32[]{:S(2)}) copy-start(f32[768]{0:T(1024)} %param.15) | copy-start | bytes 9220
  1.2 13.1 %collective-permute-start.1 = (bf16[256,768]{1,0:T(8,128)(2,1)S(1)}, bf16[256,768]{1,0:T(8,128)(2,1)S(1)}, u32[]{:S(2)}, u32[]{:S(2)}) collective-permute-start(bf16[256,768]{1,0:T(8,128)(2,1)S(1)} %get-tuple-element.20), channel_id=1, source_target_pairs={{1,0},{2,1},{3,2},{4,3},{5,4},{6,5},{7,6},{8,7},{9,8},{10,9},{11,1... | collective-permute-start | bytes 1179656 | tf_op jit(solution)/shard_map/ppermute | solution.py:437
  14.3 0.7 copy-start.6
  26.0 29.8 %all-to-all-start.2 = ((bf16[16,16,768]{2,1,0:T(8,128)(2,1)}), bf16[16,16,768]{2,1,0:T(8,128)(2,1)S(1)}, u32[]{:S(2)}, u32[]{:S(2)}) async-start(bf16[16,16,768]{2,1,0:T(8,128)(2,1)} %bitcast.14), calls=%async_computation.2 | async-start | bytes 786432 | tf_op jit(solution)/shard_map/all_to_all | solution.py:499
  33.5 10.6 %collective-permute-start = (bf16[256,768]{1,0:T(8,128)(2,1)S(1)}, bf16[256,768]{1,0:T(8,128)(2,1)S(1)}, u32[]{:S(2)}, u32[]{:S(2)}) collective-permute-start(bf16[256,768]{1,0:T(8,128)(2,1)S(1)} %get-tuple-element.19), channel_id=1, source_target_pairs={{0,1},{1,2},{2,3},{3,4},{4,5},{5,6},{6,7},{7,8},{8,9},{9,10},{10,1... | collective-permute-start | bytes 1179656 | tf_op jit(solution)/shard_map/ppermute | solution.py:436
  44.1 0.7 copy-start.7
  55.8 8.9 %copy-start = (bf16[16,16,768]{2,1,0:T(8,128)(2,1)}, bf16[16,16,768]{2,1,0:T(8,128)(2,1)S(1)}, u32[]{:S(2)}) copy-start(bf16[16,16,768]{2,1,0:T(8,128)(2,1)S(1)} %all-to-all-done.2) | copy-start | bytes 1179652
  55.8 20.8 %all-to-all-start = ((bf16[16,16,768]{2,1,0:T(8,128)(2,1)}), bf16[16,16,768]{2,1,0:T(8,128)(2,1)S(1)}, u32[]{:S(2)}, u32[]{:S(2)}) async-start(bf16[16,16,768]{2,1,0:T(8,128)(2,1)} %bitcast.15), calls=%async_computation | async-start | bytes 786432 | tf_op jit(solution)/shard_map/all_to_all | solution.py:499
  76.6 3.7 %copy-start.1 = (bf16[16,16,768]{2,1,0:T(8,128)(2,1)}, bf16[16,16,768]{2,1,0:T(8,128)(2,1)S(1)}, u32[]{:S(2)}) copy-start(bf16[16,16,768]{2,1,0:T(8,128)(2,1)S(1)} %all-to-all-done) | copy-start | bytes 1179652
  76.6 15.7 %all-to-all-start.3 = ((bf16[16,16,768]{2,1,0:T(8,128)(2,1)}), bf16[16,16,768]{2,1,0:T(8,128)(2,1)S(1)}, u32[]{:S(2)}, u32[]{:S(2)}) async-start(bf16[16,16,768]{2,1,0:T(8,128)(2,1)} %bitcast.18), calls=%async_computation.3 | async-start | bytes 786432 | tf_op jit(solution)/shard_map/all_to_all | solution.py:499
  80.3 15.7 %copy-start.2 = (bf16[256,768]{1,0:T(8,128)(2,1)S(1)}, bf16[256,768]{1,0:T(8,128)(2,1)}, u32[]{:S(2)}) copy-start(bf16[256,768]{1,0:T(8,128)(2,1)} %get-tuple-element.17) | copy-start | bytes 1179652
  86.6 21.4 %copy-start.3 = (bf16[256,768]{1,0:T(8,128)(2,1)S(1)}, bf16[256,768]{1,0:T(8,128)(2,1)}, u32[]{:S(2)}) copy-start(bf16[256,768]{1,0:T(8,128)(2,1)} %get-tuple-element.15) | copy-start | bytes 1179652
  92.3 15.7 %all-to-all-start.1 = ((bf16[16,16,768]{2,1,0:T(8,128)(2,1)}), bf16[16,16,768]{2,1,0:T(8,128)(2,1)S(1)}, u32[]{:S(2)}, u32[]{:S(2)}) async-start(bf16[16,16,768]{2,1,0:T(8,128)(2,1)} %bitcast.17), calls=%async_computation.1 | async-start | bytes 786432 | tf_op jit(solution)/shard_map/all_to_all | solution.py:499

commit v3 on v2

--- a/solution.py
+++ b/solution.py
@@ -18,6 +18,7 @@
 PAIR = 2 * HD
 CHUNK = 2 * BLK
 VMEM_LIMIT = 60 * 1024 * 1024
+ROOMY = 56 << 20
 EPS = 1e-06
 MASKED = -1e30
 
@@ -28,7 +29,7 @@
 def norm_rows(values, gain):
     wide = values.astype(F32)
     meansq = jnp.mean(wide * wide, axis=-1, keepdims=True)
-    return (wide * lax.rsqrt(meansq + EPS) * gain).astype(BF16)
+    return (wide * lax.rsqrt(meansq + EPS) * gain.reshape(1, D)).astype(BF16)
 
 
 def pair_scores(q, k):
@@ -131,9 +132,14 @@
     x_hbm,
     project_hbm,
     output_hbm,
-    first_hbm,
-    state_hbm,
-    second_hbm,
+    first0_hbm,
+    state0_hbm,
+    second0_hbm,
+    query0_hbm,
+    first1_hbm,
+    state1_hbm,
+    second1_hbm,
+    query1_hbm,
     x_s,
     project_s,
     output_s,
@@ -164,8 +170,8 @@
     for copy, cols in ((query_in, QUERY), (key_in, KEY), (value_in, VALUE)):
         copy.wait()
         first_s[:, cols] = times(hidden, project_s[:, cols]).astype(BF16)
-    first_out = pltpu.make_async_copy(first_s, first_hbm, out_sems.at[0])
-    first_out.start()
+    half = 2 * BLK
+    out = copies(out_sems.at[0:2], (first_s.at[:half], first0_hbm), (first_s.at[half:], first1_hbm))
     tables = (reach_ref, count_ref, frame_len, total)
     space_attention(
         offset + BLK,
@@ -180,16 +186,19 @@
     )
     output_in.wait()
     state_s[...] = (x_s[inner].astype(F32) + times(mixed_s[...], output_s[...])).astype(BF16)
-    state_out = pltpu.make_async_copy(state_s, state_hbm, out_sems.at[1])
-    state_out.start()
+    out += copies(out_sems.at[2:4], (state_s.at[:BLK], state0_hbm), (state_s.at[BLK:], state1_hbm))
     hidden = norm_rows(state_s[...], gain)
     for cols in (QUERY, KEY, VALUE):
         second_s[:, cols] = times(hidden, project_s[:, cols]).astype(BF16)
-    second_out = pltpu.make_async_copy(second_s, second_hbm, out_sems.at[2])
-    second_out.start()
-    first_out.wait()
-    state_out.wait()
-    second_out.wait()
+    out += copies(
+        out_sems.at[4:8],
+        (second_s.at[:, D:], second0_hbm),
+        (second_s.at[:, D:], second1_hbm),
+        (second_s.at[:BLK, QUERY], query0_hbm),
+        (second_s.at[BLK:, QUERY], query1_hbm),
+    )
+    for copy in out:
+        copy.wait()
 
 
 def side_kernel(
@@ -206,6 +215,7 @@
     first_hbm,
     middle_hbm,
     second_hbm,
+    query2_hbm,
     project_hbm,
     output_hbm,
     state_ref,
@@ -238,20 +248,18 @@
         begin = local_rows - half
         own_part, far_part = front, back
         mid_part, edge_part = front, back
-        far_edge = low
+        own_edge, far_edge = high, low
         own_at, far_at = low, high
-        mid_own, mid_at, edge_at = high, low, high
+        mid_at, edge_at = low, high
         start1, start2 = begin + BLK, begin
-        own_rows = pl.ds(begin, half)
         edge_rows = pl.ds(local_rows - BLK, BLK)
     else:
         own_part, far_part = back, front
         mid_part, edge_part = back, front
-        far_edge = high
+        own_edge, far_edge = low, high
         own_at, far_at = high, low
-        mid_own, mid_at, edge_at = low, high, low
+        mid_at, edge_at = high, low
         start1, start2 = -BLK, 0
-        own_rows = pl.ds(0, half)
         edge_rows = pl.ds(0, BLK)
     halo_in, key_in, value_in, query_in, k_in, v_in, q_in, output_in, x_in, k2_in, v2_in, q2_in, middle_in = copies(
         in_sems,
@@ -259,15 +267,15 @@
         (project_hbm.at[:, KEY], project_s.at[:, KEY]),
         (project_hbm.at[:, VALUE], project_s.at[:, VALUE]),
         (project_hbm.at[:, QUERY], project_s.at[:, QUERY]),
-        (first_hbm.at[own_rows, KEY], k_s.at[own_part]),
-        (first_hbm.at[own_rows, VALUE], v_s.at[own_part]),
-        (first_hbm.at[edge_rows, QUERY], q_s.at[own_at]),
+        (first_hbm.at[:, KEY], k_s.at[own_part]),
+        (first_hbm.at[:, VALUE], v_s.at[own_part]),
+        (first_hbm.at[own_edge, QUERY], q_s.at[own_at]),
         (output_hbm, output_s),
         (x_hbm.at[edge_rows], x_s),
-        (second_hbm.at[:, KEY], k2_s.at[mid_part]),
-        (second_hbm.at[:, VALUE], v2_s.at[mid_part]),
-        (second_hbm.at[mid_own, QUERY], q2_s.at[mid_at]),
-        (middle_hbm.at[mid_own], middle_s),
+        (second_hbm.at[:, :D], k2_s.at[mid_part]),
+        (second_hbm.at[:, D:], v2_s.at[mid_part]),
+        (query2_hbm, q2_s.at[mid_at]),
+        (middle_hbm, middle_s),
     )
     tables = (reach_ref, count_ref, frame_len, total)
     halo_in.wait()
@@ -309,32 +317,40 @@
     local_rows,
     devices,
     chunk,
+    merged,
     count_ref,
     index_ref,
     x_hbm,
     project_hbm,
     output_hbm,
-    update_ref,
-    x_s,
-    project_s,
-    output_s,
-    qkv_s,
-    mixed_s,
-    bias_s,
-    scores_s,
-    expon_s,
-    in_sems,
+    *rest,
 ):
+    other_hbm = rest[0] if merged else None
+    (
+        update_ref,
+        x_s,
+        project_s,
+        output_s,
+        qkv_s,
+        mixed_s,
+        bias_s,
+        scores_s,
+        expon_s,
+        in_sems,
+    ) = rest[1 if merged else 0 :][:10]
+    other_s = rest[-1]
     rows = x_s.shape[0]
     slots = rows // F
     piece = rows // devices
-    x_in, query_in, key_in, value_in, output_in = copies(
+    others = [(other_hbm, other_s)] if merged else []
+    x_in, query_in, key_in, value_in, output_in, *other_in = copies(
         in_sems,
         (x_hbm, x_s),
         (project_hbm.at[:, QUERY], project_s.at[:, QUERY]),
         (project_hbm.at[:, KEY], project_s.at[:, KEY]),
         (project_hbm.at[:, VALUE], project_s.at[:, VALUE]),
         (output_hbm, output_s),
+        *others,
     )
     row = lax.broadcasted_iota(jnp.int32, (rows, rows), 0)
     col = lax.broadcasted_iota(jnp.int32, (rows, rows), 1)
@@ -363,7 +379,16 @@
 
     attention(columns(0), columns(D), columns(2 * D), store, bias_s, scores_s, expon_s)
     output_in.wait()
-    update_ref[...] = times(mixed_s[...], output_s[...]).astype(BF16)
+    update = times(mixed_s[...], output_s[...]).astype(BF16)
+    if not merged:
+        update_ref[...] = update
+        return
+    other_in[0].wait()
+    for device in range(devices):
+        part = slice(device * piece, (device + 1) * piece)
+        place = 2 * device * piece
+        update_ref[place : place + piece] = other_s[part]
+        update_ref[place + piece : place + 2 * piece] = update[part]
 
 
 def smem():
@@ -399,10 +424,10 @@
     return pltpu.SemaphoreType.DMA((count,))
 
 
-def call(kernel, flops, exps, **rest):
+def call(kernel, flops, exps, limit=VMEM_LIMIT, **rest):
     return pl.pallas_call(
         kernel,
-        compiler_params=pltpu.CompilerParams(vmem_limit_bytes=VMEM_LIMIT),
+        compiler_params=pltpu.CompilerParams(vmem_limit_bytes=limit),
         cost_estimate=pl.CostEstimate(
             flops=flops, bytes_accessed=16 * D * D, transcendentals=exps
         ),
@@ -428,21 +453,27 @@
     if local_rows != 2 * CHUNK or frame_len % local_rows or CHUNK % devices:
         raise ValueError("unsupported sizes")
     index = lax.axis_index("strip").reshape(1)
-    gain = space_gain.reshape(1, D)
-    gain_t = time_gain.reshape(1, D)
+    piece = CHUNK // devices
 
     up = [(i, i + 1) for i in range(devices - 1)]
     down = [(i + 1, i) for i in range(devices - 1)]
     before = lax.ppermute(frame_tokens[local_rows - CHUNK :], "strip", up)
     after = lax.ppermute(frame_tokens[:CHUNK], "strip", down)
 
-    first, middle, second = call(
+    sides = call(
         functools.partial(middle_kernel, frame_len, total),
         2 * D * D * 10 * CHUNK,
         H * CHUNK * WIN,
-        out_shape=(rows16(local_rows, 3 * D), rows16(CHUNK, D), rows16(CHUNK, 3 * D)),
+        limit=ROOMY,
+        out_shape=(
+            rows16(CHUNK, 3 * D),
+            rows16(BLK, D),
+            rows16(CHUNK, 2 * D),
+            rows16(BLK, D),
+        )
+        * 2,
         in_specs=[smem()] * 3 + [vmem()] + [hbm()] * 3,
-        out_specs=(hbm(),) * 3,
+        out_specs=(hbm(),) * 8,
         scratch_shapes=[
             scratch(local_rows, D),
             scratch(D, 3 * D),
@@ -452,9 +483,9 @@
             scratch(CHUNK, 3 * D),
             *work(BLK, WIN),
             sems(5),
-            sems(3),
+            sems(8),
         ],
-    )(window_reach, valid_count, index, gain, frame_tokens, space_project, space_output)
+    )(window_reach, valid_count, index, space_gain, frame_tokens, space_project, space_output)
 
     def side(halo, is_after):
         return call(
@@ -462,7 +493,8 @@
             2 * D * D * 10 * CHUNK,
             2 * H * CHUNK * WIN,
             out_shape=(rows16(CHUNK, D),) * 2,
-            in_specs=[smem()] * 3 + [vmem()] * 2 + [hbm()] * 7,
+            limit=VMEM_LIMIT if is_after else ROOMY,
+            in_specs=[smem()] * 3 + [vmem()] * 2 + [hbm()] * 8,
             out_specs=(vmem(),) * 2,
             scratch_shapes=[
                 scratch(CHUNK, D),
@@ -484,13 +516,11 @@
             window_reach,
             valid_count,
             index,
-            gain,
-            gain_t,
+            space_gain,
+            time_gain,
             halo,
             frame_tokens,
-            first,
-            middle,
-            second,
+            *(sides[4:] if is_after else sides[:4]),
             space_project,
             space_output,
         )
@@ -498,13 +528,14 @@
     def exchange(x):
         return lax.all_to_all(x, "strip", split_axis=0, concat_axis=0, tiled=True)
 
-    def temporal(x, chunk):
+    def temporal(x, chunk, *other):
+        merged = len(other) > 0
         return call(
-            functools.partial(time_kernel, frame_len, local_rows, devices, chunk),
+            functools.partial(time_kernel, frame_len, local_rows, devices, chunk, merged),
             2 * D * D * 5 * CHUNK,
             H * CHUNK * CHUNK,
-            out_shape=rows16(CHUNK, D),
-            in_specs=[smem()] * 2 + [hbm()] * 3,
+            out_shape=rows16(2 * CHUNK if merged else CHUNK, D),
+            in_specs=[smem()] * 2 + [hbm()] * (3 + len(other)),
             out_specs=vmem(),
             scratch_shapes=[
                 scratch(CHUNK, D),
@@ -512,16 +543,22 @@
                 scratch(D, D),
                 scratch(CHUNK, 3 * D),
                 *work(CHUNK, CHUNK),
-                sems(5),
+                sems(5 + len(other)),
+                *[scratch(CHUNK, D)] * len(other),
             ],
-        )(valid_count, index, x, time_project, time_output)
+        )(valid_count, index, x, time_project, time_output, *other)
 
     state0, hidden0 = side(before, False)
     sent0 = exchange(hidden0)
     state1, hidden1 = side(after, True)
     sent1 = exchange(hidden1)
-    back0 = exchange(temporal(sent0, 0))
-    back1 = exchange(temporal(sent1, 1))
+    update0 = temporal(sent0, 0)
+    if piece % 8:
+        back0 = exchange(update0)
+        back1 = exchange(temporal(sent1, 1))
+    else:
+        back = exchange(temporal(sent1, 1, update0)).reshape(devices, 2, piece, D)
+        back0, back1 = back[:, 0].reshape(CHUNK, D), back[:, 1].reshape(CHUNK, D)
     wide = [
         (s.astype(F32) + b.astype(F32)).astype(BF16) for s, b in ((state0, back0), (state1, back1))
     ]

time: 110 us -> 109 us (level)
  blocking collectives: 0 us -> 24.6 us
  waiting for transfers between devices: 30.2 us -> 14.3 us
  starting transfers between devices: 29.5 us -> 19.9 us
    all_to_all x0 -> x1, blocking collectives: none -> 24.6 us  [exchange(): return lax.all_to_all(x, 'strip', split_axis=0, concat_axis=0, tiled=True)]
    all_to_all x4 -> x2, waiting for transfers between devices: 23.3 us -> 5.76 us  [exchange(): return lax.all_to_all(x, 'strip', split_axis=0, concat_axis=0, tiled=True)]
    all_to_all x4 -> x2, starting transfers between devices: 23.9 us -> 13.2 us  [exchange(): return lax.all_to_all(x, 'strip', split_axis=0, concat_axis=0, tiled=True)]
    ppermute x1, waiting for transfers between devices: 0.01 us -> 8.55 us  [on_device(): after = lax.ppermute(frame_tokens[:CHUNK], 'strip', down)]
    ppermute x1, waiting for transfers between devices: 6.88 us -> 0.01 us  [on_device(): before = lax.ppermute(frame_tokens[local_rows - CHUNK:], 'strip', up)]
    reshape x2 -> x0, local copies, waits for them, and re-layouts: 1.19 us -> none  [the longest x1 0.59 us: on_device(): gain = space_gain.reshape(1, D)]
    unnamed x16 -> x12, local copies, waits for them, and re-layouts: 1.51 us -> 2.24 us
  transfers between devices with their start and end apart: 6 -> 4, of which waited for: 4 -> 2; matrix products, arithmetic and copies ran while one was open for 1% -> 0% of each run, Pallas kernels for 30% -> 25%
where the time goes in v3:
time: 109 us; the launch traced here: 108 us
  Pallas kernels  44.5 us (41%)
  blocking collectives  24.6 us (23%)
  starting transfers between devices  19.9 us (18%)
  waiting for transfers between devices  14.3 us (13%)
  local copies, waits for them, and re-layouts  3.46 us (3%)
  other arithmetic  1.17 us (1%)
    all_to_all x1, blocking collectives, exchange(): return lax.all_to_all(x, 'strip', split_axis=0, concat_axis=0, tiled=True)  24.6 us
    pallas_call x2, Pallas kernels, side(): call(functools.partial(side_kernel, frame_len, total, is_after), 2 * D *...  21.9 us
    all_to_all x2, starting transfers between devices, exchange(): return lax.all_to_all(x, 'strip', split_axis=0, concat_axis=0, tiled=True)  13.2 us
    pallas_call x2, Pallas kernels, temporal(): call(functools.partial(time_kernel, frame_len, local_rows, devices, chunk...  12.4 us
    pallas_call x1, Pallas kernels, on_device(): call(functools.partial(middle_kernel, frame_len, total), 2 * D * D * 10 *...  10.2 us
    ppermute x1, waiting for transfers between devices, on_device(): after = lax.ppermute(frame_tokens[:CHUNK], 'strip', down)  8.55 us
    all_to_all x2, waiting for transfers between devices, exchange(): return lax.all_to_all(x, 'strip', split_axis=0, concat_axis=0, tiled=True)  5.76 us
    ppermute x1, starting transfers between devices, on_device(): before = lax.ppermute(frame_tokens[local_rows - CHUNK:], 'strip', up)  4.53 us
  transfers between devices with their start and end apart: 4, of which 2 were waited for; matrix products, arithmetic and copies ran while one was open for 0% of the time, Pallas kernels for 25%

profile of v3, /device:TPU:1, one launch (start us, length us, event | category | flops | bytes accessed | tf_op | source)
XLA Modules:
  0.0 108.1 jit_solution(5977205938208158695)
XLA Ops:
  0.0 1.2 %fusion.3 = (bf16[256,768]{1,0:T(8,128)(2,1)S(1)}, bf16[256,768]{1,0:T(8,128)(2,1)S(1)}) fusion(bf16[512,768]{1,0:T(8,128)(2,1)} %x_hbm.5), kind=kLoop, calls=%fused_computation.6 | loop fusion | bytes 1572864 | tf_op jit(solution)/shard_map/slice | solution.py:460
  1.2 4.5 %collective-permute-start = (bf16[256,768]{1,0:T(8,128)(2,1)S(1)}, bf16[256,768]{1,0:T(8,128)(2,1)S(1)}, u32[]{:S(2)}, u32[]{:S(2)}) collective-permute-start(bf16[256,768]{1,0:T(8,128)(2,1)S(1)} %get-tuple-element.31), channel_id=1, source_target_pairs={{0,1},{1,2},{2,3},{3,4},{4,5},{5,6},{6,7},{7,8},{8,9},{9,10},{10,1... | collective-permute-start | bytes 1179656 | tf_op jit(solution)/shard_map/ppermute | solution.py:460
  5.7 10.2 %shard_map.91 = (bf16[256,2304]{1,0:T(8,128)(2,1)}, bf16[128,768]{1,0:T(8,128)(2,1)}, bf16[256,1536]{1,0:T(8,128)(2,1)}, bf16[128,768]{1,0:T(8,128)(2,1)}, bf16[...) custom-call(s32[16]{0:T(128)} %reach_ref.5, ...), custom_call_target="tpu_custom_call" | custom-call | flops 3019898880 | bytes 9437184 | tf_op jit(solution)/shard_map/pallas_call | solution.py:463
  16.0 0.0 collective-permute-done.halo_hbm
  16.0 0.0 copy-start.4
  16.0 0.7 copy-done.4
  16.7 10.9 %shard_map.92 = (bf16[256,768]{1,0:T(8,128)(2,1)}, bf16[256,768]{1,0:T(8,128)(2,1)}) custom-call(s32[16]{0:T(128)} %reach_ref.5, s32[16]{0:T(128)} %count_ref.9, s32[1]{0:T(128)} %bitcast.index_ref, f32[768]{0:T(1024)} %gain_ref.5, f32[768]{0:T(1024)} %time_gain_ref.3, bf16[256,768]{1,0:T(8,128)(2,1)} %copy-done.4, bf16[512,768]{1,0:T(8,128)(2,1)} %x_hbm.5, ...), custom_call_target="tpu_custom_call" | custom-call | flops 3019898880 | bytes 9437184 | tf_op jit(solution)/shard_map/pallas_call | solution.py:491
  27.7 5.0 %all-to-all-start.1 = ((bf16[16,16,768]{2,1,0:T(8,128)(2,1)}), bf16[16,16,768]{2,1,0:T(8,128)(2,1)S(1)}, u32[]{:S(2)}, u32[]{:S(2)}) async-start(bf16[16,16,768]{2,1,0:T(8,128)(2,1)} %bitcast.21), calls=%async_computation.1 | async-start | bytes 786432 | tf_op jit(solution)/shard_map/all_to_all | solution.py:529
  32.7 2.2 %collective-permute-start.1 = (bf16[256,768]{1,0:T(8,128)(2,1)S(1)}, bf16[256,768]{1,0:T(8,128)(2,1)S(1)}, u32[]{:S(2)}, u32[]{:S(2)}) collective-permute-start(bf16[256,768]{1,0:T(8,128)(2,1)S(1)} %get-tuple-element.32), channel_id=1, source_target_pairs={{1,0},{2,1},{3,2},{4,3},{5,4},{6,5},{7,6},{8,7},{9,8},{10,9},{11,1... | collective-permute-start | bytes 1179656 | tf_op jit(solution)/shard_map/ppermute | solution.py:461
  34.9 8.5 %collective-permute-done.1.halo_hbm = bf16[256,768]{1,0:T(8,128)(2,1)S(1)} collective-permute-done((bf16[256,768]{1,0:T(8,128)(2,1)S(1)}, bf16[256,768]{1,0:T(8,128)(2,1)S(1)}, u32[]{:S(2)}, u32[]{:S(2)}) %collective-permute-start.1) | collective-permute-done | bytes 393248 | tf_op jit(solution)/shard_map/ppermute | solution.py:461
  43.4 0.0 copy-start.5
  43.4 0.7 copy-done.5
  44.2 10.9 %shard_map.93 = (bf16[256,768]{1,0:T(8,128)(2,1)}, bf16[256,768]{1,0:T(8,128)(2,1)}) custom-call(s32[16]{0:T(128)} %reach_ref.5, s32[16]{0:T(128)} %count_ref.9, s32[1]{0:T(128)} %bitcast.index_ref, f32[768]{0:T(1024)} %gain_ref.5, f32[768]{0:T(1024)} %time_gain_ref.3, bf16[256,768]{1,0:T(8,128)(2,1)} %copy-done.5, bf16[512,768]{1,0:T(8,128)(2,1)} %x_hbm.5, ...), custom_call_target="tpu_custom_call" | custom-call | flops 3019898880 | bytes 9437184 | tf_op jit(solution)/shard_map/pallas_call | solution.py:491
  55.1 0.0 all-to-all-done.1
  55.1 0.0 copy-start.3
  55.2 8.2 %all-to-all-start = ((bf16[16,16,768]{2,1,0:T(8,128)(2,1)}), bf16[16,16,768]{2,1,0:T(8,128)(2,1)S(1)}, u32[]{:S(2)}, u32[]{:S(2)}) async-start(bf16[16,16,768]{2,1,0:T(8,128)(2,1)} %bitcast.22), calls=%async_computation | async-start | bytes 786432 | tf_op jit(solution)/shard_map/all_to_all | solution.py:529
  63.3 0.0 copy-done.3
  63.3 6.1 %shard_map.94.rest_0_ = bf16[256,768]{1,0:T(8,128)(2,1)} custom-call(s32[16]{0:T(128)} %count_ref.9, s32[1]{0:T(128)} %bitcast.index_ref, bf16[256,768]{1,0:T(8,128)(2,1)} %bitcast.20, bf16[768,2304]{1,0:T(8,128)(2,1)} %project_hbm.9, bf16[768,768]{1,0:T(8,128)(2,1)} %output_hbm.9), custom_call_target="tpu_custom_call" | custom-call | flops 1509949440 | bytes 9437184 | tf_op jit(solution)/shard_map/pallas_call | solution.py:533
  69.4 5.8 %all-to-all-done = bf16[16,16,768]{2,1,0:T(8,128)(2,1)S(1)} async-done(((bf16[16,16,768]{2,1,0:T(8,128)(2,1)}), bf16[16,16,768]{2,1,0:T(8,128)(2,1)S(1)}, u32[]{:S(2)}, u32[]{:S(2)}) %all-to-all-start) | async-done | bytes 393248 | tf_op jit(solution)/shard_map/all_to_all | solution.py:529
  75.2 0.0 copy-start
  75.2 0.7 copy-done
  75.9 6.3 %shard_map.95 = bf16[512,768]{1,0:T(8,128)(2,1)} custom-call(s32[16]{0:T(128)} %count_ref.9, s32[1]{0:T(128)} %bitcast.index_ref, bf16[256,768]{1,0:T(8,128)(2,1)} %bitcast.19, bf16[768,2304]{1,0:T(8,128)(2,1)} %project_hbm.9, bf16[768,768]{1,0:T(8,128)(2,1)} %output_hbm.9, bf16[256,768]{1,0:T(8,128)(2,1)} %shard_map.94.rest_0_), custom_call_target="tpu_custom_call" | custom-call | flops 1509949440 | bytes 9437184 | tf_op jit(solution)/shard_map/pallas_call | solution.py:533
  82.2 0.0 copy-start.1
  82.2 0.0 copy-start.2
  82.2 24.6 %all_to_all.31 = bf16[16,32,768]{2,1,0:T(8,128)(2,1)S(1)} all-to-all(bf16[16,32,768]{2,1,0:T(8,128)(2,1)} %bitcast.18), channel_id=1, replica_groups=mesh['group'=2,'strip'=16] {'strip'}, dimensions={0} | all-to-all | bytes 1572864 | tf_op jit(solution)/shard_map/all_to_all | solution.py:529
  106.8 0.1 fusion.2
  106.9 0.0 copy-done.1
  106.9 0.0 copy-done.2
  106.9 0.2 fusion
  107.2 0.9 pad_maximum_fusion
Async XLA Ops:
  1.2 14.8 %collective-permute-start = (bf16[256,768]{1,0:T(8,128)(2,1)S(1)}, bf16[256,768]{1,0:T(8,128)(2,1)S(1)}, u32[]{:S(2)}, u32[]{:S(2)}) collective-permute-start(bf16[256,768]{1,0:T(8,128)(2,1)S(1)} %get-tuple-element.31), channel_id=1, source_target_pairs={{0,1},{1,2},{2,3},{3,4},{4,5},{5,6},{6,7},{7,8},{8,9},{9,10},{10,1... | collective-permute-start | bytes 1179656 | tf_op jit(solution)/shard_map/ppermute | solution.py:460
  16.0 0.7 copy-start.4
  27.7 27.5 %all-to-all-start.1 = ((bf16[16,16,768]{2,1,0:T(8,128)(2,1)}), bf16[16,16,768]{2,1,0:T(8,128)(2,1)S(1)}, u32[]{:S(2)}, u32[]{:S(2)}) async-start(bf16[16,16,768]{2,1,0:T(8,128)(2,1)} %bitcast.21), calls=%async_computation.1 | async-start | bytes 786432 | tf_op jit(solution)/shard_map/all_to_all | solution.py:529
  32.7 10.7 %collective-permute-start.1 = (bf16[256,768]{1,0:T(8,128)(2,1)S(1)}, bf16[256,768]{1,0:T(8,128)(2,1)S(1)}, u32[]{:S(2)}, u32[]{:S(2)}) collective-permute-start(bf16[256,768]{1,0:T(8,128)(2,1)S(1)} %get-tuple-element.32), channel_id=1, source_target_pairs={{1,0},{2,1},{3,2},{4,3},{5,4},{6,5},{7,6},{8,7},{9,8},{10,9},{11,1... | collective-permute-start | bytes 1179656 | tf_op jit(solution)/shard_map/ppermute | solution.py:461
  43.4 0.7 copy-start.5
  55.1 8.2 %copy-start.3 = (bf16[16,16,768]{2,1,0:T(8,128)(2,1)}, bf16[16,16,768]{2,1,0:T(8,128)(2,1)S(1)}, u32[]{:S(2)}) copy-start(bf16[16,16,768]{2,1,0:T(8,128)(2,1)S(1)} %all-to-all-done.1) | copy-start | bytes 1179652
  55.2 20.0 %all-to-all-start = ((bf16[16,16,768]{2,1,0:T(8,128)(2,1)}), bf16[16,16,768]{2,1,0:T(8,128)(2,1)S(1)}, u32[]{:S(2)}, u32[]{:S(2)}) async-start(bf16[16,16,768]{2,1,0:T(8,128)(2,1)} %bitcast.22), calls=%async_computation | async-start | bytes 786432 | tf_op jit(solution)/shard_map/all_to_all | solution.py:529
  75.2 0.7 copy-start
  82.2 24.7 %copy-start.1 = (bf16[256,768]{1,0:T(8,128)(2,1)S(1)}, bf16[256,768]{1,0:T(8,128)(2,1)}, u32[]{:S(2)}) copy-start(bf16[256,768]{1,0:T(8,128)(2,1)} %get-tuple-element.21) | copy-start | bytes 1179652
  82.2 24.7 %copy-start.2 = (bf16[256,768]{1,0:T(8,128)(2,1)S(1)}, bf16[256,768]{1,0:T(8,128)(2,1)}, u32[]{:S(2)}) copy-start(bf16[256,768]{1,0:T(8,128)(2,1)} %get-tuple-element.28) | copy-start | bytes 1179652

commit v4 on v2

v4 whole, which is shorter than its diff:
```python
import functools

import jax
import jax.numpy as jnp
from jax import lax
from jax.experimental import pallas as pl
from jax.experimental.pallas import tpu as pltpu
from jax.sharding import PartitionSpec as P


F = 16
HALO = 128
H = 12
HD = 64
D = 768
BLK = HALO
WIN = 3 * BLK
PAIR = 2 * HD
CHUNK = 2 * BLK
VMEM_LIMIT = 60 * 1024 * 1024
EPS = 1e-06
MASKED = -1e30

BF16 = jnp.bfloat16
F32 = jnp.float32


def norm_rows(values, gain):
    wide = values.astype(F32)
    meansq = jnp.mean(wide * wide, axis=-1, keepdims=True)
    return (wide * lax.rsqrt(meansq + EPS) * gain.reshape(1, D)).astype(BF16)


def pair_scores(q, k):
    lane = lax.broadcasted_iota(jnp.int32, (1, PAIR), 1)
    scale = HD ** (-0.5)
    left = jnp.where(lane < HD, scale, 0.0).astype(BF16)
    right = jnp.where(lane < HD, 0.0, scale).astype(BF16)
    both = jnp.concatenate([q * left, q * right], axis=0)
    return lax.dot_general(both, k, (((1,), (1,)), ((), ())), preferred_element_type=F32)


def pair_expon(scores, bias):
    rows, keys = bias.shape
    scores = scores.reshape(2, rows, keys) + bias[None]
    highest = jnp.max(scores, axis=-1, keepdims=True)
    return jnp.exp(scores - highest).reshape(2 * rows, keys).astype(BF16)


def pair_mixed(expon, v):
    rows = expon.shape[0] // 2
    lane = lax.broadcasted_iota(jnp.int32, (1, PAIR), 1)
    mixed = jnp.dot(
        expon, jnp.concatenate([v, jnp.ones_like(v)], axis=1), preferred_element_type=F32
    )
    mixed = (mixed[:, :PAIR] * (1.0 / mixed[:, PAIR:])).reshape(2, rows, PAIR)
    return jnp.where(lane < HD, mixed[0], mixed[1]).astype(BF16)


def lanes_of(pair):
    return slice(pair * PAIR, (pair + 1) * PAIR)


def attention(query, key, value, store, bias_ref, scores_s, expon_s):
    for pair in range(H // 2):
        scores_s[pair] = pair_scores(query(lanes_of(pair)), key(lanes_of(pair)))
    for pair in range(H // 2):
        expon_s[pair] = pair_expon(scores_s[pair], bias_ref[...])
    for pair in range(H // 2):
        store(lanes_of(pair), pair_mixed(expon_s[pair], value(lanes_of(pair))))


def window_bias(start, reach_ref, count_ref, frame_len, total):
    row = lax.broadcasted_iota(jnp.int32, (BLK, WIN), 0)
    col = lax.broadcasted_iota(jnp.int32, (BLK, WIN), 1)
    distance = col - BLK - row
    reach = reach_ref[lax.div(jnp.clip(start, 0, total - 1), frame_len)]
    least = jnp.zeros((1, WIN), jnp.int32)
    place = lax.broadcasted_iota(jnp.int32, (1, WIN), 1)
    for j in range(3):
        at = start + (j - 1) * BLK
        inside = (at >= 0) & (at < total)
        frame = lax.div(jnp.clip(at, 0, total - 1), frame_len)
        first = (frame + 1) * frame_len - count_ref[frame] - at
        first = jnp.where(inside, first, WIN) + j * BLK
        least = jnp.where(place >= j * BLK, first, least)
    living = (col >= least) | (distance == 0)
    return jnp.where((jnp.abs(distance) <= reach) & living, 0.0, MASKED).astype(F32)


def space_attention(blocks, start_of, window_of, tables, q, k, v, mixed_s, bias_s, scores_s, expon_s):
    def load(what, at, length):
        ref, row, column = what
        rows = pl.ds(pl.multiple_of(row + at, BLK), length)
        return lambda lanes: ref[rows, column + lanes.start : column + lanes.stop]

    def one_block(i, carry):
        bias_s[...] = window_bias(start_of(i), *tables)
        rows = pl.ds(pl.multiple_of(i * BLK, BLK), BLK)

        def store(lanes, mixed):
            mixed_s[rows, lanes] = mixed

        attention(
            load(q, i * BLK, BLK),
            load(k, window_of(i), WIN),
            load(v, window_of(i), WIN),
            store,
            bias_s,
            scores_s,
            expon_s,
        )
        return carry

    lax.fori_loop(0, blocks, one_block, 0)


def times(x, weight):
    return jnp.dot(x, weight, preferred_element_type=F32)


def copies(sems, *pairs):
    made = [pltpu.make_async_copy(a, b, sems.at[i]) for i, (a, b) in enumerate(pairs)]
    for copy in made:
        copy.start()
    return made


QUERY, KEY, VALUE = slice(0, D), slice(D, 2 * D), slice(2 * D, 3 * D)


def middle_kernel(
    frame_len,
    total,
    reach_ref,
    count_ref,
    index_ref,
    gain_ref,
    x_hbm,
    project_hbm,
    output_hbm,
    first_hbm,
    state_hbm,
    second_hbm,
    x_s,
    project_s,
    output_s,
    first_s,
    state_s,
    second_s,
    mixed_s,
    bias_s,
    scores_s,
    expon_s,
    in_sems,
    out_sems,
):
    rows = x_s.shape[0]
    offset = index_ref[0] * rows
    gain = gain_ref[...]
    inner = slice(BLK, rows - BLK)
    x_in, query_in, key_in, value_in, output_in = copies(
        in_sems,
        (x_hbm, x_s),
        (project_hbm.at[:, QUERY], project_s.at[:, QUERY]),
        (project_hbm.at[:, KEY], project_s.at[:, KEY]),
        (project_hbm.at[:, VALUE], project_s.at[:, VALUE]),
        (output_hbm, output_s),
    )
    x_in.wait()
    hidden = norm_rows(x_s[...], gain)
    for copy, cols in ((query_in, QUERY), (key_in, KEY), (value_in, VALUE)):
        copy.wait()
        first_s[:, cols] = times(hidden, project_s[:, cols]).astype(BF16)
    first_out = pltpu.make_async_copy(first_s, first_hbm, out_sems.at[0])
    first_out.start()
    tables = (reach_ref, count_ref, frame_len, total)
    space_attention(
        2,
        lambda i: offset + (i + 1) * BLK,
        lambda i: i * BLK,
        tables,
        (first_s, BLK, 0),
        (first_s, 0, D),
        (first_s, 0, 2 * D),
        mixed_s,
        bias_s,
        scores_s,
        expon_s,
    )
    output_in.wait()
    state_s[...] = (x_s[inner].astype(F32) + times(mixed_s[...], output_s[...])).astype(BF16)
    state_out = pltpu.make_async_copy(state_s, state_hbm, out_sems.at[1])
    state_out.start()
    hidden = norm_rows(state_s[...], gain)
    for cols in (QUERY, KEY, VALUE):
        second_s[:, cols] = times(hidden, project_s[:, cols]).astype(BF16)
    second_out = pltpu.make_async_copy(second_s, second_hbm, out_sems.at[2])
    second_out.start()
    first_out.wait()
    state_out.wait()
    second_out.wait()


def sides_kernel(
    frame_len,
    total,
    reach_ref,
    count_ref,
    index_ref,
    gain_ref,
    time_gain_ref,
    before_hbm,
    after_hbm,
    x_hbm,
    first_hbm,
    middle_hbm,
    second_hbm,
    project_hbm,
    output_hbm,
    state_ref,
    hidden_ref,
    halo_s,
    edge_s,
    middle_s,
    project_s,
    output_s,
    q_s,
    k_s,
    v_s,
    q2_s,
    k2_s,
    v2_s,
    mixed_s,
    bias_s,
    scores_s,
    expon_s,
    in_sems,
):
    rows = x_hbm.shape[0]
    offset = index_ref[0] * rows
    gain = gain_ref[...]
    half = 2 * BLK

    def block(first, last=None):
        return slice(first * BLK, (first + 1 if last is None else last) * BLK)

    (
        before_in,
        after_in,
        key_in,
        value_in,
        query_in,
        k_in,
        v_in,
        q_low_in,
        q_high_in,
        output_in,
        x_low_in,
        x_high_in,
        k2_in,
        v2_in,
        q2_in,
        middle_in,
    ) = copies(
        in_sems,
        (before_hbm, halo_s.at[block(0, 2)]),
        (after_hbm, halo_s.at[block(2, 4)]),
        (project_hbm.at[:, KEY], project_s.at[:, KEY]),
        (project_hbm.at[:, VALUE], project_s.at[:, VALUE]),
        (project_hbm.at[:, QUERY], project_s.at[:, QUERY]),
        (first_hbm.at[:, KEY], k_s.at[block(2, 6)]),
        (first_hbm.at[:, VALUE], v_s.at[block(2, 6)]),
        (first_hbm.at[block(0), QUERY], q_s.at[block(1)]),
        (first_hbm.at[block(3), QUERY], q_s.at[block(2)]),
        (output_hbm, output_s),
        (x_hbm.at[block(0)], edge_s.at[block(1)]),
        (x_hbm.at[block(3)], edge_s.at[block(2)]),
        (second_hbm.at[:, KEY], k2_s.at[block(2, 4)]),
        (second_hbm.at[:, VALUE], v2_s.at[block(2, 4)]),
        (second_hbm.at[:, QUERY], q2_s.at[block(1, 3)]),
        (middle_hbm, middle_s),
    )
    tables = (reach_ref, count_ref, frame_len, total)
    work = (mixed_s, bias_s, scores_s, expon_s)
    before_in.wait()
    after_in.wait()
    hidden = norm_rows(halo_s[...], gain)
    for copy, cols, ref in ((key_in, KEY, k_s), (value_in, VALUE, v_s)):
        copy.wait()
        made = times(hidden, project_s[:, cols]).astype(BF16)
        ref[block(0, 2)] = made[:half]
        ref[block(6, 8)] = made[half:]
    query_in.wait()
    made = times(hidden[block(1, 3)], project_s[:, QUERY]).astype(BF16)
    q_s[block(0)] = made[:BLK]
    q_s[block(3)] = made[BLK:]
    for copy in (k_in, v_in, q_low_in, q_high_in):
        copy.wait()

    def skip(i):
        return jnp.where(i >= 2, half, 0)

    space_attention(
        4,
        lambda i: offset + (i - 1) * BLK + skip(i),
        lambda i: i * BLK + skip(i),
        tables,
        (q_s, 0, 0),
        (k_s, 0, 0),
        (v_s, 0, 0),
        *work,
    )
    output_in.wait()
    x_low_in.wait()
    x_high_in.wait()
    update = times(mixed_s[...], output_s[...])
    edge_s[block(0)] = (halo_s[block(1)].astype(F32) + update[block(0)]).astype(BF16)
    edge_s[block(1, 3)] = (edge_s[block(1, 3)].astype(F32) + update[block(1, 3)]).astype(BF16)
    edge_s[block(3)] = (halo_s[block(2)].astype(F32) + update[block(3)]).astype(BF16)

    hidden = norm_rows(edge_s[...], gain)
    for cols, ref in ((KEY, k2_s), (VALUE, v2_s)):
        made = times(hidden, project_s[:, cols]).astype(BF16)
        ref[block(0, 2)] = made[:half]
        ref[block(4, 6)] = made[half:]
    made = times(hidden[block(1, 3)], project_s[:, QUERY]).astype(BF16)
    q2_s[block(0)] = made[:BLK]
    q2_s[block(3)] = made[BLK:]
    for copy in (k2_in, v2_in, q2_in):
        copy.wait()
    space_attention(
        4,
        lambda i: offset + i * BLK,
        lambda i: i * BLK,
        tables,
        (q2_s, 0, 0),
        (k2_s, 0, 0),
        (v2_s, 0, 0),
        *work,
    )
    middle_in.wait()
    update = times(mixed_s[...], output_s[...])
    state_ref[block(0)] = (edge_s[block(1)].astype(F32) + update[block(0)]).astype(BF16)
    state_ref[block(1, 3)] = (middle_s[...].astype(F32) + update[block(1, 3)]).astype(BF16)
    state_ref[block(3)] = (edge_s[block(2)].astype(F32) + update[block(3)]).astype(BF16)
    hidden_ref[...] = norm_rows(state_ref[...], time_gain_ref[...])


def time_kernel(
    frame_len,
    local_rows,
    devices,
    count_ref,
    index_ref,
    x_hbm,
    project_hbm,
    output_hbm,
    update_hbm,
    x_s,
    project_s,
    output_s,
    qkv_s,
    update_s,
    mixed_s,
    bias_s,
    scores_s,
    expon_s,
    in_sems,
    out_sems,
):
    groups, _, group, _ = x_s.shape
    rows = F * group
    piece = local_rows // devices
    *x_in, query_in, key_in, value_in, output_in = copies(
        in_sems,
        *[(x_hbm.at[:, g * group : (g + 1) * group], x_s.at[g]) for g in range(groups)],
        (project_hbm.at[:, QUERY], project_s.at[:, QUERY]),
        (project_hbm.at[:, KEY], project_s.at[:, KEY]),
        (project_hbm.at[:, VALUE], project_s.at[:, VALUE]),
        (output_hbm, output_s),
    )
    row = lax.broadcasted_iota(jnp.int32, (rows, rows), 0)
    col = lax.broadcasted_iota(jnp.int32, (rows, rows), 1)
    key = lax.broadcasted_iota(jnp.int32, (1, rows), 1)
    least = jnp.zeros((1, rows), jnp.int32)
    for g in range(F):
        least = jnp.where(lax.div(key, group) == g, frame_len - count_ref[g], least)
    same = lax.rem(row, group) == lax.rem(col, group)
    for g in range(groups):
        slot = lax.rem(key, group) + g * group
        place = lax.div(slot, piece) * local_rows + lax.rem(slot, piece) + index_ref[0] * piece
        living = jnp.where(place >= least, 1, 0)
        bias_s[g] = jnp.where(same & ((living == 1) | (row == col)), 0.0, MASKED).astype(F32)

    for copy in x_in:
        copy.wait()
    x = x_s[...].reshape(groups * rows, D)
    for copy, cols in ((query_in, QUERY), (key_in, KEY), (value_in, VALUE)):
        copy.wait()
        qkv_s[:, cols] = times(x, project_s[:, cols]).astype(BF16)
    output_in.wait()

    for g in range(groups):
        part = slice(g * rows, (g + 1) * rows)

        def columns(first):
            return lambda lanes: qkv_s[part, first + lanes.start : first + lanes.stop]

        def store(lanes, mixed):
            mixed_s[part, lanes] = mixed

        attention(columns(0), columns(D), columns(2 * D), store, bias_s.at[g], scores_s, expon_s)
    out = []
    for g in range(groups):
        part = slice(g * rows, (g + 1) * rows)
        update = times(mixed_s[part], output_s[...]).astype(BF16)
        update_s[g] = update.reshape(F, group, D)
        out += copies(
            out_sems.at[g : g + 1], (update_s.at[g], update_hbm.at[:, g * group : (g + 1) * group])
        )
    for copy in out:
        copy.wait()


def smem():
    return pl.BlockSpec(memory_space=pltpu.SMEM)


def vmem():
    return pl.BlockSpec(memory_space=pltpu.VMEM)


def hbm():
    return pl.BlockSpec(memory_space=pl.ANY)


def rows16(rows, cols):
    return jax.ShapeDtypeStruct((rows, cols), BF16)


def scratch(rows, cols):
    return pltpu.VMEM((rows, cols), BF16)


def work(mixed_rows, rows, keys, masks=()):
    return [
        scratch(mixed_rows, D),
        pltpu.VMEM((*masks, rows, keys), F32),
        pltpu.VMEM((H // 2, 2 * rows, keys), F32),
        pltpu.VMEM((H // 2, 2 * rows, keys), BF16),
    ]


def sems(count):
    return pltpu.SemaphoreType.DMA((count,))


def call(kernel, flops, exps, **rest):
    return pl.pallas_call(
        kernel,
        compiler_params=pltpu.CompilerParams(vmem_limit_bytes=VMEM_LIMIT),
        cost_estimate=pl.CostEstimate(
            flops=flops, bytes_accessed=16 * D * D, transcendentals=exps
        ),
        **rest,
    )


def on_device(
    frame_tokens,
    window_reach,
    valid_count,
    space_gain,
    space_project,
    space_output,
    time_gain,
    time_project,
    time_output,
):
    devices = lax.axis_size("strip")
    local_rows = frame_tokens.shape[0]
    total = local_rows * devices
    frame_len = total // F
    slots = local_rows // F
    groups = 2
    group = slots // groups
    if local_rows != 2 * CHUNK or frame_len % local_rows or local_rows % devices:
        raise ValueError("unsupported sizes")
    index = lax.axis_index("strip").reshape(1)

    up = [(i, i + 1) for i in range(devices - 1)]
    down = [(i + 1, i) for i in range(devices - 1)]
    before = lax.ppermute(frame_tokens[local_rows - CHUNK :], "strip", up)
    after = lax.ppermute(frame_tokens[:CHUNK], "strip", down)

    first, middle, second = call(
        functools.partial(middle_kernel, frame_len, total),
        2 * D * D * 10 * CHUNK,
        H * CHUNK * WIN,
        out_shape=(rows16(local_rows, 3 * D), rows16(CHUNK, D), rows16(CHUNK, 3 * D)),
        in_specs=[smem()] * 3 + [vmem()] + [hbm()] * 3,
        out_specs=(hbm(),) * 3,
        scratch_shapes=[
            scratch(local_rows, D),
            scratch(D, 3 * D),
            scratch(D, D),
            scratch(local_rows, 3 * D),
            scratch(CHUNK, D),
            scratch(CHUNK, 3 * D),
            *work(CHUNK, BLK, WIN),
            sems(5),
            sems(3),
        ],
    )(window_reach, valid_count, index, space_gain, frame_tokens, space_project, space_output)

    state, hidden = call(
        functools.partial(sides_kernel, frame_len, total),
        2 * D * D * 20 * CHUNK,
        4 * H * CHUNK * WIN,
        out_shape=(rows16(local_rows, D),) * 2,
        in_specs=[smem()] * 3 + [vmem()] * 2 + [hbm()] * 8,
        out_specs=(vmem(),) * 2,
        scratch_shapes=[
            scratch(local_rows, D),
            scratch(local_rows, D),
            scratch(CHUNK, D),
            scratch(D, 3 * D),
            scratch(D, D),
            scratch(local_rows, D),
            scratch(local_rows + 2 * CHUNK, D),
            scratch(local_rows + 2 * CHUNK, D),
            scratch(local_rows, D),
            scratch(local_rows + CHUNK, D),
            scratch(local_rows + CHUNK, D),
            *work(local_rows, BLK, WIN),
            sems(16),
        ],
    )(
        window_reach,
        valid_count,
        index,
        space_gain,
        time_gain,
        before,
        after,
        frame_tokens,
        first,
        middle,
        second,
        space_project,
        space_output,
    )

    def exchange(x):
        return lax.all_to_all(x, "strip", split_axis=0, concat_axis=0, tiled=True)

    gathered = exchange(hidden).reshape(F, slots, D)
    update = call(
        functools.partial(time_kernel, frame_len, local_rows, devices),
        2 * D * D * 10 * CHUNK,
        2 * H * CHUNK * CHUNK,
        out_shape=jax.ShapeDtypeStruct((F, slots, D), BF16),
        in_specs=[smem()] * 2 + [hbm()] * 3,
        out_specs=hbm(),
        scratch_shapes=[
            pltpu.VMEM((groups, F, group, D), BF16),
            scratch(D, 3 * D),
            scratch(D, D),
            scratch(local_rows, 3 * D),
            pltpu.VMEM((groups, F, group, D), BF16),
            *work(local_rows, F * group, F * group, (groups,)),
            sems(4 + groups),
            sems(groups),
        ],
    )(valid_count, index, gathered, time_project, time_output)
    returned = exchange(update.reshape(local_rows, D))
    return (state.astype(F32) + returned.astype(F32)).astype(BF16)


def solution(mesh):
    return jax.shard_map(
        on_device,
        mesh=mesh,
        in_specs=(
            P(("group", "strip"), None),
            P("group"),
            P("group"),
            P(),
            P(),
            P(),
            P(),
            P(),
            P(),
        ),
        out_specs=P(("group", "strip"), None),
        check_vma=False,
    )
```

time: 110 us -> 97.8 us (0.89)
  blocking collectives: 0 us -> 50.7 us
  waiting for transfers between devices: 30.2 us -> 0.01 us
  starting transfers between devices: 29.5 us -> 6.45 us
  Pallas kernels: 44.1 us -> 37 us
  local copies, waits for them, and re-layouts: 3.89 us -> 2.02 us
    all_to_all x0 -> x2, blocking collectives: none -> 50.7 us  [exchange(): return lax.all_to_all(x, 'strip', split_axis=0, concat_axis=0, tiled=True)]
    all_to_all x4 -> x0, starting transfers between devices: 23.9 us -> none  [exchange(): return lax.all_to_all(x, 'strip', split_axis=0, concat_axis=0, tiled=True)]
    all_to_all x4 -> x0, waiting for transfers between devices: 23.3 us -> none  [exchange(): return lax.all_to_all(x, 'strip', split_axis=0, concat_axis=0, tiled=True)]
    pallas_call x4 -> x2, Pallas kernels: 34.2 us -> 27.1 us  [the longest x1 18.2 us: on_device(): call(functools.partial(sides_kernel, frame_len, total), 2 * D * D * 20 *...]
    ppermute x1, waiting for transfers between devices: 6.88 us -> 0.01 us  [on_device(): before = lax.ppermute(frame_tokens[local_rows - CHUNK:], 'strip', up)]
    reshape x2 -> x0, local copies, waits for them, and re-layouts: 1.19 us -> none  [the longest x1 0.59 us: on_device(): gain = space_gain.reshape(1, D)]
  transfers between devices with their start and end apart: 6 -> 2, of which waited for: 4 -> 0; matrix products, arithmetic and copies ran while one was open for 1% -> 0% of each run, Pallas kernels for 30% -> 10%
where the time goes in v4:
time: 97.8 us; the launch traced here: 97.4 us
  blocking collectives  50.7 us (52%)
  Pallas kernels  37 us (38%)
  starting transfers between devices  6.45 us (7%)
  local copies, waits for them, and re-layouts  2.02 us (2%)
  other arithmetic  1.11 us (1%)
    all_to_all x2, blocking collectives, exchange(): return lax.all_to_all(x, 'strip', split_axis=0, concat_axis=0, tiled=True)  50.7 us
    pallas_call x1, Pallas kernels, on_device(): call(functools.partial(sides_kernel, frame_len, total), 2 * D * D * 20 *...  18.2 us
    pallas_call x1, Pallas kernels, on_device(): call(functools.partial(middle_kernel, frame_len, total), 2 * D * D * 10 *...  9.97 us
    pallas_call x1, Pallas kernels, on_device(): call(functools.partial(time_kernel, frame_len, local_rows, devices), 2 *...  8.88 us
    ppermute x1, starting transfers between devices, on_device(): before = lax.ppermute(frame_tokens[local_rows - CHUNK:], 'strip', up)  4.52 us
  transfers between devices with their start and end apart: 2, of which 0 were waited for; matrix products, arithmetic and copies ran while one was open for 0% of the time, Pallas kernels for 10%

profile of v4, /device:TPU:1, one launch (start us, length us, event | category | flops | bytes accessed | tf_op | source)
XLA Modules:
  0.0 97.4 jit_solution(2409744372715512399)
XLA Ops:
  0.0 1.2 %fusion.1 = (bf16[256,768]{1,0:T(8,128)(2,1)S(1)}, bf16[256,768]{1,0:T(8,128)(2,1)S(1)}) fusion(bf16[512,768]{1,0:T(8,128)(2,1)} %x_hbm.3), kind=kLoop, calls=%fused_computation.2 | loop fusion | bytes 1572864 | tf_op jit(solution)/shard_map/slice | solution.py:495
  1.2 1.9 %collective-permute-start.1 = (bf16[256,768]{1,0:T(8,128)(2,1)S(1)}, bf16[256,768]{1,0:T(8,128)(2,1)S(1)}, u32[]{:S(2)}, u32[]{:S(2)}) collective-permute-start(bf16[256,768]{1,0:T(8,128)(2,1)S(1)} %get-tuple-element.15), channel_id=1, source_target_pairs={{1,0},{2,1},{3,2},{4,3},{5,4},{6,5},{7,6},{8,7},{9,8},{10,9},{11,1... | collective-permute-start | bytes 1179656 | tf_op jit(solution)/shard_map/ppermute | solution.py:495
  3.1 4.5 %collective-permute-start = (bf16[256,768]{1,0:T(8,128)(2,1)S(1)}, bf16[256,768]{1,0:T(8,128)(2,1)S(1)}, u32[]{:S(2)}, u32[]{:S(2)}) collective-permute-start(bf16[256,768]{1,0:T(8,128)(2,1)S(1)} %get-tuple-element.16), channel_id=1, source_target_pairs={{0,1},{1,2},{2,3},{3,4},{4,5},{5,6},{6,7},{7,8},{8,9},{9,10},{10,1... | collective-permute-start | bytes 1179656 | tf_op jit(solution)/shard_map/ppermute | solution.py:494
  7.6 10.0 %shard_map.91 = (bf16[512,2304]{1,0:T(8,128)(2,1)}, bf16[256,768]{1,0:T(8,128)(2,1)}, bf16[256,2304]{1,0:T(8,128)(2,1)}) custom-call(s32[16]{0:T(128)} %reach_ref.3, s32[16]{0:T(128)} %count_ref.5, s32[1]{0:T(128)} %bitcast.index_ref, f32[768]{0:T(1024)} %gain_ref.3, bf16[512,768]{1,0:T(8,128)(2,1)} %x_hbm.3, bf16[768,2304]{1,0:T(8,128)(2,1)} %project_hbm.4, ...), custom_call_target="tpu_custom_call" | custom-call | flops 3019898880 | bytes 9437184 | tf_op jit(solution)/shard_map/pallas_call | solution.py:497
  17.6 0.0 collective-permute-done.1.after_hbm
  17.6 0.0 copy-start.1
  17.6 0.0 collective-permute-done.before_hbm
  17.6 0.0 copy-start.2
  17.7 0.7 copy-done.1
  18.4 0.1 copy-done.2
  18.5 18.2 %shard_map.92 = (bf16[512,768]{1,0:T(8,128)(2,1)}, bf16[512,768]{1,0:T(8,128)(2,1)}) custom-call(s32[16]{0:T(128)} %reach_ref.3, s32[16]{0:T(128)} %count_ref.5, s32[1]{0:T(128)} %bitcast.index_ref, f32[768]{0:T(1024)} %gain_ref.3, f32[768]{0:T(1024)} %time_gain_ref.1, bf16[256,768]{1,0:T(8,128)(2,1)} %copy-done.2, bf16[256,768]{1,0:T(8,128)(2,1)} %copy-done.1, ...), custom_call_target="tpu_custom_call" | custom-call | flops 6039797760 | bytes 9437184 | tf_op jit(solution)/shard_map/pallas_call | solution.py:517
  36.7 26.5 %all_to_all.15.x_hbm = bf16[16,32,768]{2,1,0:T(8,128)(2,1)} all-to-all(bf16[16,32,768]{2,1,0:T(8,128)(2,1)} %bitcast.5), channel_id=1, replica_groups=mesh['group'=2,'strip'=16] {'strip'}, dimensions={0} | all-to-all | bytes 1572864 | tf_op jit(solution)/shard_map/all_to_all | solution.py:556
  63.2 8.9 %shard_map.93 = bf16[16,32,768]{2,1,0:T(8,128)(2,1)} custom-call(s32[16]{0:T(128)} %count_ref.5, s32[1]{0:T(128)} %bitcast.index_ref, bf16[16,32,768]{2,1,0:T(8,128)(2,1)} %all_to_all.15.x_hbm, bf16[768,2304]{1,0:T(8,128)(2,1)} %project_hbm.5, bf16[768,768]{1,0:T(8,128)(2,1)} %output_hbm.5), custom_call_target="tpu_custom_call" | custom-call | flops 3019898880 | bytes 9437184 | tf_op jit(solution)/shard_map/pallas_call | solution.py:559
  72.1 0.0 copy-start
  72.1 24.2 %all_to_all.16 = bf16[16,32,768]{2,1,0:T(8,128)(2,1)S(1)} all-to-all(bf16[16,32,768]{2,1,0:T(8,128)(2,1)} %shard_map.93), channel_id=1, replica_groups=mesh['group'=2,'strip'=16] {'strip'}, dimensions={0} | all-to-all | bytes 1572864 | tf_op jit(solution)/shard_map/all_to_all | solution.py:556
  96.3 0.0 copy-done
  96.3 1.1 %fusion = bf16[512,768]{1,0:T(8,128)(2,1)} fusion(bf16[512,768]{1,0:T(8,128)(2,1)S(1)} %copy-done, bf16[16,32,768]{2,1,0:T(8,128)(2,1)S(1)} %all_to_all.16), kind=kLoop, calls=%fused_computation.1 | loop fusion | flops 1572864 | bytes 2359296 | tf_op jit(solution)/shard_map/convert_element_type | solution.py:578
Async XLA Ops:
  1.2 16.5 %collective-permute-start.1 = (bf16[256,768]{1,0:T(8,128)(2,1)S(1)}, bf16[256,768]{1,0:T(8,128)(2,1)S(1)}, u32[]{:S(2)}, u32[]{:S(2)}) collective-permute-start(bf16[256,768]{1,0:T(8,128)(2,1)S(1)} %get-tuple-element.15), channel_id=1, source_target_pairs={{1,0},{2,1},{3,2},{4,3},{5,4},{6,5},{7,6},{8,7},{9,8},{10,9},{11,1... | collective-permute-start | bytes 1179656 | tf_op jit(solution)/shard_map/ppermute | solution.py:495
  3.1 14.5 %collective-permute-start = (bf16[256,768]{1,0:T(8,128)(2,1)S(1)}, bf16[256,768]{1,0:T(8,128)(2,1)S(1)}, u32[]{:S(2)}, u32[]{:S(2)}) collective-permute-start(bf16[256,768]{1,0:T(8,128)(2,1)S(1)} %get-tuple-element.16), channel_id=1, source_target_pairs={{0,1},{1,2},{2,3},{3,4},{4,5},{5,6},{6,7},{7,8},{8,9},{9,10},{10,1... | collective-permute-start | bytes 1179656 | tf_op jit(solution)/shard_map/ppermute | solution.py:494
  17.6 0.8 copy-start.1
  17.6 0.9 copy-start.2
  72.1 24.2 %copy-start = (bf16[512,768]{1,0:T(8,128)(2,1)S(1)}, bf16[512,768]{1,0:T(8,128)(2,1)}, u32[]{:S(2)}) copy-start(bf16[512,768]{1,0:T(8,128)(2,1)} %get-tuple-element.13) | copy-start | bytes 2359300

commit v5 on v4

--- a/solution.py
+++ b/solution.py
@@ -17,7 +17,7 @@
 WIN = 3 * BLK
 PAIR = 2 * HD
 CHUNK = 2 * BLK
-VMEM_LIMIT = 60 * 1024 * 1024
+MIB = 1 << 20
 EPS = 1e-06
 MASKED = -1e30
 
@@ -210,21 +210,17 @@
     index_ref,
     gain_ref,
     time_gain_ref,
-    before_hbm,
-    after_hbm,
-    x_hbm,
-    first_hbm,
-    middle_hbm,
-    second_hbm,
-    project_hbm,
-    output_hbm,
+    before_ref,
+    after_ref,
+    x_ref,
+    first_ref,
+    middle_ref,
+    second_ref,
+    project_ref,
+    output_ref,
     state_ref,
     hidden_ref,
-    halo_s,
     edge_s,
-    middle_s,
-    project_s,
-    output_s,
     q_s,
     k_s,
     v_s,
@@ -237,7 +233,7 @@
     expon_s,
     in_sems,
 ):
-    rows = x_hbm.shape[0]
+    rows = x_ref.shape[0]
     offset = index_ref[0] * rows
     gain = gain_ref[...]
     half = 2 * BLK
@@ -245,57 +241,31 @@
     def block(first, last=None):
         return slice(first * BLK, (first + 1 if last is None else last) * BLK)
 
-    (
-        before_in,
-        after_in,
-        key_in,
-        value_in,
-        query_in,
-        k_in,
-        v_in,
-        q_low_in,
-        q_high_in,
-        output_in,
-        x_low_in,
-        x_high_in,
-        k2_in,
-        v2_in,
-        q2_in,
-        middle_in,
-    ) = copies(
+    moved = copies(
         in_sems,
-        (before_hbm, halo_s.at[block(0, 2)]),
-        (after_hbm, halo_s.at[block(2, 4)]),
-        (project_hbm.at[:, KEY], project_s.at[:, KEY]),
-        (project_hbm.at[:, VALUE], project_s.at[:, VALUE]),
-        (project_hbm.at[:, QUERY], project_s.at[:, QUERY]),
-        (first_hbm.at[:, KEY], k_s.at[block(2, 6)]),
-        (first_hbm.at[:, VALUE], v_s.at[block(2, 6)]),
-        (first_hbm.at[block(0), QUERY], q_s.at[block(1)]),
-        (first_hbm.at[block(3), QUERY], q_s.at[block(2)]),
-        (output_hbm, output_s),
-        (x_hbm.at[block(0)], edge_s.at[block(1)]),
-        (x_hbm.at[block(3)], edge_s.at[block(2)]),
-        (second_hbm.at[:, KEY], k2_s.at[block(2, 4)]),
-        (second_hbm.at[:, VALUE], v2_s.at[block(2, 4)]),
-        (second_hbm.at[:, QUERY], q2_s.at[block(1, 3)]),
-        (middle_hbm, middle_s),
+        (first_ref.at[:, KEY], k_s.at[block(2, 6)]),
+        (first_ref.at[:, VALUE], v_s.at[block(2, 6)]),
+        (first_ref.at[block(0), QUERY], q_s.at[block(1)]),
+        (first_ref.at[block(3), QUERY], q_s.at[block(2)]),
+    )
+    moved2 = copies(
+        in_sems.at[4:7],
+        (second_ref.at[:, KEY], k2_s.at[block(2, 4)]),
+        (second_ref.at[:, VALUE], v2_s.at[block(2, 4)]),
+        (second_ref.at[:, QUERY], q2_s.at[block(1, 3)]),
     )
     tables = (reach_ref, count_ref, frame_len, total)
     work = (mixed_s, bias_s, scores_s, expon_s)
-    before_in.wait()
-    after_in.wait()
-    hidden = norm_rows(halo_s[...], gain)
-    for copy, cols, ref in ((key_in, KEY, k_s), (value_in, VALUE, v_s)):
-        copy.wait()
-        made = times(hidden, project_s[:, cols]).astype(BF16)
+    halo = jnp.concatenate([before_ref[...], after_ref[...]], axis=0)
+    hidden = norm_rows(halo, gain)
+    for cols, ref in ((KEY, k_s), (VALUE, v_s)):
+        made = times(hidden, project_ref[:, cols]).astype(BF16)
         ref[block(0, 2)] = made[:half]
         ref[block(6, 8)] = made[half:]
-    query_in.wait()
-    made = times(hidden[block(1, 3)], project_s[:, QUERY]).astype(BF16)
+    made = times(hidden[block(1, 3)], project_ref[:, QUERY]).astype(BF16)
     q_s[block(0)] = made[:BLK]
     q_s[block(3)] = made[BLK:]
-    for copy in (k_in, v_in, q_low_in, q_high_in):
+    for copy in moved:
         copy.wait()
 
     def skip(i):
@@ -311,23 +281,21 @@
         (v_s, 0, 0),
         *work,
     )
-    output_in.wait()
-    x_low_in.wait()
-    x_high_in.wait()
-    update = times(mixed_s[...], output_s[...])
-    edge_s[block(0)] = (halo_s[block(1)].astype(F32) + update[block(0)]).astype(BF16)
-    edge_s[block(1, 3)] = (edge_s[block(1, 3)].astype(F32) + update[block(1, 3)]).astype(BF16)
-    edge_s[block(3)] = (halo_s[block(2)].astype(F32) + update[block(3)]).astype(BF16)
+    update = times(mixed_s[...], output_ref[...])
+    edge_s[block(0)] = (before_ref[block(1)].astype(F32) + update[block(0)]).astype(BF16)
+    edge_s[block(1)] = (x_ref[block(0)].astype(F32) + update[block(1)]).astype(BF16)
+    edge_s[block(2)] = (x_ref[block(3)].astype(F32) + update[block(2)]).astype(BF16)
+    edge_s[block(3)] = (after_ref[block(0)].astype(F32) + update[block(3)]).astype(BF16)
 
     hidden = norm_rows(edge_s[...], gain)
     for cols, ref in ((KEY, k2_s), (VALUE, v2_s)):
-        made = times(hidden, project_s[:, cols]).astype(BF16)
+        made = times(hidden, project_ref[:, cols]).astype(BF16)
         ref[block(0, 2)] = made[:half]
         ref[block(4, 6)] = made[half:]
-    made = times(hidden[block(1, 3)], project_s[:, QUERY]).astype(BF16)
+    made = times(hidden[block(1, 3)], project_ref[:, QUERY]).astype(BF16)
     q2_s[block(0)] = made[:BLK]
     q2_s[block(3)] = made[BLK:]
-    for copy in (k2_in, v2_in, q2_in):
+    for copy in moved2:
         copy.wait()
     space_attention(
         4,
@@ -339,10 +307,9 @@
         (v2_s, 0, 0),
         *work,
     )
-    middle_in.wait()
-    update = times(mixed_s[...], output_s[...])
+    update = times(mixed_s[...], output_ref[...])
     state_ref[block(0)] = (edge_s[block(1)].astype(F32) + update[block(0)]).astype(BF16)
-    state_ref[block(1, 3)] = (middle_s[...].astype(F32) + update[block(1, 3)]).astype(BF16)
+    state_ref[block(1, 3)] = (middle_ref[...].astype(F32) + update[block(1, 3)]).astype(BF16)
     state_ref[block(3)] = (edge_s[block(2)].astype(F32) + update[block(3)]).astype(BF16)
     hidden_ref[...] = norm_rows(state_ref[...], time_gain_ref[...])
 
@@ -353,33 +320,20 @@
     devices,
     count_ref,
     index_ref,
-    x_hbm,
-    project_hbm,
-    output_hbm,
-    update_hbm,
-    x_s,
-    project_s,
-    output_s,
+    x_ref,
+    project_ref,
+    output_ref,
+    update_ref,
     qkv_s,
-    update_s,
     mixed_s,
     bias_s,
     scores_s,
     expon_s,
-    in_sems,
-    out_sems,
 ):
-    groups, _, group, _ = x_s.shape
+    groups = bias_s.shape[0]
+    group = x_ref.shape[1] // groups
     rows = F * group
     piece = local_rows // devices
-    *x_in, query_in, key_in, value_in, output_in = copies(
-        in_sems,
-        *[(x_hbm.at[:, g * group : (g + 1) * group], x_s.at[g]) for g in range(groups)],
-        (project_hbm.at[:, QUERY], project_s.at[:, QUERY]),
-        (project_hbm.at[:, KEY], project_s.at[:, KEY]),
-        (project_hbm.at[:, VALUE], project_s.at[:, VALUE]),
-        (output_hbm, output_s),
-    )
     row = lax.broadcasted_iota(jnp.int32, (rows, rows), 0)
     col = lax.broadcasted_iota(jnp.int32, (rows, rows), 1)
     key = lax.broadcasted_iota(jnp.int32, (1, rows), 1)
@@ -393,13 +347,11 @@
         living = jnp.where(place >= least, 1, 0)
         bias_s[g] = jnp.where(same & ((living == 1) | (row == col)), 0.0, MASKED).astype(F32)
 
-    for copy in x_in:
-        copy.wait()
-    x = x_s[...].reshape(groups * rows, D)
-    for copy, cols in ((query_in, QUERY), (key_in, KEY), (value_in, VALUE)):
-        copy.wait()
-        qkv_s[:, cols] = times(x, project_s[:, cols]).astype(BF16)
-    output_in.wait()
+    x = jnp.concatenate(
+        [x_ref[:, g * group : (g + 1) * group].reshape(rows, D) for g in range(groups)], axis=0
+    )
+    for cols in (QUERY, KEY, VALUE):
+        qkv_s[:, cols] = times(x, project_ref[:, cols]).astype(BF16)
 
     for g in range(groups):
         part = slice(g * rows, (g + 1) * rows)
@@ -411,16 +363,10 @@
             mixed_s[part, lanes] = mixed
 
         attention(columns(0), columns(D), columns(2 * D), store, bias_s.at[g], scores_s, expon_s)
-    out = []
+    update = times(mixed_s[...], output_ref[...]).astype(BF16)
     for g in range(groups):
-        part = slice(g * rows, (g + 1) * rows)
-        update = times(mixed_s[part], output_s[...]).astype(BF16)
-        update_s[g] = update.reshape(F, group, D)
-        out += copies(
-            out_sems.at[g : g + 1], (update_s.at[g], update_hbm.at[:, g * group : (g + 1) * group])
-        )
-    for copy in out:
-        copy.wait()
+        part = update[g * rows : (g + 1) * rows].reshape(F, group, D)
+        update_ref[:, g * group : (g + 1) * group] = part
 
 
 def smem():
@@ -456,10 +402,10 @@
     return pltpu.SemaphoreType.DMA((count,))
 
 
-def call(kernel, flops, exps, **rest):
+def call(kernel, flops, exps, limit, **rest):
     return pl.pallas_call(
         kernel,
-        compiler_params=pltpu.CompilerParams(vmem_limit_bytes=VMEM_LIMIT),
+        compiler_params=pltpu.CompilerParams(vmem_limit_bytes=limit),
         cost_estimate=pl.CostEstimate(
             flops=flops, bytes_accessed=16 * D * D, transcendentals=exps
         ),
@@ -498,6 +444,7 @@
         functools.partial(middle_kernel, frame_len, total),
         2 * D * D * 10 * CHUNK,
         H * CHUNK * WIN,
+        40 * MIB,
         out_shape=(rows16(local_rows, 3 * D), rows16(CHUNK, D), rows16(CHUNK, 3 * D)),
         in_specs=[smem()] * 3 + [vmem()] + [hbm()] * 3,
         out_specs=(hbm(),) * 3,
@@ -512,21 +459,26 @@
             sems(5),
             sems(3),
         ],
-    )(window_reach, valid_count, index, space_gain, frame_tokens, space_project, space_output)
+    )(
+        window_reach,
+        valid_count,
+        index,
+        space_gain,
+        frame_tokens,
+        pltpu.with_memory_space_constraint(space_project, pltpu.HBM),
+        pltpu.with_memory_space_constraint(space_output, pltpu.HBM),
+    )
 
     state, hidden = call(
         functools.partial(sides_kernel, frame_len, total),
         2 * D * D * 20 * CHUNK,
         4 * H * CHUNK * WIN,
+        26 * MIB,
         out_shape=(rows16(local_rows, D),) * 2,
-        in_specs=[smem()] * 3 + [vmem()] * 2 + [hbm()] * 8,
+        in_specs=[smem()] * 3 + [vmem()] * 5 + [hbm()] + [vmem()] * 4,
         out_specs=(vmem(),) * 2,
         scratch_shapes=[
             scratch(local_rows, D),
-            scratch(local_rows, D),
-            scratch(CHUNK, D),
-            scratch(D, 3 * D),
-            scratch(D, D),
             scratch(local_rows, D),
             scratch(local_rows + 2 * CHUNK, D),
             scratch(local_rows + 2 * CHUNK, D),
@@ -534,7 +486,7 @@
             scratch(local_rows + CHUNK, D),
             scratch(local_rows + CHUNK, D),
             *work(local_rows, BLK, WIN),
-            sems(16),
+            sems(7),
         ],
     )(
         window_reach,
@@ -560,18 +512,13 @@
         functools.partial(time_kernel, frame_len, local_rows, devices),
         2 * D * D * 10 * CHUNK,
         2 * H * CHUNK * CHUNK,
+        30 * MIB,
         out_shape=jax.ShapeDtypeStruct((F, slots, D), BF16),
-        in_specs=[smem()] * 2 + [hbm()] * 3,
-        out_specs=hbm(),
+        in_specs=[smem()] * 2 + [vmem()] * 3,
+        out_specs=vmem(),
         scratch_shapes=[
-            pltpu.VMEM((groups, F, group, D), BF16),
-            scratch(D, 3 * D),
-            scratch(D, D),
             scratch(local_rows, 3 * D),
-            pltpu.VMEM((groups, F, group, D), BF16),
             *work(local_rows, F * group, F * group, (groups,)),
-            sems(4 + groups),
-            sems(groups),
         ],
     )(valid_count, index, gathered, time_project, time_output)
     returned = exchange(update.reshape(local_rows, D))

time: 97.8 us -> 89.3 us (0.913)
  Pallas kernels: 37 us -> 29.8 us
    pallas_call x1, Pallas kernels: 8.88 us -> 5.29 us  [on_device(): call(functools.partial(time_kernel, frame_len, local_rows, devices), 2 *...]
    pallas_call x1, Pallas kernels: 18.2 us -> 15 us  [on_device(): call(functools.partial(sides_kernel, frame_len, total), 2 * D * D * 20 *...]
  transfers between devices with their start and end apart: 2 -> 2, of which waited for: 0 -> 0; matrix products, arithmetic and copies ran while one was open for 0% -> 0% of each run, Pallas kernels for 10% -> 11%
where the time goes in v5:
time: 89.3 us; the launch traced here: 89.1 us
  blocking collectives  50.2 us (56%)
  Pallas kernels  29.8 us (33%)
  starting transfers between devices  6.45 us (7%)
  local copies, waits for them, and re-layouts  1.28 us (1%)
  other arithmetic  1.16 us (1%)
    all_to_all x2, blocking collectives, exchange(): return lax.all_to_all(x, 'strip', split_axis=0, concat_axis=0, tiled=True)  50.2 us
    pallas_call x1, Pallas kernels, on_device(): call(functools.partial(sides_kernel, frame_len, total), 2 * D * D * 20 *...  15 us
    pallas_call x1, Pallas kernels, on_device(): call(functools.partial(middle_kernel, frame_len, total), 2 * D * D * 10 *...  9.55 us
    pallas_call x1, Pallas kernels, on_device(): call(functools.partial(time_kernel, frame_len, local_rows, devices), 2 *...  5.29 us
    ppermute x1, starting transfers between devices, on_device(): before = lax.ppermute(frame_tokens[local_rows - CHUNK:], 'strip', up)  4.53 us
    ppermute x1, starting transfers between devices, on_device(): after = lax.ppermute(frame_tokens[:CHUNK], 'strip', down)  1.92 us
  transfers between devices with their start and end apart: 2, of which 0 were waited for; matrix products, arithmetic and copies ran while one was open for 0% of the time, Pallas kernels for 11%

profile of v5, /device:TPU:1, one launch (start us, length us, event | category | flops | bytes accessed | tf_op | source)
XLA Modules:
  0.0 89.1 jit_solution(9250954307821851186)
XLA Ops:
  0.0 0.0 copy-start
  0.0 0.0 copy-start.8
  0.0 0.0 copy-start.5
  0.0 0.0 copy-start.7
  0.0 1.2 %fusion.1 = (bf16[256,768]{1,0:T(8,128)(2,1)S(1)}, bf16[256,768]{1,0:T(8,128)(2,1)S(1)}) fusion(bf16[512,768]{1,0:T(8,128)(2,1)} %x_ref.1), kind=kLoop, calls=%fused_computation.2 | loop fusion | bytes 1572864 | tf_op jit(solution)/shard_map/slice | solution.py:441
  1.3 1.9 %collective-permute-start.1 = (bf16[256,768]{1,0:T(8,128)(2,1)S(1)}, bf16[256,768]{1,0:T(8,128)(2,1)S(1)}, u32[]{:S(2)}, u32[]{:S(2)}) collective-permute-start(bf16[256,768]{1,0:T(8,128)(2,1)S(1)} %get-tuple-element.15), channel_id=1, source_target_pairs={{1,0},{2,1},{3,2},{4,3},{5,4},{6,5},{7,6},{8,7},{9,8},{10,9},{11,1... | collective-permute-start | bytes 1179656 | tf_op jit(solution)/shard_map/ppermute | solution.py:441
  3.2 4.5 %collective-permute-start = (bf16[256,768]{1,0:T(8,128)(2,1)S(1)}, bf16[256,768]{1,0:T(8,128)(2,1)S(1)}, u32[]{:S(2)}, u32[]{:S(2)}) collective-permute-start(bf16[256,768]{1,0:T(8,128)(2,1)S(1)} %get-tuple-element.16), channel_id=1, source_target_pairs={{0,1},{1,2},{2,3},{3,4},{4,5},{5,6},{6,7},{7,8},{8,9},{9,10},{10,1... | collective-permute-start | bytes 1179656 | tf_op jit(solution)/shard_map/ppermute | solution.py:440
  7.7 0.0 copy-done
  7.7 0.0 copy-done.8
  7.7 0.0 copy-done.5
  7.8 0.0 copy-done.7
  7.8 0.0 copy-start.1
  7.8 0.0 copy-start.3
  7.8 0.0 copy-start.6
  7.8 9.5 %shard_map.91 = (bf16[512,2304]{1,0:T(8,128)(2,1)S(1)}, bf16[256,768]{1,0:T(8,128)(2,1)S(1)}, bf16[256,2304]{1,0:T(8,128)(2,1)S(1)}) custom-call(s32[16]{0:T(128)S(1)} %copy-done.7, s32[16]{0:T(128)S(1)} %copy-done.8, s32[1]{0:T(128)} %bitcast.index_ref, f32[768]{0:T(1024)S(1)} %copy-done.5, bf16[512,768]{1,0:T(8,128)(2,1)S(1)} %copy-done, ...), custom_call_target="tpu_custom_call" | custom-call | flops 3019898880 | bytes 9437184 | tf_op jit(solution)/shard_map/pallas_call | solution.py:443
  17.4 0.0 collective-permute-done.1.after_ref
  17.4 0.0 collective-permute-done.before_ref
  17.4 0.0 copy-done.1
  17.4 0.0 copy-done.3
  17.4 0.0 copy-done.6
  17.4 0.0 copy-start.2
  17.4 15.0 %shard_map.92 = (bf16[512,768]{1,0:T(8,128)(2,1)S(1)}, bf16[512,768]{1,0:T(8,128)(2,1)S(1)}) custom-call(s32[16]{0:T(128)S(1)} %copy-done.7, s32[16]{0:T(128)S(1)} %copy-done.8, s32[1]{0:T(128)} %bitcast.index_ref, f32[768]{0:T(1024)S(1)} %copy-done.5, f32[768]{0:T(1024)S(1)} %copy-done.6, bf16[256,768]{1,0:T(8,128)(2,1)S(1)} %collective-permute-done.before_ref, ...), custom_call_target="tpu_custom_call" | custom-call | flops 6039797760 | bytes 9437184 | tf_op jit(solution)/shard_map/pallas_call | solution.py:472
  32.4 0.0 copy-start.4
  32.4 26.3 %all_to_all.15.x_ref = bf16[16,32,768]{2,1,0:T(8,128)(2,1)S(1)} all-to-all(bf16[16,32,768]{2,1,0:T(8,128)(2,1)S(1)} %bitcast.5), channel_id=1, replica_groups=mesh['group'=2,'strip'=16] {'strip'}, dimensions={0} | all-to-all | bytes 1572864 | tf_op jit(solution)/shard_map/all_to_all | solution.py:508
  58.8 0.0 copy-done.2
  58.8 0.0 copy-done.4
  58.8 5.3 %shard_map.93 = bf16[16,32,768]{2,1,0:T(8,128)(2,1)S(1)} custom-call(s32[16]{0:T(128)S(1)} %copy-done.8, s32[1]{0:T(128)} %bitcast.index_ref, bf16[16,32,768]{2,1,0:T(8,128)(2,1)S(1)} %all_to_all.15.x_ref, bf16[768,2304]{1,0:T(8,128)(2,1)S(1)} %copy-done.2, bf16[768,768]{1,0:T(8,128)(2,1)S(1)} %copy-done.4), custom_call_target="tpu_custom_call" | custom-call | flops 3019898880 | bytes 9437184 | tf_op jit(solution)/shard_map/pallas_call | solution.py:511
  64.1 23.9 %all_to_all.16 = bf16[16,32,768]{2,1,0:T(8,128)(2,1)S(1)} all-to-all(bf16[16,32,768]{2,1,0:T(8,128)(2,1)S(1)} %shard_map.93), channel_id=1, replica_groups=mesh['group'=2,'strip'=16] {'strip'}, dimensions={0} | all-to-all | bytes 1572864 | tf_op jit(solution)/shard_map/all_to_all | solution.py:508
  87.9 1.2 %fusion = bf16[512,768]{1,0:T(8,128)(2,1)} fusion(bf16[512,768]{1,0:T(8,128)(2,1)S(1)} %get-tuple-element.13, bf16[16,32,768]{2,1,0:T(8,128)(2,1)S(1)} %all_to_all.16), kind=kLoop, calls=%fused_computation.1 | loop fusion | flops 1572864 | bytes 2359296 | tf_op jit(solution)/shard_map/convert_element_type | solution.py:525
Async XLA Ops:
  0.0 7.7 %copy-start = (bf16[512,768]{1,0:T(8,128)(2,1)S(1)}, bf16[512,768]{1,0:T(8,128)(2,1)}, u32[]{:S(2)}) copy-start(bf16[512,768]{1,0:T(8,128)(2,1)} %x_ref.1) | copy-start | bytes 2359300
  0.0 7.7 %copy-start.8 = (s32[16]{0:T(128)S(1)}, s32[16]{0:T(128)}, u32[]{:S(2)}) copy-start(s32[16]{0:T(128)} %count_ref.5) | copy-start | bytes 196
  0.0 7.7 %copy-start.5 = (f32[768]{0:T(1024)S(1)}, f32[768]{0:T(1024)}, u32[]{:S(2)}) copy-start(f32[768]{0:T(1024)} %gain_ref.3) | copy-start | bytes 9220
  0.0 7.7 %copy-start.7 = (s32[16]{0:T(128)S(1)}, s32[16]{0:T(128)}, u32[]{:S(2)}) copy-start(s32[16]{0:T(128)} %reach_ref.3) | copy-start | bytes 196
  1.3 16.1 %collective-permute-start.1 = (bf16[256,768]{1,0:T(8,128)(2,1)S(1)}, bf16[256,768]{1,0:T(8,128)(2,1)S(1)}, u32[]{:S(2)}, u32[]{:S(2)}) collective-permute-start(bf16[256,768]{1,0:T(8,128)(2,1)S(1)} %get-tuple-element.15), channel_id=1, source_target_pairs={{1,0},{2,1},{3,2},{4,3},{5,4},{6,5},{7,6},{8,7},{9,8},{10,9},{11,1... | collective-permute-start | bytes 1179656 | tf_op jit(solution)/shard_map/ppermute | solution.py:441
  3.2 14.2 %collective-permute-start = (bf16[256,768]{1,0:T(8,128)(2,1)S(1)}, bf16[256,768]{1,0:T(8,128)(2,1)S(1)}, u32[]{:S(2)}, u32[]{:S(2)}) collective-permute-start(bf16[256,768]{1,0:T(8,128)(2,1)S(1)} %get-tuple-element.16), channel_id=1, source_target_pairs={{0,1},{1,2},{2,3},{3,4},{4,5},{5,6},{6,7},{7,8},{8,9},{9,10},{10,1... | collective-permute-start | bytes 1179656 | tf_op jit(solution)/shard_map/ppermute | solution.py:440
  7.8 9.6 %copy-start.1 = (bf16[768,2304]{1,0:T(8,128)(2,1)S(1)}, bf16[768,2304]{1,0:T(8,128)(2,1)}, u32[]{:S(2)}) copy-start(bf16[768,2304]{1,0:T(8,128)(2,1)} %project_ref.2) | copy-start | bytes 10616836
  7.8 9.6 %copy-start.3 = (bf16[768,768]{1,0:T(8,128)(2,1)S(1)}, bf16[768,768]{1,0:T(8,128)(2,1)}, u32[]{:S(2)}) copy-start(bf16[768,768]{1,0:T(8,128)(2,1)} %output_ref.2) | copy-start | bytes 3538948
  7.8 9.6 %copy-start.6 = (f32[768]{0:T(1024)S(1)}, f32[768]{0:T(1024)}, u32[]{:S(2)}) copy-start(f32[768]{0:T(1024)} %time_gain_ref.1) | copy-start | bytes 9220
  17.4 41.4 %copy-start.2 = (bf16[768,2304]{1,0:T(8,128)(2,1)S(1)}, bf16[768,2304]{1,0:T(8,128)(2,1)}, u32[]{:S(2)}) copy-start(bf16[768,2304]{1,0:T(8,128)(2,1)} %project_ref.3) | copy-start | bytes 10616836
  32.4 26.4 %copy-start.4 = (bf16[768,768]{1,0:T(8,128)(2,1)S(1)}, bf16[768,768]{1,0:T(8,128)(2,1)}, u32[]{:S(2)}) copy-start(bf16[768,768]{1,0:T(8,128)(2,1)} %output_ref.3) | copy-start | bytes 3538948

commit v6 on v5

--- a/solution.py
+++ b/solution.py
@@ -112,7 +112,7 @@
         )
         return carry
 
-    lax.fori_loop(0, blocks, one_block, 0)
+    lax.fori_loop(0, blocks, one_block, 0, unroll=True)
 
 
 def times(x, weight):
@@ -136,13 +136,12 @@
     count_ref,
     index_ref,
     gain_ref,
-    x_hbm,
+    x_ref,
     project_hbm,
     output_hbm,
     first_hbm,
     state_hbm,
     second_hbm,
-    x_s,
     project_s,
     output_s,
     first_s,
@@ -155,20 +154,18 @@
     in_sems,
     out_sems,
 ):
-    rows = x_s.shape[0]
+    rows = x_ref.shape[0]
     offset = index_ref[0] * rows
     gain = gain_ref[...]
     inner = slice(BLK, rows - BLK)
-    x_in, query_in, key_in, value_in, output_in = copies(
+    query_in, key_in, value_in, output_in = copies(
         in_sems,
-        (x_hbm, x_s),
         (project_hbm.at[:, QUERY], project_s.at[:, QUERY]),
         (project_hbm.at[:, KEY], project_s.at[:, KEY]),
         (project_hbm.at[:, VALUE], project_s.at[:, VALUE]),
         (output_hbm, output_s),
     )
-    x_in.wait()
-    hidden = norm_rows(x_s[...], gain)
+    hidden = norm_rows(x_ref[...], gain)
     for copy, cols in ((query_in, QUERY), (key_in, KEY), (value_in, VALUE)):
         copy.wait()
         first_s[:, cols] = times(hidden, project_s[:, cols]).astype(BF16)
@@ -189,7 +186,7 @@
         expon_s,
     )
     output_in.wait()
-    state_s[...] = (x_s[inner].astype(F32) + times(mixed_s[...], output_s[...])).astype(BF16)
+    state_s[...] = (x_ref[inner].astype(F32) + times(mixed_s[...], output_s[...])).astype(BF16)
     state_out = pltpu.make_async_copy(state_s, state_hbm, out_sems.at[1])
     state_out.start()
     hidden = norm_rows(state_s[...], gain)
@@ -440,23 +437,26 @@
     before = lax.ppermute(frame_tokens[local_rows - CHUNK :], "strip", up)
     after = lax.ppermute(frame_tokens[:CHUNK], "strip", down)
 
-    first, middle, second = call(
+    first, middle, second, project, output = call(
         functools.partial(middle_kernel, frame_len, total),
         2 * D * D * 10 * CHUNK,
         H * CHUNK * WIN,
         40 * MIB,
-        out_shape=(rows16(local_rows, 3 * D), rows16(CHUNK, D), rows16(CHUNK, 3 * D)),
-        in_specs=[smem()] * 3 + [vmem()] + [hbm()] * 3,
-        out_specs=(hbm(),) * 3,
+        out_shape=(
+            rows16(local_rows, 3 * D),
+            rows16(CHUNK, D),
+            rows16(CHUNK, 3 * D),
+            rows16(D, 3 * D),
+            rows16(D, D),
+        ),
+        in_specs=[smem()] * 3 + [vmem()] * 2 + [hbm()] * 2,
+        out_specs=(hbm(),) * 3 + (vmem(),) * 2,
         scratch_shapes=[
-            scratch(local_rows, D),
-            scratch(D, 3 * D),
-            scratch(D, D),
             scratch(local_rows, 3 * D),
             scratch(CHUNK, D),
             scratch(CHUNK, 3 * D),
             *work(CHUNK, BLK, WIN),
-            sems(5),
+            sems(4),
             sems(3),
         ],
     )(
@@ -500,8 +500,8 @@
         first,
         middle,
         second,
-        space_project,
-        space_output,
+        project,
+        output,
     )
 
     def exchange(x):

time: 89.3 us -> 88 us (0.985)
  Pallas kernels: 29.8 us -> 28.5 us
    pallas_call x1, Pallas kernels: 15 us -> 14 us  [on_device(): call(functools.partial(sides_kernel, frame_len, total), 2 * D * D * 20 *...]
where the time goes in v6:
time: 88 us; the launch traced here: 87.7 us
  blocking collectives  50.2 us (57%)
  Pallas kernels  28.5 us (32%)
  starting transfers between devices  6.45 us (7%)
  local copies, waits for them, and re-layouts  1.27 us (1%)
  other arithmetic  1.16 us (1%)
    all_to_all x2, blocking collectives, exchange(): return lax.all_to_all(x, 'strip', split_axis=0, concat_axis=0, tiled=True)  50.2 us
    pallas_call x1, Pallas kernels, on_device(): call(functools.partial(sides_kernel, frame_len, total), 2 * D * D * 20 *...  14 us
    pallas_call x1, Pallas kernels, on_device(): call(functools.partial(middle_kernel, frame_len, total), 2 * D * D * 10 *...  9.27 us
    pallas_call x1, Pallas kernels, on_device(): call(functools.partial(time_kernel, frame_len, local_rows, devices), 2 *...  5.29 us
    ppermute x1, starting transfers between devices, on_device(): before = lax.ppermute(frame_tokens[local_rows - CHUNK:], 'strip', up)  4.53 us
    ppermute x1, starting transfers between devices, on_device(): after = lax.ppermute(frame_tokens[:CHUNK], 'strip', down)  1.92 us
  transfers between devices with their start and end apart: 2, of which 0 were waited for; matrix products, arithmetic and copies ran while one was open for 0% of the time, Pallas kernels for 11%

profile of v6, /device:TPU:1, one launch (start us, length us, event | category | flops | bytes accessed | tf_op | source)
XLA Modules:
  0.0 87.7 jit_solution(10272627157530384181)
XLA Ops:
  0.0 0.0 copy-start
  0.0 0.0 copy-start.6
  0.0 0.0 copy-start.3
  0.0 0.0 copy-start.5
  0.0 1.2 %fusion.1 = (bf16[256,768]{1,0:T(8,128)(2,1)S(1)}, bf16[256,768]{1,0:T(8,128)(2,1)S(1)}) fusion(bf16[512,768]{1,0:T(8,128)(2,1)} %x_ref.3), kind=kLoop, calls=%fused_computation.2 | loop fusion | bytes 1572864 | tf_op jit(solution)/shard_map/slice | solution.py:438
  1.3 1.9 %collective-permute-start.1 = (bf16[256,768]{1,0:T(8,128)(2,1)S(1)}, bf16[256,768]{1,0:T(8,128)(2,1)S(1)}, u32[]{:S(2)}, u32[]{:S(2)}) collective-permute-start(bf16[256,768]{1,0:T(8,128)(2,1)S(1)} %get-tuple-element.19), channel_id=1, source_target_pairs={{1,0},{2,1},{3,2},{4,3},{5,4},{6,5},{7,6},{8,7},{9,8},{10,9},{11,1... | collective-permute-start | bytes 1179656 | tf_op jit(solution)/shard_map/ppermute | solution.py:438
  3.2 4.5 %collective-permute-start = (bf16[256,768]{1,0:T(8,128)(2,1)S(1)}, bf16[256,768]{1,0:T(8,128)(2,1)S(1)}, u32[]{:S(2)}, u32[]{:S(2)}) collective-permute-start(bf16[256,768]{1,0:T(8,128)(2,1)S(1)} %get-tuple-element.20), channel_id=1, source_target_pairs={{0,1},{1,2},{2,3},{3,4},{4,5},{5,6},{6,7},{7,8},{8,9},{9,10},{10,1... | collective-permute-start | bytes 1179656 | tf_op jit(solution)/shard_map/ppermute | solution.py:437
  7.7 0.0 copy-done
  7.7 0.0 copy-done.6
  7.7 0.0 copy-done.3
  7.8 0.0 copy-done.5
  7.8 0.0 copy-start.4
  7.8 9.3 %shard_map.91 = (bf16[512,2304]{1,0:T(8,128)(2,1)S(1)}, bf16[256,768]{1,0:T(8,128)(2,1)S(1)}, bf16[256,2304]{1,0:T(8,128)(2,1)S(1)}, bf16[768,2304]{1,0:T(8,128)(2,1)S(1)}, bf16[768,768]{1,0:T(8,128)(2,1)S(1)}) custom-call(s32[16]{0:T(128)S(1)} %copy-done.5, s32[16]{0:T(128)S(1)} %copy-done.6, s32[1]{0:T(128)} %bitcast.index_ref, f32[768]{0:T(1024)S(1)} %copy-done.3, ...), custom_call_target="tpu_custom_call" | custom-call | flops 3019898880 | bytes 9437184 | tf_op jit(solution)/shard_map/pallas_call | solution.py:440
  17.1 0.0 collective-permute-done.1.after_ref
  17.1 0.0 collective-permute-done.before_ref
  17.1 0.0 copy-done.4
  17.1 0.0 copy-start.1
  17.1 14.0 %shard_map.92 = (bf16[512,768]{1,0:T(8,128)(2,1)S(1)}, bf16[512,768]{1,0:T(8,128)(2,1)S(1)}) custom-call(s32[16]{0:T(128)S(1)} %copy-done.5, s32[16]{0:T(128)S(1)} %copy-done.6, s32[1]{0:T(128)} %bitcast.index_ref, f32[768]{0:T(1024)S(1)} %copy-done.3, f32[768]{0:T(1024)S(1)} %copy-done.4, bf16[256,768]{1,0:T(8,128)(2,1)S(1)} %collective-permute-done.before_ref, ...), custom_call_target="tpu_custom_call" | custom-call | flops 6039797760 | bytes 9437184 | tf_op jit(solution)/shard_map/pallas_call | solution.py:472
  31.1 0.0 copy-start.2
  31.1 26.3 %all_to_all.15.x_ref = bf16[16,32,768]{2,1,0:T(8,128)(2,1)S(1)} all-to-all(bf16[16,32,768]{2,1,0:T(8,128)(2,1)S(1)} %bitcast.5), channel_id=1, replica_groups=mesh['group'=2,'strip'=16] {'strip'}, dimensions={0} | all-to-all | bytes 1572864 | tf_op jit(solution)/shard_map/all_to_all | solution.py:508
  57.4 0.0 copy-done.1
  57.4 0.0 copy-done.2
  57.4 5.3 %shard_map.93 = bf16[16,32,768]{2,1,0:T(8,128)(2,1)S(1)} custom-call(s32[16]{0:T(128)S(1)} %copy-done.6, s32[1]{0:T(128)} %bitcast.index_ref, bf16[16,32,768]{2,1,0:T(8,128)(2,1)S(1)} %all_to_all.15.x_ref, bf16[768,2304]{1,0:T(8,128)(2,1)S(1)} %copy-done.1, bf16[768,768]{1,0:T(8,128)(2,1)S(1)} %copy-done.2), custom_call_target="tpu_custom_call" | custom-call | flops 3019898880 | bytes 9437184 | tf_op jit(solution)/shard_map/pallas_call | solution.py:511
  62.7 23.9 %all_to_all.16 = bf16[16,32,768]{2,1,0:T(8,128)(2,1)S(1)} all-to-all(bf16[16,32,768]{2,1,0:T(8,128)(2,1)S(1)} %shard_map.93), channel_id=1, replica_groups=mesh['group'=2,'strip'=16] {'strip'}, dimensions={0} | all-to-all | bytes 1572864 | tf_op jit(solution)/shard_map/all_to_all | solution.py:508
  86.6 1.2 %fusion = bf16[512,768]{1,0:T(8,128)(2,1)} fusion(bf16[512,768]{1,0:T(8,128)(2,1)S(1)} %get-tuple-element.17, bf16[16,32,768]{2,1,0:T(8,128)(2,1)S(1)} %all_to_all.16), kind=kLoop, calls=%fused_computation.1 | loop fusion | flops 1572864 | bytes 2359296 | tf_op jit(solution)/shard_map/convert_element_type | solution.py:525
Async XLA Ops:
  0.0 7.7 %copy-start = (bf16[512,768]{1,0:T(8,128)(2,1)S(1)}, bf16[512,768]{1,0:T(8,128)(2,1)}, u32[]{:S(2)}) copy-start(bf16[512,768]{1,0:T(8,128)(2,1)} %x_ref.3) | copy-start | bytes 2359300
  0.0 7.7 %copy-start.6 = (s32[16]{0:T(128)S(1)}, s32[16]{0:T(128)}, u32[]{:S(2)}) copy-start(s32[16]{0:T(128)} %count_ref.5) | copy-start | bytes 196
  0.0 7.7 %copy-start.3 = (f32[768]{0:T(1024)S(1)}, f32[768]{0:T(1024)}, u32[]{:S(2)}) copy-start(f32[768]{0:T(1024)} %gain_ref.3) | copy-start | bytes 9220
  0.0 7.7 %copy-start.5 = (s32[16]{0:T(128)S(1)}, s32[16]{0:T(128)}, u32[]{:S(2)}) copy-start(s32[16]{0:T(128)} %reach_ref.3) | copy-start | bytes 196
  1.3 15.8 %collective-permute-start.1 = (bf16[256,768]{1,0:T(8,128)(2,1)S(1)}, bf16[256,768]{1,0:T(8,128)(2,1)S(1)}, u32[]{:S(2)}, u32[]{:S(2)}) collective-permute-start(bf16[256,768]{1,0:T(8,128)(2,1)S(1)} %get-tuple-element.19), channel_id=1, source_target_pairs={{1,0},{2,1},{3,2},{4,3},{5,4},{6,5},{7,6},{8,7},{9,8},{10,9},{11,1... | collective-permute-start | bytes 1179656 | tf_op jit(solution)/shard_map/ppermute | solution.py:438
  3.2 13.9 %collective-permute-start = (bf16[256,768]{1,0:T(8,128)(2,1)S(1)}, bf16[256,768]{1,0:T(8,128)(2,1)S(1)}, u32[]{:S(2)}, u32[]{:S(2)}) collective-permute-start(bf16[256,768]{1,0:T(8,128)(2,1)S(1)} %get-tuple-element.20), channel_id=1, source_target_pairs={{0,1},{1,2},{2,3},{3,4},{4,5},{5,6},{6,7},{7,8},{8,9},{9,10},{10,1... | collective-permute-start | bytes 1179656 | tf_op jit(solution)/shard_map/ppermute | solution.py:437
  7.8 9.3 %copy-start.4 = (f32[768]{0:T(1024)S(1)}, f32[768]{0:T(1024)}, u32[]{:S(2)}) copy-start(f32[768]{0:T(1024)} %time_gain_ref.1) | copy-start | bytes 9220
  17.1 40.4 %copy-start.1 = (bf16[768,2304]{1,0:T(8,128)(2,1)S(1)}, bf16[768,2304]{1,0:T(8,128)(2,1)}, u32[]{:S(2)}) copy-start(bf16[768,2304]{1,0:T(8,128)(2,1)} %project_ref.1) | copy-start | bytes 10616836
  31.1 26.4 %copy-start.2 = (bf16[768,768]{1,0:T(8,128)(2,1)S(1)}, bf16[768,768]{1,0:T(8,128)(2,1)}, u32[]{:S(2)}) copy-start(bf16[768,768]{1,0:T(8,128)(2,1)} %output_ref.1) | copy-start | bytes 3538948

commit v7 on v6

--- a/solution.py
+++ b/solution.py
@@ -207,8 +207,8 @@
     index_ref,
     gain_ref,
     time_gain_ref,
-    before_ref,
-    after_ref,
+    near_ref,
+    far_ref,
     x_ref,
     first_ref,
     middle_ref,
@@ -217,6 +217,7 @@
     output_ref,
     state_ref,
     hidden_ref,
+    halo_s,
     edge_s,
     q_s,
     k_s,
@@ -253,8 +254,19 @@
     )
     tables = (reach_ref, count_ref, frame_len, total)
     work = (mixed_s, bias_s, scores_s, expon_s)
-    halo = jnp.concatenate([before_ref[...], after_ref[...]], axis=0)
-    hidden = norm_rows(halo, gain)
+    odd = lax.rem(index_ref[0], 2)
+
+    @pl.when(odd == 1)
+    def _():
+        halo_s[:half] = near_ref[...]
+        halo_s[half:] = far_ref[...]
+
+    @pl.when(odd == 0)
+    def _():
+        halo_s[:half] = far_ref[...]
+        halo_s[half:] = near_ref[...]
+
+    hidden = norm_rows(halo_s[...], gain)
     for cols, ref in ((KEY, k_s), (VALUE, v_s)):
         made = times(hidden, project_ref[:, cols]).astype(BF16)
         ref[block(0, 2)] = made[:half]
@@ -279,10 +291,10 @@
         *work,
     )
     update = times(mixed_s[...], output_ref[...])
-    edge_s[block(0)] = (before_ref[block(1)].astype(F32) + update[block(0)]).astype(BF16)
+    edge_s[block(0)] = (halo_s[block(1)].astype(F32) + update[block(0)]).astype(BF16)
     edge_s[block(1)] = (x_ref[block(0)].astype(F32) + update[block(1)]).astype(BF16)
     edge_s[block(2)] = (x_ref[block(3)].astype(F32) + update[block(2)]).astype(BF16)
-    edge_s[block(3)] = (after_ref[block(0)].astype(F32) + update[block(3)]).astype(BF16)
+    edge_s[block(3)] = (halo_s[block(2)].astype(F32) + update[block(3)]).astype(BF16)
 
     hidden = norm_rows(edge_s[...], gain)
     for cols, ref in ((KEY, k2_s), (VALUE, v2_s)):
@@ -428,14 +440,18 @@
     slots = local_rows // F
     groups = 2
     group = slots // groups
-    if local_rows != 2 * CHUNK or frame_len % local_rows or local_rows % devices:
+    if devices % 2 or local_rows != 2 * CHUNK or frame_len % local_rows or local_rows % devices:
         raise ValueError("unsupported sizes")
     index = lax.axis_index("strip").reshape(1)
 
-    up = [(i, i + 1) for i in range(devices - 1)]
-    down = [(i + 1, i) for i in range(devices - 1)]
-    before = lax.ppermute(frame_tokens[local_rows - CHUNK :], "strip", up)
-    after = lax.ppermute(frame_tokens[:CHUNK], "strip", down)
+    partners = [(i, i ^ 1) for i in range(devices)]
+    others = [(i, i + 1 if i % 2 else i - 1) for i in range(1, devices - 1)]
+    odd = lax.rem(lax.axis_index("strip"), 2)
+    last = local_rows - CHUNK
+    near = lax.ppermute(
+        lax.dynamic_slice_in_dim(frame_tokens, (1 - odd) * last, CHUNK), "strip", partners
+    )
+    far = lax.ppermute(lax.dynamic_slice_in_dim(frame_tokens, odd * last, CHUNK), "strip", others)
 
     first, middle, second, project, output = call(
         functools.partial(middle_kernel, frame_len, total),
@@ -480,6 +496,7 @@
         scratch_shapes=[
             scratch(local_rows, D),
             scratch(local_rows, D),
+            scratch(local_rows, D),
             scratch(local_rows + 2 * CHUNK, D),
             scratch(local_rows + 2 * CHUNK, D),
             scratch(local_rows, D),
@@ -494,8 +511,8 @@
         index,
         space_gain,
         time_gain,
-        before,
-        after,
+        near,
+        far,
         frame_tokens,
         first,
         middle,

time: 88 us -> 86.3 us (0.981)
  starting transfers between devices: 6.45 us -> 4.6 us
    ppermute x2, starting transfers between devices: 6.45 us -> 4.6 us  [the longest x1 4.53 us: on_device(): lax.ppermute(lax.dynamic_slice_in_dim(frame_tokens, odd * last, CHUNK), '...]
    dynamic_slice x0 -> x1, local copies, waits for them, and re-layouts: none -> 1.24 us  [on_device(): lax.dynamic_slice_in_dim(frame_tokens, odd * last, CHUNK)]
    slice x1 -> x0, local copies, waits for them, and re-layouts: 1.24 us -> none  [on_device(): after = lax.ppermute(frame_tokens[:CHUNK], 'strip', down)]
where the time goes in v7:
time: 86.3 us; the launch traced here: 86.1 us
  blocking collectives  50.3 us (58%)
  Pallas kernels  28.6 us (33%)
  starting transfers between devices  4.6 us (5%)
  local copies, waits for them, and re-layouts  1.27 us (1%)
  other arithmetic  1.15 us (1%)
    all_to_all x2, blocking collectives, exchange(): return lax.all_to_all(x, 'strip', split_axis=0, concat_axis=0, tiled=True)  50.3 us
    pallas_call x1, Pallas kernels, on_device(): call(functools.partial(sides_kernel, frame_len, total), 2 * D * D * 20 *...  14 us
    pallas_call x1, Pallas kernels, on_device(): call(functools.partial(middle_kernel, frame_len, total), 2 * D * D * 10 *...  9.27 us
    pallas_call x1, Pallas kernels, on_device(): call(functools.partial(time_kernel, frame_len, local_rows, devices), 2 *...  5.29 us
    ppermute x1, starting transfers between devices, on_device(): lax.ppermute(lax.dynamic_slice_in_dim(frame_tokens, odd * last, CHUNK), '...  4.53 us
  transfers between devices with their start and end apart: 2, of which 0 were waited for; matrix products, arithmetic and copies ran while one was open for 0% of the time, Pallas kernels for 11%

profile of v7, /device:TPU:1, one launch (start us, length us, event | category | flops | bytes accessed | tf_op | source)
XLA Modules:
  0.0 86.1 jit_solution(8053131245202345581)
XLA Ops:
  0.0 0.0 copy-start
  0.0 0.0 copy-start.6
  0.0 0.0 copy-start.3
  0.0 0.0 copy-start.5
  0.0 1.2 %constant_dynamic-slice_fusion = (bf16[256,768]{1,0:T(8,128)(2,1)S(1)}, bf16[256,768]{1,0:T(8,128)(2,1)S(1)}) fusion(bf16[512,768]{1,0:T(8,128)(2,1)} %x_ref.3, s32[]{:T(128)S(6)} %select_n.7, s32[]{:T(128)S(6)} %select_n.6), kind=kLoop, calls=%fused_computation.2 | loop fusion | bytes 1572872 | tf_op jit(solution)/shard_map/dynamic_slice | solution.py:454
  1.3 4.5 %collective-permute-start.1 = (bf16[256,768]{1,0:T(8,128)(2,1)S(1)}, bf16[256,768]{1,0:T(8,128)(2,1)S(1)}, u32[]{:S(2)}, u32[]{:S(2)}) collective-permute-start(bf16[256,768]{1,0:T(8,128)(2,1)S(1)} %get-tuple-element.19), channel_id=1, source_target_pairs={{1,2},{2,1},{3,4},{4,3},{5,6},{6,5},{7,8},{8,7},{9,10},{10,9},{11,... | collective-permute-start | bytes 1179656 | tf_op jit(solution)/shard_map/ppermute | solution.py:454
  5.8 0.1 collective-permute-start
  5.9 0.0 copy-done
  5.9 0.0 copy-done.6
  5.9 0.0 copy-done.3
  5.9 0.0 copy-done.5
  5.9 0.0 copy-start.4
  5.9 9.3 %shard_map.91 = (bf16[512,2304]{1,0:T(8,128)(2,1)S(1)}, bf16[256,768]{1,0:T(8,128)(2,1)S(1)}, bf16[256,2304]{1,0:T(8,128)(2,1)S(1)}, bf16[768,2304]{1,0:T(8,128)(2,1)S(1)}, bf16[768,768]{1,0:T(8,128)(2,1)S(1)}) custom-call(s32[16]{0:T(128)S(1)} %copy-done.5, s32[16]{0:T(128)S(1)} %copy-done.6, s32[1]{0:T(128)} %bitcast.index_ref, f32[768]{0:T(1024)S(1)} %copy-done.3, ...), custom_call_target="tpu_custom_call" | custom-call | flops 3019898880 | bytes 9437184 | tf_op jit(solution)/shard_map/pallas_call | solution.py:456
  15.2 0.0 collective-permute-done.1.far_ref
  15.2 0.0 collective-permute-done.near_ref
  15.2 0.0 copy-done.4
  15.2 0.0 copy-start.1
  15.3 14.0 %shard_map.92 = (bf16[512,768]{1,0:T(8,128)(2,1)S(1)}, bf16[512,768]{1,0:T(8,128)(2,1)S(1)}) custom-call(s32[16]{0:T(128)S(1)} %copy-done.5, s32[16]{0:T(128)S(1)} %copy-done.6, s32[1]{0:T(128)} %bitcast.index_ref, f32[768]{0:T(1024)S(1)} %copy-done.3, f32[768]{0:T(1024)S(1)} %copy-done.4, bf16[256,768]{1,0:T(8,128)(2,1)S(1)} %collective-permute-done.near_ref, ...), custom_call_target="tpu_custom_call" | custom-call | flops 6039797760 | bytes 9437184 | tf_op jit(solution)/shard_map/pallas_call | solution.py:488
  29.3 0.0 copy-start.2
  29.3 26.4 %all_to_all.15.x_ref = bf16[16,32,768]{2,1,0:T(8,128)(2,1)S(1)} all-to-all(bf16[16,32,768]{2,1,0:T(8,128)(2,1)S(1)} %bitcast.5), channel_id=1, replica_groups=mesh['group'=2,'strip'=16] {'strip'}, dimensions={0} | all-to-all | bytes 1572864 | tf_op jit(solution)/shard_map/all_to_all | solution.py:525
  55.8 0.0 copy-done.1
  55.8 0.0 copy-done.2
  55.8 5.3 %shard_map.93 = bf16[16,32,768]{2,1,0:T(8,128)(2,1)S(1)} custom-call(s32[16]{0:T(128)S(1)} %copy-done.6, s32[1]{0:T(128)} %bitcast.index_ref, bf16[16,32,768]{2,1,0:T(8,128)(2,1)S(1)} %all_to_all.15.x_ref, bf16[768,2304]{1,0:T(8,128)(2,1)S(1)} %copy-done.1, bf16[768,768]{1,0:T(8,128)(2,1)S(1)} %copy-done.2), custom_call_target="tpu_custom_call" | custom-call | flops 3019898880 | bytes 9437184 | tf_op jit(solution)/shard_map/pallas_call | solution.py:528
  61.1 23.9 %all_to_all.16 = bf16[16,32,768]{2,1,0:T(8,128)(2,1)S(1)} all-to-all(bf16[16,32,768]{2,1,0:T(8,128)(2,1)S(1)} %shard_map.93), channel_id=1, replica_groups=mesh['group'=2,'strip'=16] {'strip'}, dimensions={0} | all-to-all | bytes 1572864 | tf_op jit(solution)/shard_map/all_to_all | solution.py:525
  84.9 1.2 %fusion = bf16[512,768]{1,0:T(8,128)(2,1)} fusion(bf16[512,768]{1,0:T(8,128)(2,1)S(1)} %get-tuple-element.17, bf16[16,32,768]{2,1,0:T(8,128)(2,1)S(1)} %all_to_all.16), kind=kLoop, calls=%fused_computation.1 | loop fusion | flops 1572864 | bytes 2359296 | tf_op jit(solution)/shard_map/convert_element_type | solution.py:542
Async XLA Ops:
  0.0 5.9 %copy-start = (bf16[512,768]{1,0:T(8,128)(2,1)S(1)}, bf16[512,768]{1,0:T(8,128)(2,1)}, u32[]{:S(2)}) copy-start(bf16[512,768]{1,0:T(8,128)(2,1)} %x_ref.3) | copy-start | bytes 2359300
  0.0 5.9 %copy-start.6 = (s32[16]{0:T(128)S(1)}, s32[16]{0:T(128)}, u32[]{:S(2)}) copy-start(s32[16]{0:T(128)} %count_ref.5) | copy-start | bytes 196
  0.0 5.9 %copy-start.3 = (f32[768]{0:T(1024)S(1)}, f32[768]{0:T(1024)}, u32[]{:S(2)}) copy-start(f32[768]{0:T(1024)} %gain_ref.3) | copy-start | bytes 9220
  0.0 5.9 %copy-start.5 = (s32[16]{0:T(128)S(1)}, s32[16]{0:T(128)}, u32[]{:S(2)}) copy-start(s32[16]{0:T(128)} %reach_ref.3) | copy-start | bytes 196
  1.3 13.9 %collective-permute-start.1 = (bf16[256,768]{1,0:T(8,128)(2,1)S(1)}, bf16[256,768]{1,0:T(8,128)(2,1)S(1)}, u32[]{:S(2)}, u32[]{:S(2)}) collective-permute-start(bf16[256,768]{1,0:T(8,128)(2,1)S(1)} %get-tuple-element.19), channel_id=1, source_target_pairs={{1,2},{2,1},{3,4},{4,3},{5,6},{6,5},{7,8},{8,7},{9,10},{10,9},{11,... | collective-permute-start | bytes 1179656 | tf_op jit(solution)/shard_map/ppermute | solution.py:454
  5.8 9.4 %collective-permute-start = (bf16[256,768]{1,0:T(8,128)(2,1)S(1)}, bf16[256,768]{1,0:T(8,128)(2,1)S(1)}, u32[]{:S(2)}, u32[]{:S(2)}) collective-permute-start(bf16[256,768]{1,0:T(8,128)(2,1)S(1)} %get-tuple-element.20), channel_id=1, source_target_pairs={{0,1},{1,0},{2,3},{3,2},{4,5},{5,4},{6,7},{7,6},{8,9},{9,8},{10,11... | collective-permute-start | bytes 1179656 | tf_op jit(solution)/shard_map/ppermute | solution.py:451
  5.9 9.3 %copy-start.4 = (f32[768]{0:T(1024)S(1)}, f32[768]{0:T(1024)}, u32[]{:S(2)}) copy-start(f32[768]{0:T(1024)} %time_gain_ref.1) | copy-start | bytes 9220
  15.2 40.5 %copy-start.1 = (bf16[768,2304]{1,0:T(8,128)(2,1)S(1)}, bf16[768,2304]{1,0:T(8,128)(2,1)}, u32[]{:S(2)}) copy-start(bf16[768,2304]{1,0:T(8,128)(2,1)} %project_ref.1) | copy-start | bytes 10616836
  29.3 26.5 %copy-start.2 = (bf16[768,768]{1,0:T(8,128)(2,1)S(1)}, bf16[768,768]{1,0:T(8,128)(2,1)}, u32[]{:S(2)}) copy-start(bf16[768,768]{1,0:T(8,128)(2,1)} %output_ref.1) | copy-start | bytes 3538948

commit v8 on v7

--- a/solution.py
+++ b/solution.py
@@ -139,20 +139,16 @@
     x_ref,
     project_hbm,
     output_hbm,
-    first_hbm,
-    state_hbm,
-    second_hbm,
-    project_s,
-    output_s,
     first_s,
     state_s,
     second_s,
+    project_s,
+    output_s,
     mixed_s,
     bias_s,
     scores_s,
     expon_s,
     in_sems,
-    out_sems,
 ):
     rows = x_ref.shape[0]
     offset = index_ref[0] * rows
@@ -169,8 +165,6 @@
     for copy, cols in ((query_in, QUERY), (key_in, KEY), (value_in, VALUE)):
         copy.wait()
         first_s[:, cols] = times(hidden, project_s[:, cols]).astype(BF16)
-    first_out = pltpu.make_async_copy(first_s, first_hbm, out_sems.at[0])
-    first_out.start()
     tables = (reach_ref, count_ref, frame_len, total)
     space_attention(
         2,
@@ -187,16 +181,9 @@
     )
     output_in.wait()
     state_s[...] = (x_ref[inner].astype(F32) + times(mixed_s[...], output_s[...])).astype(BF16)
-    state_out = pltpu.make_async_copy(state_s, state_hbm, out_sems.at[1])
-    state_out.start()
     hidden = norm_rows(state_s[...], gain)
     for cols in (QUERY, KEY, VALUE):
         second_s[:, cols] = times(hidden, project_s[:, cols]).astype(BF16)
-    second_out = pltpu.make_async_copy(second_s, second_hbm, out_sems.at[2])
-    second_out.start()
-    first_out.wait()
-    state_out.wait()
-    second_out.wait()
 
 
 def sides_kernel(
@@ -466,14 +453,10 @@
             rows16(D, D),
         ),
         in_specs=[smem()] * 3 + [vmem()] * 2 + [hbm()] * 2,
-        out_specs=(hbm(),) * 3 + (vmem(),) * 2,
+        out_specs=(vmem(),) * 5,
         scratch_shapes=[
-            scratch(local_rows, 3 * D),
-            scratch(CHUNK, D),
-            scratch(CHUNK, 3 * D),
             *work(CHUNK, BLK, WIN),
             sems(4),
-            sems(3),
         ],
     )(
         window_reach,

time: 86.3 us -> 86.3 us (level)
  Pallas kernels: 28.6 us -> 27.4 us
    pallas_call x1, Pallas kernels: 9.27 us -> 8.1 us  [on_device(): call(functools.partial(middle_kernel, frame_len, total), 2 * D * D * 10 *...]
  transfers between devices with their start and end apart: 2 -> 2, of which waited for: 0 -> 1; matrix products, arithmetic and copies ran while one was open for 0% -> 0% of each run, Pallas kernels for 11% -> 9%
where the time goes in v8:
time: 86.3 us; the launch traced here: 86.1 us
  blocking collectives  50.8 us (59%)
  Pallas kernels  27.4 us (32%)
  starting transfers between devices  4.6 us (5%)
  local copies, waits for them, and re-layouts  1.27 us (1%)
  other arithmetic  1.15 us (1%)
    all_to_all x2, blocking collectives, exchange(): return lax.all_to_all(x, 'strip', split_axis=0, concat_axis=0, tiled=True)  50.8 us
    pallas_call x1, Pallas kernels, on_device(): call(functools.partial(sides_kernel, frame_len, total), 2 * D * D * 20 *...  14 us
    pallas_call x1, Pallas kernels, on_device(): call(functools.partial(middle_kernel, frame_len, total), 2 * D * D * 10 *...  8.1 us
    pallas_call x1, Pallas kernels, on_device(): call(functools.partial(time_kernel, frame_len, local_rows, devices), 2 *...  5.29 us
    ppermute x1, starting transfers between devices, on_device(): lax.ppermute(lax.dynamic_slice_in_dim(frame_tokens, odd * last, CHUNK), '...  4.53 us
  transfers between devices with their start and end apart: 2, of which 1 were waited for; matrix products, arithmetic and copies ran while one was open for 0% of the time, Pallas kernels for 9%

profile of v8, /device:TPU:1, one launch (start us, length us, event | category | flops | bytes accessed | tf_op | source)
XLA Modules:
  0.0 86.1 jit_solution(13942252954664688701)
XLA Ops:
  0.0 0.0 copy-start
  0.0 0.0 copy-start.6
  0.0 0.0 copy-start.3
  0.0 0.0 copy-start.5
  0.0 1.2 %constant_dynamic-slice_fusion = (bf16[256,768]{1,0:T(8,128)(2,1)S(1)}, bf16[256,768]{1,0:T(8,128)(2,1)S(1)}) fusion(bf16[512,768]{1,0:T(8,128)(2,1)} %x_ref.3, s32[]{:T(128)S(6)} %select_n.7, s32[]{:T(128)S(6)} %select_n.6), kind=kLoop, calls=%fused_computation.2 | loop fusion | bytes 1572872 | tf_op jit(solution)/shard_map/dynamic_slice | solution.py:441
  1.3 4.5 %collective-permute-start.1 = (bf16[256,768]{1,0:T(8,128)(2,1)S(1)}, bf16[256,768]{1,0:T(8,128)(2,1)S(1)}, u32[]{:S(2)}, u32[]{:S(2)}) collective-permute-start(bf16[256,768]{1,0:T(8,128)(2,1)S(1)} %get-tuple-element.19), channel_id=1, source_target_pairs={{1,2},{2,1},{3,4},{4,3},{5,6},{6,5},{7,8},{8,7},{9,10},{10,9},{11,... | collective-permute-start | bytes 1179656 | tf_op jit(solution)/shard_map/ppermute | solution.py:441
  5.8 0.1 collective-permute-start
  5.9 0.0 copy-done
  5.9 0.0 copy-done.6
  5.9 0.0 copy-done.3
  5.9 0.0 copy-done.5
  5.9 0.0 copy-start.4
  5.9 8.1 %shard_map.91 = (bf16[512,2304]{1,0:T(8,128)(2,1)S(1)}, bf16[256,768]{1,0:T(8,128)(2,1)S(1)}, bf16[256,2304]{1,0:T(8,128)(2,1)S(1)}, bf16[768,2304]{1,0:T(8,128)(2,1)S(1)}, bf16[768,768]{1,0:T(8,128)(2,1)S(1)}) custom-call(s32[16]{0:T(128)S(1)} %copy-done.5, s32[16]{0:T(128)S(1)} %copy-done.6, s32[1]{0:T(128)} %bitcast.index_ref, f32[768]{0:T(1024)S(1)} %copy-done.3, ...), custom_call_target="tpu_custom_call" | custom-call | flops 3019898880 | bytes 9437184 | tf_op jit(solution)/shard_map/pallas_call | solution.py:443
  14.0 0.7 collective-permute-done.1.far_ref
  14.7 0.0 collective-permute-done.near_ref
  14.7 0.0 copy-done.4
  14.7 0.0 copy-start.1
  14.7 14.0 %shard_map.92 = (bf16[512,768]{1,0:T(8,128)(2,1)S(1)}, bf16[512,768]{1,0:T(8,128)(2,1)S(1)}) custom-call(s32[16]{0:T(128)S(1)} %copy-done.5, s32[16]{0:T(128)S(1)} %copy-done.6, s32[1]{0:T(128)} %bitcast.index_ref, f32[768]{0:T(1024)S(1)} %copy-done.3, f32[768]{0:T(1024)S(1)} %copy-done.4, bf16[256,768]{1,0:T(8,128)(2,1)S(1)} %collective-permute-done.near_ref, ...), custom_call_target="tpu_custom_call" | custom-call | flops 6039797760 | bytes 9437184 | tf_op jit(solution)/shard_map/pallas_call | solution.py:471
  28.8 0.0 copy-start.2
  28.8 27.0 %all_to_all.15.x_ref = bf16[16,32,768]{2,1,0:T(8,128)(2,1)S(1)} all-to-all(bf16[16,32,768]{2,1,0:T(8,128)(2,1)S(1)} %bitcast.5), channel_id=1, replica_groups=mesh['group'=2,'strip'=16] {'strip'}, dimensions={0} | all-to-all | bytes 1572864 | tf_op jit(solution)/shard_map/all_to_all | solution.py:508
  55.8 0.0 copy-done.1
  55.8 0.0 copy-done.2
  55.8 5.3 %shard_map.93 = bf16[16,32,768]{2,1,0:T(8,128)(2,1)S(1)} custom-call(s32[16]{0:T(128)S(1)} %copy-done.6, s32[1]{0:T(128)} %bitcast.index_ref, bf16[16,32,768]{2,1,0:T(8,128)(2,1)S(1)} %all_to_all.15.x_ref, bf16[768,2304]{1,0:T(8,128)(2,1)S(1)} %copy-done.1, bf16[768,768]{1,0:T(8,128)(2,1)S(1)} %copy-done.2), custom_call_target="tpu_custom_call" | custom-call | flops 3019898880 | bytes 9437184 | tf_op jit(solution)/shard_map/pallas_call | solution.py:511
  61.1 23.9 %all_to_all.16 = bf16[16,32,768]{2,1,0:T(8,128)(2,1)S(1)} all-to-all(bf16[16,32,768]{2,1,0:T(8,128)(2,1)S(1)} %shard_map.93), channel_id=1, replica_groups=mesh['group'=2,'strip'=16] {'strip'}, dimensions={0} | all-to-all | bytes 1572864 | tf_op jit(solution)/shard_map/all_to_all | solution.py:508
  84.9 1.2 %fusion = bf16[512,768]{1,0:T(8,128)(2,1)} fusion(bf16[512,768]{1,0:T(8,128)(2,1)S(1)} %get-tuple-element.17, bf16[16,32,768]{2,1,0:T(8,128)(2,1)S(1)} %all_to_all.16), kind=kLoop, calls=%fused_computation.1 | loop fusion | flops 1572864 | bytes 2359296 | tf_op jit(solution)/shard_map/convert_element_type | solution.py:525
Async XLA Ops:
  0.0 5.9 %copy-start = (bf16[512,768]{1,0:T(8,128)(2,1)S(1)}, bf16[512,768]{1,0:T(8,128)(2,1)}, u32[]{:S(2)}) copy-start(bf16[512,768]{1,0:T(8,128)(2,1)} %x_ref.3) | copy-start | bytes 2359300
  0.0 5.9 %copy-start.6 = (s32[16]{0:T(128)S(1)}, s32[16]{0:T(128)}, u32[]{:S(2)}) copy-start(s32[16]{0:T(128)} %count_ref.5) | copy-start | bytes 196
  0.0 5.9 %copy-start.3 = (f32[768]{0:T(1024)S(1)}, f32[768]{0:T(1024)}, u32[]{:S(2)}) copy-start(f32[768]{0:T(1024)} %gain_ref.3) | copy-start | bytes 9220
  0.0 5.9 %copy-start.5 = (s32[16]{0:T(128)S(1)}, s32[16]{0:T(128)}, u32[]{:S(2)}) copy-start(s32[16]{0:T(128)} %reach_ref.3) | copy-start | bytes 196
  1.3 13.4 %collective-permute-start.1 = (bf16[256,768]{1,0:T(8,128)(2,1)S(1)}, bf16[256,768]{1,0:T(8,128)(2,1)S(1)}, u32[]{:S(2)}, u32[]{:S(2)}) collective-permute-start(bf16[256,768]{1,0:T(8,128)(2,1)S(1)} %get-tuple-element.19), channel_id=1, source_target_pairs={{1,2},{2,1},{3,4},{4,3},{5,6},{6,5},{7,8},{8,7},{9,10},{10,9},{11,... | collective-permute-start | bytes 1179656 | tf_op jit(solution)/shard_map/ppermute | solution.py:441
  5.8 8.9 %collective-permute-start = (bf16[256,768]{1,0:T(8,128)(2,1)S(1)}, bf16[256,768]{1,0:T(8,128)(2,1)S(1)}, u32[]{:S(2)}, u32[]{:S(2)}) collective-permute-start(bf16[256,768]{1,0:T(8,128)(2,1)S(1)} %get-tuple-element.20), channel_id=1, source_target_pairs={{0,1},{1,0},{2,3},{3,2},{4,5},{5,4},{6,7},{7,6},{8,9},{9,8},{10,11... | collective-permute-start | bytes 1179656 | tf_op jit(solution)/shard_map/ppermute | solution.py:438
  5.9 8.8 %copy-start.4 = (f32[768]{0:T(1024)S(1)}, f32[768]{0:T(1024)}, u32[]{:S(2)}) copy-start(f32[768]{0:T(1024)} %time_gain_ref.1) | copy-start | bytes 9220
  14.7 41.0 %copy-start.1 = (bf16[768,2304]{1,0:T(8,128)(2,1)S(1)}, bf16[768,2304]{1,0:T(8,128)(2,1)}, u32[]{:S(2)}) copy-start(bf16[768,2304]{1,0:T(8,128)(2,1)} %project_ref.1) | copy-start | bytes 10616836
  28.8 27.0 %copy-start.2 = (bf16[768,768]{1,0:T(8,128)(2,1)S(1)}, bf16[768,768]{1,0:T(8,128)(2,1)}, u32[]{:S(2)}) copy-start(bf16[768,768]{1,0:T(8,128)(2,1)} %output_ref.1) | copy-start | bytes 3538948
